TPU v7x, 32 devices: a whole 2x2x4 slice. The times are simulated.
32 devices in a mesh: dp: 8 (over z, x), tensor: 4 (over y, core).
Axes of the slice: x: 2, y: 2, z: 4, core: 2. Of those that a mesh axis runs over, the one named last changes fastest.
Arguments:
- layer_input: bfloat16 [2048, 1024], P(('dp', 'tensor')), may hold values from -6 to 6
- seq_ids: int32 [8, 256], P('dp'), may hold values from 0 to 2, never falling along the last dimension, each value on 1 to 128 neighbouring positions
- expert_ids: int32 [2048, 8], P('dp'), may hold values from 0 to 31, all different within a row; in each aligned block of 256 rows (0 to 255, 256 to 511, ...) at most 128 rows name the same one
- out_grad: bfloat16 [2048, 1024], P(('dp', 'tensor')), may hold values from -6 to 6
- gain_attn: bfloat16 [1024], P('dp'), may hold values from 0.099609375 to 1.8984375
- gain_moe: bfloat16 [1024], P('dp'), may hold values from 0.099609375 to 1.8984375
- w_query: bfloat16 [1024, 1024], P('dp', 'tensor'), may hold values from -0.1875 to 0.1875
- w_key: bfloat16 [1024, 512], P('dp', 'tensor'), may hold values from -0.1875 to 0.1875
- w_value: bfloat16 [1024, 512], P('dp', 'tensor'), may hold values from -0.1875 to 0.1875
- w_output: bfloat16 [1024, 1024], P('tensor', 'dp'), may hold values from -0.75 to 0.75
- w_router: bfloat16 [1024, 32], P('dp'), may hold values from -0.046875 to 0.046875
- w_gate: bfloat16 [32, 1024, 512], P(None, 'dp', 'tensor'), may hold values from -0.1875 to 0.1875
- w_up: bfloat16 [32, 1024, 512], P(None, 'dp', 'tensor'), may hold values from -0.1875 to 0.1875
- w_down: bfloat16 [32, 512, 1024], P(None, 'tensor', 'dp'), may hold values from -2 to 2
Outputs:
- layer_output: bfloat16 [2048, 1024], P(('dp', 'tensor'))
- input_grad: bfloat16 [2048, 1024], P(('dp', 'tensor'))
- grad_gain_attn: float32 [1024], P('dp')
- grad_gain_moe: float32 [1024], P('dp')
- grad_query: float32 [1024, 1024], P('dp', 'tensor')
- grad_key: float32 [1024, 512], P('dp', 'tensor')
- grad_value: float32 [1024, 512], P('dp', 'tensor')
- grad_output: float32 [1024, 1024], P('tensor', 'dp')
- grad_router: float32 [1024, 32], P('dp')
- grad_gate: float32 [32, 1024, 512], P(None, 'dp', 'tensor')
- grad_up: float32 [32, 1024, 512], P(None, 'dp', 'tensor')
- grad_down: float32 [32, 512, 1024], P(None, 'tensor', 'dp')
Inputs may be any that keep to these rules, and one draw needn't show every extreme that they name: `seq_ids`: in each row the sequence number never falls; each of the 3 sequences holds 1 to 128 tokens and one holds exactly 128. `expert_ids`: each row names 8 different experts. Within each aligned block of 256 rows no expert is named by more than 128 rows, a bound that some block reaches.
All inputs are finite; a program needn't handle non-finite values.
Results may differ from a plain program's by a relative error of at most 0.018.
Values may be sent and summed in bfloat16 or wider, within the bound.
No kernel may reach another device: no remote copies, remote signals or barrier semaphores. Data moves between devices by JAX's collectives and lax.ppermute only.
A program may use at most 192 MiB of HBM per device.

v0:
```python
import functools

import jax
import jax.numpy as jnp
import numpy as np
from jax import lax
from jax.experimental import pallas as pl
from jax.experimental.pallas import tpu as pltpu
from jax.sharding import PartitionSpec as P


HD = 64
CAP = 128
LANES = 128

eps_norm = 1e-05
score_scale = 0.125
rope_base = 10000.0

BF = jnp.bfloat16
F32 = jnp.float32


def mm(a, b, ca, cb):
    return lax.dot_general(a, b, (((ca,), (cb,)), ((), ())), preferred_element_type=F32)


def call(kernel, outs, scratch=(), smem=0):
    def run(*args):
        in_specs = [pl.BlockSpec(memory_space=pltpu.SMEM)] * smem
        in_specs += [pl.BlockSpec(memory_space=pltpu.VMEM)] * (len(args) - smem)
        return pl.pallas_call(
            kernel,
            out_shape=[jax.ShapeDtypeStruct(s, d) for s, d in outs],
            in_specs=in_specs,
            out_specs=[pl.BlockSpec(memory_space=pltpu.VMEM)] * len(outs),
            scratch_shapes=[pltpu.VMEM(s, d) for s, d in scratch],
        )(*args)

    return run


def split_refs(refs, *counts):
    parts, at = [], 0
    for count in counts:
        parts.append(refs[at : at + count])
        at += count
    return parts


def norm_parts(values):
    inverse = lax.rsqrt(jnp.mean(values * values, axis=-1, keepdims=True) + eps_norm)
    return values * inverse, inverse


def norm_backward(upstream, normed, inverse, gain):
    scaled = upstream * gain
    return inverse * (scaled - normed * jnp.mean(scaled * normed, axis=-1, keepdims=True))


def rotate_lanes(values, cosine, signed_sine):
    width = values.shape[1]
    half = HD // 2
    lane = lax.broadcasted_iota(jnp.int32, values.shape, 1)
    ahead = pltpu.roll(values, width - half, 1)
    behind = pltpu.roll(values, half, 1)
    partner = jnp.where(lane % HD < half, ahead, behind)
    copies = width // LANES
    return values * jnp.concatenate([cosine] * copies, 1) + partner * jnp.concatenate(
        [signed_sine] * copies, 1
    )


def allowed_pairs(seg_col, seg_row, length):
    rows = lax.broadcasted_iota(jnp.int32, (length, length), 0)
    cols = lax.broadcasted_iota(jnp.int32, (length, length), 1)
    return (seg_col == seg_row) & (rows >= cols)


def scatter_rows(whole, parts, own):
    span = parts[0].shape[0]
    for s, out in enumerate(parts):
        at = pl.multiple_of(jnp.bitwise_xor(own, s) * span, span)
        out[...] = whole[pl.ds(at, span), :].astype(out.dtype)


def attn_fwd_kernel(peers, shares, dims, *refs):
    n_q, n_kv = dims
    (idx,), (x,), w_in, (cos, sin, seg_c, seg_r), parts, outs, (part,) = split_refs(
        refs, 1, 1, peers, 4, shares, 6, 1
    )
    wall, gains, qkv, att, log_out, hid = outs
    rows = w_in[0].shape[0]
    for m in range(peers):
        at = pl.multiple_of(jnp.bitwise_xor(idx[0], m) * rows, rows)
        wall[pl.ds(at, rows), :] = w_in[m][...]
    qk_w = (n_q + n_kv) * HD
    all_w = (n_q + 2 * n_kv) * HD
    o_at = all_w + n_q * HD
    misc_t = jnp.transpose(wall[:, o_at : o_at + LANES].astype(F32))
    gains[...] = misc_t[32:40, :]
    gain = misc_t[32:33, :]
    normed, _ = norm_parts(x[...].astype(F32))
    hidden = (normed * gain).astype(BF)
    hid[...] = hidden
    pre = jnp.dot(hidden, wall[:, :all_w], preferred_element_type=F32)
    qk = rotate_lanes(pre[:, :qk_w], cos[...], sin[...]).astype(BF)
    value = pre[:, qk_w:].astype(BF)
    qkv[...] = jnp.concatenate([qk, value], 1)
    length = x.shape[0]
    allowed = allowed_pairs(seg_c[...], seg_r[...], length)
    group = n_q // n_kv
    outs_h, logs = [], []
    for h in range(n_q):
        g = h // group
        q_h = qk[:, h * HD : (h + 1) * HD]
        k_g = qk[:, (n_q + g) * HD : (n_q + g + 1) * HD]
        v_g = value[:, g * HD : (g + 1) * HD]
        scores = mm(q_h, k_g, 1, 1) * score_scale
        total = jnp.sum(jnp.where(allowed, jnp.exp(scores), 0.0), axis=-1, keepdims=True)
        log_total = jnp.log(total)
        probs = jnp.where(allowed, jnp.exp(scores - log_total), 0.0).astype(BF)
        outs_h.append(jnp.dot(probs, v_g, preferred_element_type=F32).astype(BF))
        logs.append(log_total)
    flat = jnp.concatenate(outs_h, 1)
    att[...] = flat
    lane = lax.broadcasted_iota(jnp.int32, (length, LANES), 1)
    packed = jnp.zeros((length, LANES), F32)
    for h in range(n_q):
        packed = jnp.where(lane == h, logs[h], packed)
    log_out[...] = packed
    part[...] = mm(flat, wall[:, all_w:o_at], 1, 1)
    scatter_rows(part, parts, idx[1])


def post_attn_kernel(experts, shares, *refs):
    parts, (x, gains, misc, res, router, msg) = split_refs(refs, shares, 6)
    width = x.shape[1]
    total = x[...].astype(F32)
    for part in parts:
        total = total + part[...].astype(F32)
    res[...] = total
    normed, _ = norm_parts(total)
    h2 = (normed * gains[1:2, :]).astype(BF)
    logits = jnp.dot(h2, misc[...], preferred_element_type=F32)
    lane = lax.broadcasted_iota(jnp.int32, logits.shape, 1)
    exponent = jnp.where(lane < experts, jnp.exp(logits), 0.0)
    probs = exponent / jnp.sum(exponent, axis=-1, keepdims=True)
    router[...] = probs
    msg[:, :width] = h2
    msg[:, width:] = probs.astype(BF)


def onehot_kernel(peers, shares, idx, ids, grads, *outs):
    gt = outs[0]
    slots = outs[1:]
    length = ids.shape[0]
    lane = lax.broadcasted_iota(jnp.int32, (length, LANES), 1)
    expert = jnp.bitwise_xor(idx[0], lane) * shares + idx[1]
    ids_v = ids[...]
    member = jnp.zeros((length, LANES), F32)
    for k in range(ids_v.shape[1]):
        hit = (ids_v[:, k : k + 1] == expert) & (lane < peers)
        member = member + jnp.where(hit, 1.0, 0.0)
    r = lax.broadcasted_iota(jnp.int32, (length, length), 0)
    c = lax.broadcasted_iota(jnp.int32, (length, length), 1)
    lower = jnp.where(r > c, 1.0, 0.0).astype(BF)
    rank = jnp.dot(lower, member.astype(BF), preferred_element_type=F32)
    place = jnp.where(member > 0.0, rank, -1.0)
    slot = lane.astype(F32)
    for m in range(peers):
        hot = jnp.where(place[:, m : m + 1] == slot, 1.0, 0.0).astype(BF)
        gt[:, m * CAP : (m + 1) * CAP] = hot
        slots[m][...] = mm(hot, grads[...], 0, 0).astype(BF)


def dispatch_kernel(peers, gt, rows, *slots):
    for m in range(peers):
        slots[m][...] = mm(gt[:, m * CAP : (m + 1) * CAP], rows[...], 0, 0).astype(BF)


def gate_column(router_cols, expert):
    values = router_cols.astype(F32)
    lane = lax.broadcasted_iota(jnp.int32, values.shape, 1)
    return jnp.sum(jnp.where(lane == expert, values, 0.0), axis=-1, keepdims=True)


def load_down(own, pieces, down, shares):
    for m, piece in enumerate(pieces):
        at = pl.ds(pl.multiple_of(jnp.bitwise_xor(own, m) * 128, 128), 128)
        for t in range(shares):
            down[t * 128 : (t + 1) * 128, at] = piece[t, 256:384, :]


def weight_pack_kernel(peers, shares, idx, gate, up, down, *outs):
    for s in range(shares):
        for m in range(peers):
            e = jnp.bitwise_xor(idx[0], m) * shares + jnp.bitwise_xor(idx[1], s)
            for k, w in enumerate((gate, up, down)):
                outs[s][m, k * 128 : (k + 1) * 128, :] = w[e]


def regroup_kernel(peers, shares, *refs):
    ins, outs = split_refs(refs, shares, peers)
    for m in range(peers):
        for s in range(shares):
            outs[m][s] = ins[s][m]


def weight_grad_kernel(peers, shares, idx, *refs):
    ins, outs = split_refs(refs, peers, 3)
    for m in range(peers):
        for s in range(shares):
            e = jnp.bitwise_xor(idx[0], m) * shares + jnp.bitwise_xor(idx[1], s)
            for k in range(3):
                outs[k][e] = ins[m][s, k * 128 : (k + 1) * 128, :].astype(F32)


def expert_main_kernel(peers, shares, step, *refs):
    (idx,), rows_in, grads_in, pieces, rg_out, (hid, gpu), scratch = split_refs(
        refs, 1, peers, peers, peers, peers, 2, 5
    )
    rows, grads, wgu, down, back = scratch
    ff = shares * 128
    width = grads.shape[1]
    for m in range(peers):
        rows[m * CAP : (m + 1) * CAP, :] = rows_in[m][...]
        grads[m * CAP : (m + 1) * CAP, :] = grads_in[m][...]
    for m, piece in enumerate(pieces):
        at = pl.ds(pl.multiple_of(jnp.bitwise_xor(idx[0], m) * 128, 128), 128)
        for t in range(shares):
            wgu[at, t * 128 : (t + 1) * 128] = piece[t, 0:128, :]
            wgu[at, ff + t * 128 : ff + (t + 1) * 128] = piece[t, 128:256, :]
    load_down(idx[0], pieces, down, shares)
    expert = idx[0] * shares + idx[1]

    def body(c, carry):
        at = pl.ds(pl.multiple_of(c * step, step), step)
        gate = gate_column(rows[at, width:], expert)
        pre = jnp.dot(rows[at, :width], wgu[...], preferred_element_type=F32)
        raw = mm(grads[at, :], down[...], 1, 1)
        gate_pre = pre[:, :ff]
        up_pre = pre[:, ff:]
        sig = jax.nn.sigmoid(gate_pre)
        silu = gate_pre * sig
        hidden = (silu * up_pre).astype(BF)
        hid[at, :] = hidden
        gate_grad = jnp.sum(hidden.astype(F32) * raw, axis=-1, keepdims=True)
        hidden_grad = raw * gate
        gp = (hidden_grad * up_pre * sig * (1.0 + gate_pre * (1.0 - sig))).astype(BF)
        up = (hidden_grad * silu).astype(BF)
        both = jnp.concatenate([gp, up], 1)
        gpu[at, :] = both
        back[at, :width] = mm(both, wgu[...], 1, 1).astype(BF)
        lane = lax.broadcasted_iota(jnp.int32, (step, LANES), 1)
        back[at, width:] = jnp.where(lane == expert, gate_grad, 0.0).astype(BF)
        return carry

    lax.fori_loop(0, peers * CAP // step, body, 0)
    for m in range(peers):
        rg_out[m][...] = back[m * CAP : (m + 1) * CAP, :]


def expert_rest_kernel(peers, shares, step, *refs):
    (idx,), rows_in, grads_in, pieces, (hid, gpu), y_out, grad_out, scratch = split_refs(
        refs, 1, peers, peers, peers, 2, peers, shares, 3
    )
    rows, scaled, down = scratch
    width = rows.shape[1]
    expert = idx[0] * shares + idx[1]
    load_down(idx[0], pieces, down, shares)
    for m in range(peers):
        part = slice(m * CAP, (m + 1) * CAP)
        gate = gate_column(rows_in[m][:, width:], expert)
        rows[part, :] = rows_in[m][:, :width]
        scaled[part, :] = (grads_in[m][...].astype(F32) * gate).astype(BF)

    for m in range(peers):
        gate = gate_column(rows_in[m][:, width:], expert)
        out = jnp.dot(hid[m * CAP : (m + 1) * CAP, :], down[...], preferred_element_type=F32)
        y_out[m][...] = (out * gate).astype(BF)

    def body(c, carry):
        at = pl.ds(pl.multiple_of(c * step, step), step)
        both = mm(rows[:, at], gpu[...], 0, 0).astype(BF)
        down_g = mm(hid[...], scaled[:, at], 0, 0).astype(BF)
        for s in range(step // 128):
            for t in range(shares):
                m = jnp.bitwise_xor(c * (step // 128) + s, idx[0])
                r = slice(s * 128, (s + 1) * 128)
                out = grad_out[t]
                out[m, 0:128, :] = both[r, t * 128 : (t + 1) * 128]
                out[m, 128:256, :] = both[r, (shares + t) * 128 : (shares + t + 1) * 128]
                out[m, 256:384, :] = down_g[t * 128 : (t + 1) * 128, r]
        return carry

    lax.fori_loop(0, width // step, body, 0)


def combine_kernel(peers, shares, *refs):
    (idx, gt), slots, parts, (all_slots, total) = split_refs(refs, 2, peers, shares, 2)
    for m in range(peers):
        all_slots[m * CAP : (m + 1) * CAP, :] = slots[m][...]
    total[...] = jnp.dot(gt[...], all_slots[...], preferred_element_type=F32)
    scatter_rows(total, parts, idx[1])


def hi_lo_rows(row, count):
    hi = row.astype(BF)
    lo = (row - hi.astype(F32)).astype(BF)
    place = lax.broadcasted_iota(jnp.int32, (count, row.shape[1]), 0)
    out = jnp.where(place == 0, hi.astype(F32), jnp.where(place == 1, lo.astype(F32), 0.0))
    return out.astype(BF)


def moe_back_kernel(shares, *refs):
    backs, (router, res, gains, misc, out_grad, rgrad, msg) = split_refs(refs, shares, 7)
    own, width = res.shape
    total = backs[0][...].astype(F32)
    for back in backs[1:]:
        total = total + back[...].astype(F32)
    upstream = total[:, :width]
    prob_grad = total[:, width:]
    probs = router[...]
    logit = (probs * (prob_grad - jnp.sum(probs * prob_grad, axis=-1, keepdims=True))).astype(BF)
    upstream = upstream + mm(logit, misc[...], 1, 1)
    normed, inverse = norm_parts(res[...])
    gain_grad = jnp.sum(upstream * normed, axis=0, keepdims=True)
    grad = out_grad[...].astype(F32) + norm_backward(upstream, normed, inverse, gains[1:2, :])
    rgrad[...] = grad
    msg[0:own, :width] = grad.astype(BF)
    msg[0:own, width:] = logit
    msg[own:, :width] = hi_lo_rows(gain_grad, msg.shape[0] - own)
    msg[own:, width:] = jnp.zeros((msg.shape[0] - own, LANES), BF)


def attn_bwd_kernel(peers, shares, dims, *refs):
    n_q, n_kv = dims
    ins, g_out, msg2, (sums, partial) = split_refs(refs, 13, peers, shares, 2)
    idx, msg, wall, qkv, att, logs, cos, sin, seg_c, seg_r, hid, rows2, x = ins
    length, width = x.shape
    own = length // shares
    span = msg.shape[0] // shares
    qk_w = (n_q + n_kv) * HD
    all_w = (n_q + 2 * n_kv) * HD
    o_at = all_w + n_q * HD
    resid = jnp.concatenate([msg[s * span : s * span + own, :width] for s in range(shares)], 0)
    logit = jnp.concatenate([msg[s * span : s * span + own, width:] for s in range(shares)], 0)
    gain_moe = jnp.zeros((1, width), F32)
    for s in range(shares):
        extra = msg[s * span + own : (s + 1) * span, :width].astype(F32)
        gain_moe = gain_moe + jnp.sum(extra, axis=0, keepdims=True)
    att_grad = jnp.dot(resid, wall[:, all_w:o_at], preferred_element_type=F32).astype(BF)
    allowed = allowed_pairs(seg_c[...], seg_r[...], length)
    group = n_q // n_kv
    lane = lax.broadcasted_iota(jnp.int32, (length, LANES), 1)
    log_all = logs[...]
    q_grads, k_grads, v_grads = [], [], []
    for g in range(n_kv):
        k_g = qkv[:, (n_q + g) * HD : (n_q + g + 1) * HD]
        v_g = qkv[:, qk_w + g * HD : qk_w + (g + 1) * HD]
        k_sum = jnp.zeros((length, HD), F32)
        v_sum = jnp.zeros((length, HD), F32)
        for h in range(g * group, (g + 1) * group):
            cut = slice(h * HD, (h + 1) * HD)
            q_h = qkv[:, cut]
            log_h = jnp.sum(jnp.where(lane == h, log_all, 0.0), axis=-1, keepdims=True)
            scores = mm(q_h, k_g, 1, 1) * score_scale
            probs = jnp.where(allowed, jnp.exp(scores - log_h), 0.0)
            a_h = att_grad[:, cut]
            delta = jnp.sum(
                a_h.astype(F32) * att[:, cut].astype(F32), axis=-1, keepdims=True
            )
            prob_grad = mm(a_h, v_g, 1, 1)
            s_grad = (probs * (prob_grad - delta) * score_scale).astype(BF)
            q_grads.append(jnp.dot(s_grad, k_g, preferred_element_type=F32))
            k_sum = k_sum + mm(s_grad, q_h, 0, 0)
            v_sum = v_sum + mm(probs.astype(BF), a_h, 0, 0)
        k_grads.append(k_sum)
        v_grads.append(v_sum)
    qk_grad = jnp.concatenate(q_grads + k_grads, 1)
    qk_low = rotate_lanes(qk_grad, cos[...], -sin[...]).astype(BF)
    low = jnp.concatenate([qk_low, jnp.concatenate(v_grads, 1).astype(BF)], 1)
    sums[:, :all_w] = mm(hid[...], low, 0, 0)
    sums[:, all_w:o_at] = mm(resid, att[...], 0, 0)
    place = lax.broadcasted_iota(jnp.int32, (LANES, width), 0)
    gain_hi = gain_moe.astype(BF).astype(F32)
    rows = jnp.where(place == 32, gain_hi, jnp.where(place == 33, gain_moe - gain_hi, 0.0))
    sums[:, o_at:] = mm(rows2[:, :width], logit, 0, 0) + jnp.transpose(rows)
    depth = g_out[0].shape[0]
    for m in range(peers):
        at = pl.multiple_of(jnp.bitwise_xor(idx[0], m) * depth, depth)
        g_out[m][...] = sums[pl.ds(at, depth), :].astype(BF)
    partial[...] = mm(low, wall[:, :all_w], 1, 1)
    normed, _ = norm_parts(x[...].astype(F32))
    extra = hi_lo_rows(jnp.sum(partial[...] * normed, axis=0, keepdims=True), span - own)
    scatter_rows(partial, [out.at[0:own, :] for out in msg2], idx[1])
    for out in msg2:
        out[own:, :] = extra


def input_grad_kernel(shares, *refs):
    msgs, (x, gains, rgrad, out, gain_out) = split_refs(refs, shares, 5)
    own, width = x.shape
    upstream = jnp.zeros((own, width), F32)
    gain_sum = jnp.zeros((1, width), F32)
    for msg in msgs:
        upstream = upstream + msg[0:own, :].astype(F32)
        gain_sum = gain_sum + jnp.sum(msg[own:, :].astype(F32), axis=0, keepdims=True)
    normed, inverse = norm_parts(x[...].astype(F32))
    through = norm_backward(upstream, normed, inverse, gains[0:1, :])
    out[...] = (rgrad[...] + through).astype(BF)
    gain_out[...] = jnp.broadcast_to(gain_sum, gain_out.shape)


def layer_out_kernel(shares, *refs):
    parts, (res, out) = split_refs(refs, shares, 2)
    total = res[...]
    for part in parts:
        total = total + part[...].astype(F32)
    out[...] = total.astype(BF)


def swap(values, axis):
    got = [values[0]]
    for m in range(1, len(values)):
        got.append(lax.ppermute(values[m], axis, [(i, i ^ m) for i in range(len(values))]))
    return got


def per_device(
    rep,
    layer_input,
    seq_ids,
    expert_ids,
    out_grad,
    gain_attn,
    gain_moe,
    w_query,
    w_key,
    w_value,
    w_output,
    w_router,
    w_gate,
    w_up,
    w_down,
):
    peers = lax.axis_size("dp")
    shares = lax.axis_size("tensor")
    own, width = layer_input.shape
    experts = w_gate.shape[0]
    length = seq_ids.shape[1]
    depth = width // peers
    q_w, kv_w = w_query.shape[1], w_key.shape[1]
    dims = (q_w // HD, kv_w // HD)
    all_w = q_w + 2 * kv_w
    pack_w = all_w + q_w + LANES
    slots = peers * CAP
    wide = width + LANES
    idx = jnp.stack([lax.axis_index("dp"), lax.axis_index("tensor")]).astype(jnp.int32)

    local = w_router.shape[0]
    pack = jnp.concatenate(
        [
            w_query,
            w_key,
            w_value,
            w_output.T,
            w_router,
            gain_attn[:, None],
            gain_moe[:, None],
            jnp.zeros((local, LANES - experts - 2), BF),
        ],
        axis=1,
    )
    if rep > 1:
        pack = lax.all_gather(pack, "rep", axis=0, tiled=True)
    packs = swap([pack] * peers, "dp")

    if rep > 1:
        w_gate = lax.all_gather(w_gate, "rep", axis=1, tiled=True)
        w_up = lax.all_gather(w_up, "rep", axis=1, tiled=True)
        w_down = lax.all_gather(w_down, "rep", axis=2, tiled=True)
    weight_parts = call(
        functools.partial(weight_pack_kernel, peers, shares),
        [((peers, 384, LANES), BF)] * shares,
        smem=1,
    )(idx, w_gate, w_up, w_down)
    weight_parts = swap(weight_parts, "tensor")

    x_all = lax.all_gather(layer_input, "tensor", axis=0, tiled=True)
    segment = seq_ids[0]
    before = jnp.sum((segment[None, :] < segment[:, None]).astype(jnp.int32), axis=1)
    position = (jnp.arange(length, dtype=jnp.int32) - before).astype(F32)
    lane = jnp.arange(LANES, dtype=jnp.int32) % HD
    half = HD // 2
    frequency = rope_base ** (-2.0 * (lane % half).astype(F32) / HD)
    angles = position[:, None] * frequency[None, :]
    cosine = jnp.cos(angles)
    sine = jnp.where(lane[None, :] < half, -1.0, 1.0) * jnp.sin(angles)
    seg_c = segment[:, None]
    seg_r = segment[None, :]

    grads_all = lax.all_gather(out_grad, "tensor", axis=0, tiled=True)
    gt, *grad_slots = call(
        functools.partial(onehot_kernel, peers, shares),
        [((length, slots), BF)] + [((CAP, width), BF)] * peers,
        smem=1,
    )(idx, expert_ids, grads_all)
    x_all, grad_slots = lax.optimization_barrier((x_all, grad_slots))
    grad_in = swap(grad_slots, "dp")

    *parts, wall, gains, qkv, att, logs, hid = call(
        functools.partial(attn_fwd_kernel, peers, shares, dims),
        [((own, width), BF)] * shares
        + [
            ((width, pack_w), BF),
            ((8, width), F32),
            ((length, all_w), BF),
            ((length, q_w), BF),
            ((length, LANES), F32),
            ((length, width), BF),
        ],
        scratch=[((length, width), F32)],
        smem=1,
    )(idx, x_all, *packs, cosine, sine, seg_c, seg_r)

    misc = wall[:, all_w + q_w :]
    parts = swap(parts, "tensor")
    weight_parts = call(
        functools.partial(regroup_kernel, peers, shares), [((shares, 384, LANES), BF)] * peers
    )(*weight_parts)
    pieces = swap(weight_parts, "dp")
    res, router, msg = call(
        functools.partial(post_attn_kernel, experts, shares),
        [((own, width), F32), ((own, LANES), F32), ((own, wide), BF)],
    )(*parts, layer_input, gains, misc)
    rows_all = lax.all_gather(msg, "tensor", axis=0, tiled=True)
    row_slots = call(
        functools.partial(dispatch_kernel, peers), [((CAP, wide), BF)] * peers
    )(gt, rows_all)
    rows_in = swap(row_slots, "dp")

    ff = w_gate.shape[2] * shares
    *row_back, hidden, gate_up = call(
        functools.partial(expert_main_kernel, peers, shares, 256),
        [((CAP, wide), BF)] * peers + [((slots, ff), BF), ((slots, 2 * ff), BF)],
        scratch=[
            ((slots, wide), BF),
            ((slots, width), BF),
            ((width, 2 * ff), BF),
            ((ff, width), BF),
            ((slots, wide), BF),
        ],
        smem=1,
    )(idx, *rows_in, *grad_in, *pieces)
    back_in = swap(row_back, "dp")
    rest = call(
        functools.partial(expert_rest_kernel, peers, shares, 256),
        [((CAP, width), BF)] * peers + [((peers, 384, LANES), BF)] * shares,
        scratch=[((slots, width), BF), ((slots, width), BF), ((ff, width), BF)],
        smem=1,
    )(idx, *rows_in, *grad_in, *pieces, hidden, gate_up)

    y_slots, grad_parts = rest[:peers], rest[peers:]
    grad_parts = swap(grad_parts, "tensor")
    back_in, y_slots = lax.optimization_barrier((back_in, y_slots))
    y_in = swap(y_slots, "dp")
    row_grad = call(
        functools.partial(combine_kernel, peers, shares),
        [((own, wide), BF)] * shares,
        scratch=[((slots, wide), BF), ((length, wide), F32)],
        smem=1,
    )(idx, gt, *back_in)
    row_grad = swap(row_grad, "tensor")
    grad_parts = call(
        functools.partial(regroup_kernel, peers, shares), [((shares, 384, LANES), BF)] * peers
    )(*grad_parts)
    grad_parts = swap(grad_parts, "dp")
    rgrad, msg = call(
        functools.partial(moe_back_kernel, shares), [((own, width), F32), ((own + 16, wide), BF)]
    )(*row_grad, router, res, gains, misc, out_grad)
    msg_all = lax.all_gather(msg, "tensor", axis=0, tiled=True)

    outs = call(
        functools.partial(attn_bwd_kernel, peers, shares, dims),
        [((depth, pack_w), BF)] * peers + [((own + 16, width), BF)] * shares,
        scratch=[((width, pack_w), F32), ((length, width), F32)],
        smem=1,
    )(idx, msg_all, wall, qkv, att, logs, cosine, sine, seg_c, seg_r, hid, rows_all, x_all)
    w_grads, msg2 = outs[:peers], outs[peers:]
    w_sums = swap(w_grads, "dp")
    total = sum(piece.astype(F32) for piece in w_sums)
    if rep > 1:
        total = lax.psum_scatter(total, "rep", scatter_dimension=0, tiled=True)

    msg2 = swap(msg2, "tensor")
    input_grad, gain_rows = call(
        functools.partial(input_grad_kernel, shares), [((own, width), BF), ((8, width), F32)]
    )(*msg2, layer_input, gains, rgrad)
    gain_cut = gain_rows[:1].reshape(peers, depth)
    gain_cut = lax.all_to_all(gain_cut, "dp", split_axis=0, concat_axis=0, tiled=True)
    gain_attn_grad = jnp.sum(gain_cut, axis=0)
    if rep > 1:
        gain_attn_grad = lax.psum_scatter(gain_attn_grad, "rep", scatter_dimension=0, tiled=True)

    mixed = call(
        functools.partial(combine_kernel, peers, shares),
        [((own, width), BF)] * shares,
        scratch=[((slots, width), BF), ((length, width), F32)],
        smem=1,
    )(idx, gt, *y_in)
    mixed = swap(mixed, "tensor")
    (layer_output,) = call(
        functools.partial(layer_out_kernel, shares), [((own, width), BF)]
    )(*mixed, res)

    gate_grad, up_grad, down_grad = call(
        functools.partial(weight_grad_kernel, peers, shares),
        [((experts, 128, LANES), F32)] * 3,
        smem=1,
    )(idx, *grad_parts)
    if rep > 1:
        gate_grad = lax.psum_scatter(gate_grad, "rep", scatter_dimension=1, tiled=True)
        up_grad = lax.psum_scatter(up_grad, "rep", scatter_dimension=1, tiled=True)
        down_grad = lax.psum_scatter(down_grad, "rep", scatter_dimension=2, tiled=True)
    o_at = all_w + q_w
    return (
        layer_output,
        input_grad,
        gain_attn_grad,
        total[:, o_at + experts] + total[:, o_at + experts + 1],
        total[:, :q_w],
        total[:, q_w : q_w + kv_w],
        total[:, q_w + kv_w : all_w],
        total[:, all_w:o_at].T,
        total[:, o_at : o_at + experts],
        gate_grad,
        up_grad,
        down_grad,
    )


def solution(mesh):
    shares = mesh.shape["tensor"]
    peers = 32 // shares
    rep = mesh.shape["dp"] // peers
    dp = "dp"
    if rep > 1:
        devices = np.asarray(mesh.devices).reshape(peers, rep, shares)
        mesh = jax.sharding.Mesh(devices, ("dp", "rep", "tensor"))
        dp = ("dp", "rep")
    both = ("dp", "tensor") if rep == 1 else ("dp", "rep", "tensor")
    in_specs = (
        P(both, None),
        P(dp, None),
        P(dp, None),
        P(both, None),
        P(dp),
        P(dp),
        P(dp, "tensor"),
        P(dp, "tensor"),
        P(dp, "tensor"),
        P("tensor", dp),
        P(dp, None),
        P(None, dp, "tensor"),
        P(None, dp, "tensor"),
        P(None, "tensor", dp),
    )
    out_specs = (
        P(both, None),
        P(both, None),
        P(dp),
        P(dp),
        P(dp, "tensor"),
        P(dp, "tensor"),
        P(dp, "tensor"),
        P("tensor", dp),
        P(dp, None),
        P(None, dp, "tensor"),
        P(None, dp, "tensor"),
        P(None, "tensor", dp),
    )

    def body(*args):
        return per_device(rep, *args)

    return jax.shard_map(
        body, mesh=mesh, in_specs=in_specs, out_specs=out_specs, check_vma=False
    )
```

profile of v0, /device:TPU:8, one launch (start us, length us, event | category | flops | bytes accessed | tf_op | source)
XLA Modules:
  0.0 533.3 jit_solution(2574772276480360063)
XLA Ops:
  14.1 8.2 %all_gather.12.grads = bf16[256,1024]{1,0:T(8,128)(2,1)} all-gather(bf16[64,1024]{1,0:T(8,128)(2,1)} %refs_8_.1), channel_id=1, replica_groups=mesh['dp'=8,'tensor'=4] {'tensor'}, dimensions={0}, use_global_device_ids=true | all-gather | bytes 655360 | tf_op jit(solution)/shard_map/all_gather | solution.py:504
  22.3 8.2 %all_gather.13.refs_1_.refs_12_ = bf16[256,1024]{1,0:T(8,128)(2,1)} all-gather(bf16[64,1024]{1,0:T(8,128)(2,1)} %refs_4_.3), channel_id=1, replica_groups=mesh['dp'=8,'tensor'=4] {'tensor'}, dimensions={0}, use_global_device_ids=true | all-gather | bytes 655360 | tf_op jit(solution)/shard_map/all_gather | solution.py:491
  62.9 5.5 %shard_map.230 = (bf16[64,1024]{1,0:T(8,128)(2,1)}, bf16[64,1024]{1,0:T(8,128)(2,1)}, bf16[64,1024]{1,0:T(8,128)(2,1)}, bf16[64,1024]{1,0:T(8,128)(2,1)}, bf16[1...) custom-call(s32[2]{0:T(128)} %pad_add_fusion.idx.refs_0_, ...), custom_call_target="tpu_custom_call" | custom-call | tf_op jit(solution)/shard_map/pallas_call | solution.py:32
  71.7 26.8 %collective-permute-done.8.refs_2_ = bf16[64,1024]{1,0:T(8,128)(2,1)S(1)} collective-permute-done((bf16[64,1024]{1,0:T(8,128)(2,1)}, bf16[64,1024]{1,0:T(8,128)(2,1)S(1)}, u32[]{:S(2)}, u32[]{:S(2)}) %collective-permute-start.8) | collective-permute-done | bytes 131104 | tf_op jit(solution)/shard_map/ppermute | solution.py:427
  105.1 9.4 %all_gather.14.rows.refs_11_ = bf16[256,1152]{1,0:T(8,128)(2,1)} all-gather(bf16[64,1152]{1,0:T(8,128)(2,1)} %get-tuple-element.152), channel_id=1, replica_groups=mesh['dp'=8,'tensor'=4] {'tensor'}, dimensions={0}, use_global_device_ids=true | all-gather | bytes 737280 | tf_op jit(solution)/shard_map/all_gather | solution.py:538
  131.3 5.5 %collective-permute-done.23.refs_16_ = bf16[128,1024]{1,0:T(8,128)(2,1)S(1)} collective-permute-done((bf16[128,1024]{1,0:T(8,128)(2,1)}, bf16[128,1024]{1,0:T(8,128)(2,1)S(1)}, u32[]{:S(2)}, u32[]{:S(2)}) %collective-permute-start.23) | collective-permute-done | bytes 262176 | tf_op jit(solution)/shard_map/ppermute | solution.py:427
  142.3 7.7 %collective-permute-done.12.refs_4_ = bf16[128,1152]{1,0:T(8,128)(2,1)S(1)} collective-permute-done((bf16[128,1152]{1,0:T(8,128)(2,1)}, bf16[128,1152]{1,0:T(8,128)(2,1)S(1)}, u32[]{:S(2)}, u32[]{:S(2)}) %collective-permute-start.12) | collective-permute-done | bytes 294944 | tf_op jit(solution)/shard_map/ppermute | solution.py:427
  150.0 4.7 collective-permute-start.15
  155.7 10.8 %collective-permute-done.14.refs_6_ = bf16[128,1152]{1,0:T(8,128)(2,1)S(1)} collective-permute-done((bf16[128,1152]{1,0:T(8,128)(2,1)}, bf16[128,1152]{1,0:T(8,128)(2,1)S(1)}, u32[]{:S(2)}, u32[]{:S(2)}) %collective-permute-start.14) | collective-permute-done | bytes 294944 | tf_op jit(solution)/shard_map/ppermute | solution.py:427
  166.6 14.5 %collective-permute-done.15.refs_7_ = bf16[128,1152]{1,0:T(8,128)(2,1)S(1)} collective-permute-done((bf16[128,1152]{1,0:T(8,128)(2,1)}, bf16[128,1152]{1,0:T(8,128)(2,1)S(1)}, u32[]{:S(2)}, u32[]{:S(2)}) %collective-permute-start.15) | collective-permute-done | bytes 294944 | tf_op jit(solution)/shard_map/ppermute | solution.py:427
  181.1 18.8 %collective-permute-done.16.refs_8_ = bf16[128,1152]{1,0:T(8,128)(2,1)S(1)} collective-permute-done((bf16[128,1152]{1,0:T(8,128)(2,1)S(1)}, bf16[128,1152]{1,0:T(8,128)(2,1)S(1)}, u32[]{:S(2)}, u32[]{:S(2)}) %collective-permute-start.16) | collective-permute-done | bytes 294944 | tf_op jit(solution)/shard_map/ppermute | solution.py:427
  204.3 25.4 %collective-permute-done.30.refs_21_ = bf16[4,384,128]{2,1,0:T(8,128)(2,1)S(1)} collective-permute-done((bf16[4,384,128]{2,1,0:T(8,128)(2,1)}, bf16[4,384,128]{2,1,0:T(8,128)(2,1)S(1)}, u32[]{:S(2)}, u32[]{:S(2)}) %collective-permute-start.30) | collective-permute-done | bytes 393248 | tf_op jit(solution)/shard_map/ppermute | solution.py:427
  229.7 8.4 %collective-permute-done.31.refs_22_ = bf16[4,384,128]{2,1,0:T(8,128)(2,1)S(1)} collective-permute-done((bf16[4,384,128]{2,1,0:T(8,128)(2,1)}, bf16[4,384,128]{2,1,0:T(8,128)(2,1)S(1)}, u32[]{:S(2)}, u32[]{:S(2)}) %collective-permute-start.31) | collective-permute-done | bytes 393248 | tf_op jit(solution)/shard_map/ppermute | solution.py:427
  238.1 10.2 %collective-permute-done.32.refs_23_ = bf16[4,384,128]{2,1,0:T(8,128)(2,1)S(1)} collective-permute-done((bf16[4,384,128]{2,1,0:T(8,128)(2,1)}, bf16[4,384,128]{2,1,0:T(8,128)(2,1)S(1)}, u32[]{:S(2)}, u32[]{:S(2)}) %collective-permute-start.32) | collective-permute-done | bytes 393248 | tf_op jit(solution)/shard_map/ppermute | solution.py:427
  248.3 6.3 %collective-permute-done.33.refs_24_ = bf16[4,384,128]{2,1,0:T(8,128)(2,1)S(1)} collective-permute-done((bf16[4,384,128]{2,1,0:T(8,128)(2,1)}, bf16[4,384,128]{2,1,0:T(8,128)(2,1)S(1)}, u32[]{:S(2)}, u32[]{:S(2)}) %collective-permute-start.33) | collective-permute-done | bytes 393248 | tf_op jit(solution)/shard_map/ppermute | solution.py:427
  255.4 13.2 %shard_map.235 = (bf16[128,1152]{1,0:T(8,128)(2,1)}, bf16[128,1152]{1,0:T(8,128)(2,1)}, bf16[128,1152]{1,0:T(8,128)(2,1)}, bf16[128,1152]{1,0:T(8,128)(2,1)}, bf...) custom-call(s32[2]{0:T(128)} %pad_add_fusion.idx.refs_0_, ...), custom_call_target="tpu_custom_call" | custom-call | tf_op jit(solution)/shard_map/pallas_call | solution.py:32
  280.4 9.9 %collective-permute-done.35.refs_4_ = bf16[128,1152]{1,0:T(8,128)(2,1)S(1)} collective-permute-done((bf16[128,1152]{1,0:T(8,128)(2,1)}, bf16[128,1152]{1,0:T(8,128)(2,1)S(1)}, u32[]{:S(2)}, u32[]{:S(2)}) %collective-permute-start.35) | collective-permute-done | bytes 294944 | tf_op jit(solution)/shard_map/ppermute | solution.py:427
  291.1 12.4 %shard_map.236 = (bf16[128,1024]{1,0:T(8,128)(2,1)}, bf16[128,1024]{1,0:T(8,128)(2,1)}, bf16[128,1024]{1,0:T(8,128)(2,1)}, bf16[128,1024]{1,0:T(8,128)(2,1)}, bf...) custom-call(s32[2]{0:T(128)} %pad_add_fusion.idx.refs_0_, ...), custom_call_target="tpu_custom_call" | custom-call | tf_op jit(solution)/shard_map/pallas_call | solution.py:32
  303.6 9.8 %collective-permute-done.38.refs_7_ = bf16[128,1152]{1,0:T(8,128)(2,1)S(1)} collective-permute-done((bf16[128,1152]{1,0:T(8,128)(2,1)}, bf16[128,1152]{1,0:T(8,128)(2,1)S(1)}, u32[]{:S(2)}, u32[]{:S(2)}) %collective-permute-start.38) | collective-permute-done | bytes 294944 | tf_op jit(solution)/shard_map/ppermute | solution.py:427
  313.4 7.4 %collective-permute-done.39.refs_8_ = bf16[128,1152]{1,0:T(8,128)(2,1)S(1)} collective-permute-done((bf16[128,1152]{1,0:T(8,128)(2,1)}, bf16[128,1152]{1,0:T(8,128)(2,1)S(1)}, u32[]{:S(2)}, u32[]{:S(2)}) %collective-permute-start.39) | collective-permute-done | bytes 294944 | tf_op jit(solution)/shard_map/ppermute | solution.py:427
  320.9 5.0 collective-permute-done.40.refs_9_
  347.2 10.3 %collective-permute-done.44.refs_6_ = bf16[128,1024]{1,0:T(8,128)(2,1)S(1)} collective-permute-done((bf16[128,1024]{1,0:T(8,128)(2,1)}, bf16[128,1024]{1,0:T(8,128)(2,1)S(1)}, u32[]{:S(2)}, u32[]{:S(2)}) %collective-permute-start.44) | collective-permute-done | bytes 262176 | tf_op jit(solution)/shard_map/ppermute | solution.py:427
  358.8 24.0 %all_gather.15.refs_1_ = bf16[320,1152]{1,0:T(8,128)(2,1)} all-gather(bf16[80,1152]{1,0:T(8,128)(2,1)} %get-tuple-element.225), channel_id=1, replica_groups=mesh['dp'=8,'tensor'=4] {'tensor'}, dimensions={0}, use_global_device_ids=true | all-gather | bytes 921600 | tf_op jit(solution)/shard_map/all_gather | solution.py:583
  382.8 6.8 %shard_map.241 = (bf16[128,896]{1,0:T(8,128)(2,1)}, bf16[128,896]{1,0:T(8,128)(2,1)}, bf16[128,896]{1,0:T(8,128)(2,1)}, bf16[128,896]{1,0:T(8,128)(2,1)}, bf16[1...) custom-call(s32[2]{0:T(128)} %pad_add_fusion.idx.refs_0_, ...), custom_call_target="tpu_custom_call" | custom-call | tf_op jit(solution)/shard_map/pallas_call | solution.py:32
  391.5 5.8 %collective-permute-done.55.refs_2_ = bf16[80,1024]{1,0:T(8,128)(2,1)S(1)} collective-permute-done((bf16[80,1024]{1,0:T(8,128)(2,1)}, bf16[80,1024]{1,0:T(8,128)(2,1)S(1)}, u32[]{:S(2)}, u32[]{:S(2)}) %collective-permute-start.55) | collective-permute-done | bytes 163872 | tf_op jit(solution)/shard_map/ppermute | solution.py:427
  423.5 11.9 %collective-permute-start.68 = (bf16[4,384,128]{2,1,0:T(8,128)(2,1)}, bf16[4,384,128]{2,1,0:T(8,128)(2,1)S(1)}, u32[]{:S(2)}, u32[]{:S(2)}) collective-permute-start(bf16[4,384,128]{2,1,0:T(8,128)(2,1)} %get-tuple-element.251), channel_id=1, source_target_pairs={{0,8},{4,12},{8,0},{12,4},{16,24},{20,28},{24,16},{28,20},{1,9},{5... | collective-permute-start | bytes 1179656 | tf_op jit(solution)/shard_map/ppermute | solution.py:427
  444.4 5.8 %all-to-all-done = f32[8,1,128]{2,1,0:T(1,128)S(1)} async-done(((f32[8,1,128]{2,1,0:T(1,128)}), f32[8,1,128]{2,1,0:T(1,128)S(1)}, u32[]{:S(2)}, u32[]{:S(2)}) %all-to-all-start) | async-done | bytes 4128 | tf_op jit(solution)/shard_map/all_to_all | solution.py:602
  469.9 32.7 %collective-permute-done.70.refs_4_ = bf16[4,384,128]{2,1,0:T(8,128)(2,1)S(1)} collective-permute-done((bf16[4,384,128]{2,1,0:T(8,128)(2,1)}, bf16[4,384,128]{2,1,0:T(8,128)(2,1)S(1)}, u32[]{:S(2)}, u32[]{:S(2)}) %collective-permute-start.70) | collective-permute-done | bytes 393248 | tf_op jit(solution)/shard_map/ppermute | solution.py:427
  502.6 8.4 %collective-permute-done.71.refs_5_ = bf16[4,384,128]{2,1,0:T(8,128)(2,1)S(1)} collective-permute-done((bf16[4,384,128]{2,1,0:T(8,128)(2,1)}, bf16[4,384,128]{2,1,0:T(8,128)(2,1)S(1)}, u32[]{:S(2)}, u32[]{:S(2)}) %collective-permute-start.71) | collective-permute-done | bytes 393248 | tf_op jit(solution)/shard_map/ppermute | solution.py:427
  511.0 10.0 %collective-permute-done.72.refs_6_ = bf16[4,384,128]{2,1,0:T(8,128)(2,1)S(1)} collective-permute-done((bf16[4,384,128]{2,1,0:T(8,128)(2,1)}, bf16[4,384,128]{2,1,0:T(8,128)(2,1)S(1)}, u32[]{:S(2)}, u32[]{:S(2)}) %collective-permute-start.72) | collective-permute-done | bytes 393248 | tf_op jit(solution)/shard_map/ppermute | solution.py:427
  521.0 6.6 %collective-permute-done.73.refs_7_ = bf16[4,384,128]{2,1,0:T(8,128)(2,1)S(1)} collective-permute-done((bf16[4,384,128]{2,1,0:T(8,128)(2,1)}, bf16[4,384,128]{2,1,0:T(8,128)(2,1)S(1)}, u32[]{:S(2)}, u32[]{:S(2)}) %collective-permute-start.73) | collective-permute-done | bytes 393248 | tf_op jit(solution)/shard_map/ppermute | solution.py:427
  528.3 4.9 shard_map.244
  (295 shorter events, 176.8 us)
Async XLA Ops:
  8.0 35.5 %collective-permute-start.4 = (bf16[128,896]{1,0:T(8,128)(2,1)S(1)}, bf16[128,896]{1,0:T(8,128)(2,1)S(1)}, u32[]{:S(2)}, u32[]{:S(2)}) collective-permute-start(bf16[128,896]{1,0:T(8,128)(2,1)S(1)} %concatenate.3.refs_2_), channel_id=1, source_target_pairs={{0,20},{4,16},{8,28},{12,24},{16,4},{20,0},{24,12},{28,8},{1,21},{... | collective-permute-start | bytes 688136 | tf_op jit(solution)/shard_map/ppermute | solution.py:427
  12.4 34.9 %collective-permute-start.3 = (bf16[128,896]{1,0:T(8,128)(2,1)S(1)}, bf16[128,896]{1,0:T(8,128)(2,1)S(1)}, u32[]{:S(2)}, u32[]{:S(2)}) collective-permute-start(bf16[128,896]{1,0:T(8,128)(2,1)S(1)} %concatenate.3.refs_2_), channel_id=1, source_target_pairs={{0,16},{4,20},{8,24},{12,28},{16,0},{20,4},{24,8},{28,12},{1,17},{... | collective-permute-start | bytes 688136 | tf_op jit(solution)/shard_map/ppermute | solution.py:427
  12.4 37.6 %collective-permute-start.2 = (bf16[128,896]{1,0:T(8,128)(2,1)S(1)}, bf16[128,896]{1,0:T(8,128)(2,1)S(1)}, u32[]{:S(2)}, u32[]{:S(2)}) collective-permute-start(bf16[128,896]{1,0:T(8,128)(2,1)S(1)} %concatenate.3.refs_2_), channel_id=1, source_target_pairs={{0,12},{4,8},{8,4},{12,0},{16,28},{20,24},{24,20},{28,16},{1,13},{... | collective-permute-start | bytes 688136 | tf_op jit(solution)/shard_map/ppermute | solution.py:427
  58.2 65.9 %collective-permute-start.24 = (bf16[8,384,128]{2,1,0:T(8,128)(2,1)}, bf16[8,384,128]{2,1,0:T(8,128)(2,1)S(1)}, u32[]{:S(2)}, u32[]{:S(2)}) collective-permute-start(bf16[8,384,128]{2,1,0:T(8,128)(2,1)} %get-tuple-element.170), channel_id=1, source_target_pairs={{0,1},{1,0},{2,3},{3,2},{4,5},{5,4},{6,7},{7,6},{8,9},{9,8},{10,11... | collective-permute-start | bytes 2359304 | tf_op jit(solution)/shard_map/ppermute | solution.py:427
  58.2 65.9 %collective-permute-start.25 = (bf16[8,384,128]{2,1,0:T(8,128)(2,1)}, bf16[8,384,128]{2,1,0:T(8,128)(2,1)}, u32[]{:S(2)}, u32[]{:S(2)}) collective-permute-start(bf16[8,384,128]{2,1,0:T(8,128)(2,1)} %get-tuple-element.171), channel_id=1, source_target_pairs={{0,2},{1,3},{2,0},{3,1},{4,6},{5,7},{6,4},{7,5},{8,10},{9,11},{10,... | collective-permute-start | bytes 2359304 | tf_op jit(solution)/shard_map/ppermute | solution.py:427
  61.4 65.7 %collective-permute-start.26 = (bf16[8,384,128]{2,1,0:T(8,128)(2,1)}, bf16[8,384,128]{2,1,0:T(8,128)(2,1)}, u32[]{:S(2)}, u32[]{:S(2)}) collective-permute-start(bf16[8,384,128]{2,1,0:T(8,128)(2,1)} %get-tuple-element.172), channel_id=1, source_target_pairs={{0,3},{1,2},{2,1},{3,0},{4,7},{5,6},{6,5},{7,4},{8,11},{9,10},{10,... | collective-permute-start | bytes 2359304 | tf_op jit(solution)/shard_map/ppermute | solution.py:427
  137.4 62.5 %collective-permute-start.27 = (bf16[4,384,128]{2,1,0:T(8,128)(2,1)}, bf16[4,384,128]{2,1,0:T(8,128)(2,1)S(1)}, u32[]{:S(2)}, u32[]{:S(2)}) collective-permute-start(bf16[4,384,128]{2,1,0:T(8,128)(2,1)} %get-tuple-element.174), channel_id=1, source_target_pairs={{0,4},{4,0},{8,12},{12,8},{16,20},{20,16},{24,28},{28,24},{1,5},{5... | collective-permute-start | bytes 1179656 | tf_op jit(solution)/shard_map/ppermute | solution.py:427
  138.8 61.9 %collective-permute-start.28 = (bf16[4,384,128]{2,1,0:T(8,128)(2,1)}, bf16[4,384,128]{2,1,0:T(8,128)(2,1)S(1)}, u32[]{:S(2)}, u32[]{:S(2)}) collective-permute-start(bf16[4,384,128]{2,1,0:T(8,128)(2,1)} %get-tuple-element.175), channel_id=1, source_target_pairs={{0,8},{4,12},{8,0},{12,4},{16,24},{20,28},{24,16},{28,20},{1,9},{5... | collective-permute-start | bytes 1179656 | tf_op jit(solution)/shard_map/ppermute | solution.py:427
  154.7 45.3 %collective-permute-start.16 = (bf16[128,1152]{1,0:T(8,128)(2,1)S(1)}, bf16[128,1152]{1,0:T(8,128)(2,1)S(1)}, u32[]{:S(2)}, u32[]{:S(2)}) collective-permute-start(bf16[128,1152]{1,0:T(8,128)(2,1)S(1)} %copy-done.66), channel_id=1, source_target_pairs={{0,28},{4,24},{8,20},{12,16},{16,12},{20,8},{24,4},{28,0},{1,29},{... | collective-permute-start | bytes 884744 | tf_op jit(solution)/shard_map/ppermute | solution.py:427
  166.5 37.8 %collective-permute-start.29 = (bf16[4,384,128]{2,1,0:T(8,128)(2,1)}, bf16[4,384,128]{2,1,0:T(8,128)(2,1)S(1)}, u32[]{:S(2)}, u32[]{:S(2)}) collective-permute-start(bf16[4,384,128]{2,1,0:T(8,128)(2,1)} %get-tuple-element.176), channel_id=1, source_target_pairs={{0,12},{4,8},{8,4},{12,0},{16,28},{20,24},{24,20},{28,16},{1,13},{... | collective-permute-start | bytes 1179656 | tf_op jit(solution)/shard_map/ppermute | solution.py:427
  181.1 48.5 %collective-permute-start.30 = (bf16[4,384,128]{2,1,0:T(8,128)(2,1)}, bf16[4,384,128]{2,1,0:T(8,128)(2,1)S(1)}, u32[]{:S(2)}, u32[]{:S(2)}) collective-permute-start(bf16[4,384,128]{2,1,0:T(8,128)(2,1)} %get-tuple-element.177), channel_id=1, source_target_pairs={{0,16},{4,20},{8,24},{12,28},{16,0},{20,4},{24,8},{28,12},{1,17},{... | collective-permute-start | bytes 1179656 | tf_op jit(solution)/shard_map/ppermute | solution.py:427
  199.9 38.2 %collective-permute-start.31 = (bf16[4,384,128]{2,1,0:T(8,128)(2,1)}, bf16[4,384,128]{2,1,0:T(8,128)(2,1)S(1)}, u32[]{:S(2)}, u32[]{:S(2)}) collective-permute-start(bf16[4,384,128]{2,1,0:T(8,128)(2,1)} %get-tuple-element.178), channel_id=1, source_target_pairs={{0,20},{4,16},{8,28},{12,24},{16,4},{20,0},{24,12},{28,8},{1,21},{... | collective-permute-start | bytes 1179656 | tf_op jit(solution)/shard_map/ppermute | solution.py:427
  200.7 47.7 %collective-permute-start.32 = (bf16[4,384,128]{2,1,0:T(8,128)(2,1)}, bf16[4,384,128]{2,1,0:T(8,128)(2,1)S(1)}, u32[]{:S(2)}, u32[]{:S(2)}) collective-permute-start(bf16[4,384,128]{2,1,0:T(8,128)(2,1)} %get-tuple-element.179), channel_id=1, source_target_pairs={{0,24},{4,28},{8,16},{12,20},{16,8},{20,12},{24,0},{28,4},{1,25},{... | collective-permute-start | bytes 1179656 | tf_op jit(solution)/shard_map/ppermute | solution.py:427
  200.7 54.0 %collective-permute-start.33 = (bf16[4,384,128]{2,1,0:T(8,128)(2,1)}, bf16[4,384,128]{2,1,0:T(8,128)(2,1)S(1)}, u32[]{:S(2)}, u32[]{:S(2)}) collective-permute-start(bf16[4,384,128]{2,1,0:T(8,128)(2,1)} %get-tuple-element.180), channel_id=1, source_target_pairs={{0,28},{4,24},{8,20},{12,16},{16,12},{20,8},{24,4},{28,0},{1,29},{... | collective-permute-start | bytes 1179656 | tf_op jit(solution)/shard_map/ppermute | solution.py:427
  271.4 32.2 %collective-permute-start.36 = (bf16[128,1152]{1,0:T(8,128)(2,1)}, bf16[128,1152]{1,0:T(8,128)(2,1)S(1)}, u32[]{:S(2)}, u32[]{:S(2)}) collective-permute-start(bf16[128,1152]{1,0:T(8,128)(2,1)} %get-tuple-element.184), channel_id=1, source_target_pairs={{0,12},{4,8},{8,4},{12,0},{16,28},{20,24},{24,20},{28,16},{1,13},{... | collective-permute-start | bytes 884744 | tf_op jit(solution)/shard_map/ppermute | solution.py:427
  274.1 39.3 %collective-permute-start.38 = (bf16[128,1152]{1,0:T(8,128)(2,1)}, bf16[128,1152]{1,0:T(8,128)(2,1)S(1)}, u32[]{:S(2)}, u32[]{:S(2)}) collective-permute-start(bf16[128,1152]{1,0:T(8,128)(2,1)} %get-tuple-element.186), channel_id=1, source_target_pairs={{0,20},{4,16},{8,28},{12,24},{16,4},{20,0},{24,12},{28,8},{1,21},{... | collective-permute-start | bytes 884744 | tf_op jit(solution)/shard_map/ppermute | solution.py:427
  278.5 42.4 %collective-permute-start.39 = (bf16[128,1152]{1,0:T(8,128)(2,1)}, bf16[128,1152]{1,0:T(8,128)(2,1)S(1)}, u32[]{:S(2)}, u32[]{:S(2)}) collective-permute-start(bf16[128,1152]{1,0:T(8,128)(2,1)} %get-tuple-element.187), channel_id=1, source_target_pairs={{0,24},{4,28},{8,16},{12,20},{16,8},{20,12},{24,0},{28,4},{1,25},{... | collective-permute-start | bytes 884744 | tf_op jit(solution)/shard_map/ppermute | solution.py:427
  290.2 35.6 %collective-permute-start.40 = (bf16[128,1152]{1,0:T(8,128)(2,1)}, bf16[128,1152]{1,0:T(8,128)(2,1)S(1)}, u32[]{:S(2)}, u32[]{:S(2)}) collective-permute-start(bf16[128,1152]{1,0:T(8,128)(2,1)} %get-tuple-element.188), channel_id=1, source_target_pairs={{0,28},{4,24},{8,20},{12,16},{16,12},{20,8},{24,4},{28,0},{1,29},{... | collective-permute-start | bytes 884744 | tf_op jit(solution)/shard_map/ppermute | solution.py:427
  340.5 59.3 %collective-permute-start.64 = (bf16[8,384,128]{2,1,0:T(8,128)(2,1)}, bf16[8,384,128]{2,1,0:T(8,128)(2,1)S(1)}, u32[]{:S(2)}, u32[]{:S(2)}) collective-permute-start(bf16[8,384,128]{2,1,0:T(8,128)(2,1)} %get-tuple-element.246), channel_id=1, source_target_pairs={{0,1},{1,0},{2,3},{3,2},{4,5},{5,4},{6,7},{7,6},{8,9},{9,8},{10,11... | collective-permute-start | bytes 2359304 | tf_op jit(solution)/shard_map/ppermute | solution.py:427
  340.5 62.0 %collective-permute-start.65 = (bf16[8,384,128]{2,1,0:T(8,128)(2,1)}, bf16[8,384,128]{2,1,0:T(8,128)(2,1)S(1)}, u32[]{:S(2)}, u32[]{:S(2)}) collective-permute-start(bf16[8,384,128]{2,1,0:T(8,128)(2,1)} %get-tuple-element.247), channel_id=1, source_target_pairs={{0,2},{1,3},{2,0},{3,1},{4,6},{5,7},{6,4},{7,5},{8,10},{9,11},{10,... | collective-permute-start | bytes 2359304 | tf_op jit(solution)/shard_map/ppermute | solution.py:427
  341.1 61.5 %collective-permute-start.66 = (bf16[8,384,128]{2,1,0:T(8,128)(2,1)}, bf16[8,384,128]{2,1,0:T(8,128)(2,1)S(1)}, u32[]{:S(2)}, u32[]{:S(2)}) collective-permute-start(bf16[8,384,128]{2,1,0:T(8,128)(2,1)} %get-tuple-element.248), channel_id=1, source_target_pairs={{0,3},{1,2},{2,1},{3,0},{4,7},{5,6},{6,5},{7,4},{8,11},{9,10},{10,... | collective-permute-start | bytes 2359304 | tf_op jit(solution)/shard_map/ppermute | solution.py:427
  344.9 44.7 %collective-permute-start.45 = (bf16[128,1024]{1,0:T(8,128)(2,1)}, bf16[128,1024]{1,0:T(8,128)(2,1)}, u32[]{:S(2)}, u32[]{:S(2)}) collective-permute-start(bf16[128,1024]{1,0:T(8,128)(2,1)} %get-tuple-element.204), channel_id=1, source_target_pairs={{0,20},{4,16},{8,28},{12,24},{16,4},{20,0},{24,12},{28,8},{1,21},{... | collective-permute-start | bytes 786440 | tf_op jit(solution)/shard_map/ppermute | solution.py:427
  357.5 32.5 %collective-permute-start.46 = (bf16[128,1024]{1,0:T(8,128)(2,1)}, bf16[128,1024]{1,0:T(8,128)(2,1)}, u32[]{:S(2)}, u32[]{:S(2)}) collective-permute-start(bf16[128,1024]{1,0:T(8,128)(2,1)} %get-tuple-element.205), channel_id=1, source_target_pairs={{0,24},{4,28},{8,16},{12,20},{16,8},{20,12},{24,0},{28,4},{1,25},{... | collective-permute-start | bytes 786440 | tf_op jit(solution)/shard_map/ppermute | solution.py:427
  412.6 38.2 %collective-permute-start.61 = (bf16[128,896]{1,0:T(8,128)(2,1)}, bf16[128,896]{1,0:T(8,128)(2,1)S(1)}, u32[]{:S(2)}, u32[]{:S(2)}) collective-permute-start(bf16[128,896]{1,0:T(8,128)(2,1)} %get-tuple-element.242), channel_id=1, source_target_pairs={{0,20},{4,16},{8,28},{12,24},{16,4},{20,0},{24,12},{28,8},{1,21},{... | collective-permute-start | bytes 688136 | tf_op jit(solution)/shard_map/ppermute | solution.py:427
  413.4 37.4 %collective-permute-start.62 = (bf16[128,896]{1,0:T(8,128)(2,1)}, bf16[128,896]{1,0:T(8,128)(2,1)S(1)}, u32[]{:S(2)}, u32[]{:S(2)}) collective-permute-start(bf16[128,896]{1,0:T(8,128)(2,1)} %get-tuple-element.243), channel_id=1, source_target_pairs={{0,24},{4,28},{8,16},{12,20},{16,8},{20,12},{24,0},{28,4},{1,25},{... | collective-permute-start | bytes 688136 | tf_op jit(solution)/shard_map/ppermute | solution.py:427
  415.9 35.3 %collective-permute-start.63 = (bf16[128,896]{1,0:T(8,128)(2,1)}, bf16[128,896]{1,0:T(8,128)(2,1)S(1)}, u32[]{:S(2)}, u32[]{:S(2)}) collective-permute-start(bf16[128,896]{1,0:T(8,128)(2,1)} %get-tuple-element.244), channel_id=1, source_target_pairs={{0,28},{4,24},{8,20},{12,16},{16,12},{20,8},{24,4},{28,0},{1,29},{... | collective-permute-start | bytes 688136 | tf_op jit(solution)/shard_map/ppermute | solution.py:427
  421.6 40.0 %collective-permute-start.67 = (bf16[4,384,128]{2,1,0:T(8,128)(2,1)}, bf16[4,384,128]{2,1,0:T(8,128)(2,1)S(1)}, u32[]{:S(2)}, u32[]{:S(2)}) collective-permute-start(bf16[4,384,128]{2,1,0:T(8,128)(2,1)} %get-tuple-element.250), channel_id=1, source_target_pairs={{0,4},{4,0},{8,12},{12,8},{16,20},{20,16},{24,28},{28,24},{1,5},{5... | collective-permute-start | bytes 1179656 | tf_op jit(solution)/shard_map/ppermute | solution.py:427
  423.5 39.2 %collective-permute-start.68 = (bf16[4,384,128]{2,1,0:T(8,128)(2,1)}, bf16[4,384,128]{2,1,0:T(8,128)(2,1)S(1)}, u32[]{:S(2)}, u32[]{:S(2)}) collective-permute-start(bf16[4,384,128]{2,1,0:T(8,128)(2,1)} %get-tuple-element.251), channel_id=1, source_target_pairs={{0,8},{4,12},{8,0},{12,4},{16,24},{20,28},{24,16},{28,20},{1,9},{5... | collective-permute-start | bytes 1179656 | tf_op jit(solution)/shard_map/ppermute | solution.py:427
  457.4 45.1 %collective-permute-start.70 = (bf16[4,384,128]{2,1,0:T(8,128)(2,1)}, bf16[4,384,128]{2,1,0:T(8,128)(2,1)S(1)}, u32[]{:S(2)}, u32[]{:S(2)}) collective-permute-start(bf16[4,384,128]{2,1,0:T(8,128)(2,1)} %get-tuple-element.253), channel_id=1, source_target_pairs={{0,16},{4,20},{8,24},{12,28},{16,0},{20,4},{24,8},{28,12},{1,17},{... | collective-permute-start | bytes 1179656 | tf_op jit(solution)/shard_map/ppermute | solution.py:427
  459.8 51.2 %collective-permute-start.71 = (bf16[4,384,128]{2,1,0:T(8,128)(2,1)}, bf16[4,384,128]{2,1,0:T(8,128)(2,1)S(1)}, u32[]{:S(2)}, u32[]{:S(2)}) collective-permute-start(bf16[4,384,128]{2,1,0:T(8,128)(2,1)} %get-tuple-element.254), channel_id=1, source_target_pairs={{0,20},{4,16},{8,28},{12,24},{16,4},{20,0},{24,12},{28,8},{1,21},{... | collective-permute-start | bytes 1179656 | tf_op jit(solution)/shard_map/ppermute | solution.py:427
  461.6 59.4 %collective-permute-start.72 = (bf16[4,384,128]{2,1,0:T(8,128)(2,1)}, bf16[4,384,128]{2,1,0:T(8,128)(2,1)S(1)}, u32[]{:S(2)}, u32[]{:S(2)}) collective-permute-start(bf16[4,384,128]{2,1,0:T(8,128)(2,1)} %get-tuple-element.255), channel_id=1, source_target_pairs={{0,24},{4,28},{8,16},{12,20},{16,8},{20,12},{24,0},{28,4},{1,25},{... | collective-permute-start | bytes 1179656 | tf_op jit(solution)/shard_map/ppermute | solution.py:427
  462.7 64.9 %collective-permute-start.73 = (bf16[4,384,128]{2,1,0:T(8,128)(2,1)}, bf16[4,384,128]{2,1,0:T(8,128)(2,1)S(1)}, u32[]{:S(2)}, u32[]{:S(2)}) collective-permute-start(bf16[4,384,128]{2,1,0:T(8,128)(2,1)} %get-tuple-element.256), channel_id=1, source_target_pairs={{0,28},{4,24},{8,20},{12,16},{16,12},{20,8},{24,4},{28,0},{1,29},{... | collective-permute-start | bytes 1179656 | tf_op jit(solution)/shard_map/ppermute | solution.py:427
  (110 other events, 2381.1 us)
where the time goes:
time: 534 us; the launch traced here: 533 us
  waiting for transfers between devices  281 us (53%)
  starting transfers between devices  105 us (20%)
  Pallas kernels  76 us (14%)
  blocking collectives  49.9 us (9%)
  local copies, waits for them, and re-layouts  16.7 us (3%)
    ppermute x74, waiting for transfers between devices, swap(): lax.ppermute(values[m], axis, [(i, i ^ m) for i in range(len(values))])  275 us
    ppermute x74, starting transfers between devices, swap(): lax.ppermute(values[m], axis, [(i, i ^ m) for i in range(len(values))])  101 us
    pallas_call x16, Pallas kernels, run(): pl.pallas_call(kernel, out_shape=[jax.ShapeDtypeStruct(s, d) for s, d in...  76 us
    all_gather x1, blocking collectives, per_device(): msg_all = lax.all_gather(msg, 'tensor', axis=0, tiled=True)  24 us
  transfers between devices with their start and end apart: 75, of which 40 were waited for; matrix products, arithmetic and copies ran while one was open for 2% of the time, Pallas kernels for 11%

commit v1 on v0

--- a/solution.py
+++ b/solution.py
@@ -16,6 +16,10 @@
 eps_norm = 1e-05
 score_scale = 0.125
 rope_base = 10000.0
+
+TOKEN_BITS = (4, 2, 1)
+QKV_BITS = (4, 2, 1)
+REST_BITS = (1, 4, 2)
 
 BF = jnp.bfloat16
 F32 = jnp.float32
@@ -77,6 +81,13 @@
     return (seg_col == seg_row) & (rows >= cols)
 
 
+def visit_order(bits):
+    order = [0]
+    for bit in bits:
+        order = order + [m ^ bit for m in order]
+    return order
+
+
 def scatter_rows(whole, parts, own):
     span = parts[0].shape[0]
     for s, out in enumerate(parts):
@@ -87,13 +98,19 @@
 def attn_fwd_kernel(peers, shares, dims, *refs):
     n_q, n_kv = dims
     (idx,), (x,), w_in, (cos, sin, seg_c, seg_r), parts, outs, (part,) = split_refs(
-        refs, 1, 1, peers, 4, shares, 6, 1
+        refs, 1, 1, 4, 4, shares, 6, 1
     )
     wall, gains, qkv, att, log_out, hid = outs
-    rows = w_in[0].shape[0]
-    for m in range(peers):
-        at = pl.multiple_of(jnp.bitwise_xor(idx[0], m) * rows, rows)
-        wall[pl.ds(at, rows), :] = w_in[m][...]
+    rows = wall.shape[0] // peers
+    column = 0
+    for pair, bits in ((w_in[:2], QKV_BITS), (w_in[2:], REST_BITS)):
+        cols = slice(column, column + pair[0].shape[1])
+        column = column + pair[0].shape[1]
+        for k, m in enumerate(visit_order(bits)):
+            at = pl.multiple_of(jnp.bitwise_xor(idx[0], m) * rows, rows)
+            got = pair[k // (peers // 2)]
+            k = k % (peers // 2)
+            wall[pl.ds(at, rows), cols] = got[k * rows : (k + 1) * rows, :]
     qk_w = (n_q + n_kv) * HD
     all_w = (n_q + 2 * n_kv) * HD
     o_at = all_w + n_q * HD
@@ -134,7 +151,7 @@
 
 
 def post_attn_kernel(experts, shares, *refs):
-    parts, (x, gains, misc, res, router, msg) = split_refs(refs, shares, 6)
+    parts, (x, ids, gains, misc, res, router, msg) = split_refs(refs, shares, 7)
     width = x.shape[1]
     total = x[...].astype(F32)
     for part in parts:
@@ -148,35 +165,11 @@
     probs = exponent / jnp.sum(exponent, axis=-1, keepdims=True)
     router[...] = probs
     msg[:, :width] = h2
-    msg[:, width:] = probs.astype(BF)
-
-
-def onehot_kernel(peers, shares, idx, ids, grads, *outs):
-    gt = outs[0]
-    slots = outs[1:]
-    length = ids.shape[0]
-    lane = lax.broadcasted_iota(jnp.int32, (length, LANES), 1)
-    expert = jnp.bitwise_xor(idx[0], lane) * shares + idx[1]
     ids_v = ids[...]
-    member = jnp.zeros((length, LANES), F32)
+    member = jnp.zeros(probs.shape, F32)
     for k in range(ids_v.shape[1]):
-        hit = (ids_v[:, k : k + 1] == expert) & (lane < peers)
-        member = member + jnp.where(hit, 1.0, 0.0)
-    r = lax.broadcasted_iota(jnp.int32, (length, length), 0)
-    c = lax.broadcasted_iota(jnp.int32, (length, length), 1)
-    lower = jnp.where(r > c, 1.0, 0.0).astype(BF)
-    rank = jnp.dot(lower, member.astype(BF), preferred_element_type=F32)
-    place = jnp.where(member > 0.0, rank, -1.0)
-    slot = lane.astype(F32)
-    for m in range(peers):
-        hot = jnp.where(place[:, m : m + 1] == slot, 1.0, 0.0).astype(BF)
-        gt[:, m * CAP : (m + 1) * CAP] = hot
-        slots[m][...] = mm(hot, grads[...], 0, 0).astype(BF)
-
-
-def dispatch_kernel(peers, gt, rows, *slots):
-    for m in range(peers):
-        slots[m][...] = mm(gt[:, m * CAP : (m + 1) * CAP], rows[...], 0, 0).astype(BF)
+        member = member + jnp.where(ids_v[:, k : k + 1] + experts == lane, 1.0, 0.0)
+    msg[:, width:] = (probs + member).astype(BF)
 
 
 def gate_column(router_cols, expert):
@@ -216,29 +209,57 @@
                 outs[k][e] = ins[m][s, k * 128 : (k + 1) * 128, :].astype(F32)
 
 
-def expert_main_kernel(peers, shares, step, *refs):
-    (idx,), rows_in, grads_in, pieces, rg_out, (hid, gpu), scratch = split_refs(
-        refs, 1, peers, peers, peers, peers, 2, 5
-    )
-    rows, grads, wgu, down, back = scratch
+def expert_main_kernel(peers, shares, experts, *refs):
+    (idx,), rows_in, grads_in, pieces, back, outs, (wgu, down) = split_refs(
+        refs, 1, shares, shares, peers, shares, 7, 2
+    )
+    rows_out, scaled_out, hid, gpu, hot_out, gate_out, near_out = outs
     ff = shares * 128
-    width = grads.shape[1]
-    for m in range(peers):
-        rows[m * CAP : (m + 1) * CAP, :] = rows_in[m][...]
-        grads[m * CAP : (m + 1) * CAP, :] = grads_in[m][...]
+    width = grads_in[0].shape[1]
+    span = rows_in[0].shape[0] // peers
+    block = shares * span
     for m, piece in enumerate(pieces):
         at = pl.ds(pl.multiple_of(jnp.bitwise_xor(idx[0], m) * 128, 128), 128)
         for t in range(shares):
             wgu[at, t * 128 : (t + 1) * 128] = piece[t, 0:128, :]
             wgu[at, ff + t * 128 : ff + (t + 1) * 128] = piece[t, 128:256, :]
     load_down(idx[0], pieces, down, shares)
+    for s in range(shares):
+        near_out[s * span : (s + 1) * span, :] = rows_in[s][0:span, :width]
     expert = idx[0] * shares + idx[1]
-
-    def body(c, carry):
-        at = pl.ds(pl.multiple_of(c * step, step), step)
-        gate = gate_column(rows[at, width:], expert)
-        pre = jnp.dot(rows[at, :width], wgu[...], preferred_element_type=F32)
-        raw = mm(grads[at, :], down[...], 1, 1)
+    r = lax.broadcasted_iota(jnp.int32, (block, block), 0)
+    c = lax.broadcasted_iota(jnp.int32, (block, block), 1)
+    lower = jnp.where(r > c, 1.0, 0.0).astype(BF)
+    slot = lax.broadcasted_iota(jnp.int32, (block, CAP), 1)
+    lane = lax.broadcasted_iota(jnp.int32, (2 * CAP, LANES), 1)
+
+    def body(step, carry):
+        slots, grads = [], []
+        for half in range(2):
+            k = step * 2 + half
+            at = pl.ds(pl.multiple_of(k * span, span), span)
+            tokens = jnp.concatenate([ref[at, :] for ref in rows_in], 0)
+            cotangents = jnp.concatenate([ref[at, :] for ref in grads_in], 0)
+            tail = tokens[:, width:].astype(F32)
+            member = jnp.where(slot == expert + experts, tail, 0.0)
+            rank = jnp.dot(lower, member.astype(BF), preferred_element_type=F32)
+            rank = jnp.sum(jnp.where(slot == expert + experts, rank, 0.0), -1, keepdims=True)
+            is_member = jnp.sum(member, axis=-1, keepdims=True) > 0.0
+            place = jnp.where(is_member, rank, -1.0)
+            hot = jnp.where(place == slot.astype(F32), 1.0, 0.0).astype(BF)
+            hot_out[pl.ds(pl.multiple_of(k * block, block), block), :] = hot
+            slots.append(mm(hot, tokens, 0, 0).astype(BF))
+            grads.append(mm(hot, cotangents, 0, 0).astype(BF))
+        rows = jnp.concatenate(slots, 0)
+        grad_rows = jnp.concatenate(grads, 0)
+        at = pl.ds(pl.multiple_of(step * 2 * CAP, 2 * CAP), 2 * CAP)
+        gate = gate_column(rows[:, width:], expert)
+        rows = rows[:, :width]
+        rows_out[at, :] = rows
+        scaled_out[at, :] = (grad_rows.astype(F32) * gate).astype(BF)
+        gate_out[at, :] = jnp.broadcast_to(gate, (2 * CAP, LANES))
+        pre = jnp.dot(rows, wgu[...], preferred_element_type=F32)
+        raw = mm(grad_rows, down[...], 1, 1)
         gate_pre = pre[:, :ff]
         up_pre = pre[:, ff:]
         sig = jax.nn.sigmoid(gate_pre)
@@ -251,34 +272,45 @@
         up = (hidden_grad * silu).astype(BF)
         both = jnp.concatenate([gp, up], 1)
         gpu[at, :] = both
-        back[at, :width] = mm(both, wgu[...], 1, 1).astype(BF)
-        lane = lax.broadcasted_iota(jnp.int32, (step, LANES), 1)
-        back[at, width:] = jnp.where(lane == expert, gate_grad, 0.0).astype(BF)
+        row_grad = mm(both, wgu[...], 1, 1).astype(BF)
+        tail_grad = jnp.where(lane == expert, gate_grad, 0.0).astype(BF)
+        for half in range(2):
+            k = step * 2 + half
+            hot = hot_out[pl.ds(pl.multiple_of(k * block, block), block), :]
+            cut = slice(half * CAP, (half + 1) * CAP)
+            to = pl.ds(pl.multiple_of(k * span, span), span)
+            spread = jnp.dot(hot, row_grad[cut, :], preferred_element_type=F32).astype(BF)
+            tail = jnp.dot(hot, tail_grad[cut, :], preferred_element_type=F32).astype(BF)
+            for s in range(shares):
+                back[s][to, :width] = spread[s * span : (s + 1) * span, :]
+                back[s][to, width:] = tail[s * span : (s + 1) * span, :]
         return carry
 
-    lax.fori_loop(0, peers * CAP // step, body, 0)
-    for m in range(peers):
-        rg_out[m][...] = back[m * CAP : (m + 1) * CAP, :]
+    lax.fori_loop(0, peers // 2, body, 0)
 
 
 def expert_rest_kernel(peers, shares, step, *refs):
-    (idx,), rows_in, grads_in, pieces, (hid, gpu), y_out, grad_out, scratch = split_refs(
-        refs, 1, peers, peers, peers, 2, peers, shares, 3
-    )
-    rows, scaled, down = scratch
+    (idx,), pieces, ins, y_out, grad_out, (down,) = split_refs(
+        refs, 1, peers, 6, shares, shares, 1
+    )
+    rows, scaled, hid, gpu, hot_in, gate_in = ins
     width = rows.shape[1]
-    expert = idx[0] * shares + idx[1]
+    span = y_out[0].shape[0] // peers
+    block = shares * span
     load_down(idx[0], pieces, down, shares)
-    for m in range(peers):
-        part = slice(m * CAP, (m + 1) * CAP)
-        gate = gate_column(rows_in[m][:, width:], expert)
-        rows[part, :] = rows_in[m][:, :width]
-        scaled[part, :] = (grads_in[m][...].astype(F32) * gate).astype(BF)
-
-    for m in range(peers):
-        gate = gate_column(rows_in[m][:, width:], expert)
-        out = jnp.dot(hid[m * CAP : (m + 1) * CAP, :], down[...], preferred_element_type=F32)
-        y_out[m][...] = (out * gate).astype(BF)
+
+    def out_rows(k, carry):
+        at = pl.ds(pl.multiple_of(k * CAP, CAP), CAP)
+        out = jnp.dot(hid[at, :], down[...], preferred_element_type=F32)
+        out = (out * gate_in[at, 0:1]).astype(BF)
+        hot = hot_in[pl.ds(pl.multiple_of(k * block, block), block), :]
+        spread = jnp.dot(hot, out, preferred_element_type=F32).astype(BF)
+        to = pl.ds(pl.multiple_of(k * span, span), span)
+        for s in range(shares):
+            y_out[s][to, :] = spread[s * span : (s + 1) * span, :]
+        return carry
+
+    lax.fori_loop(0, peers, out_rows, 0)
 
     def body(c, carry):
         at = pl.ds(pl.multiple_of(c * step, step), step)
@@ -297,14 +329,6 @@
     lax.fori_loop(0, width // step, body, 0)
 
 
-def combine_kernel(peers, shares, *refs):
-    (idx, gt), slots, parts, (all_slots, total) = split_refs(refs, 2, peers, shares, 2)
-    for m in range(peers):
-        all_slots[m * CAP : (m + 1) * CAP, :] = slots[m][...]
-    total[...] = jnp.dot(gt[...], all_slots[...], preferred_element_type=F32)
-    scatter_rows(total, parts, idx[1])
-
-
 def hi_lo_rows(row, count):
     hi = row.astype(BF)
     lo = (row - hi.astype(F32)).astype(BF)
@@ -313,12 +337,10 @@
     return out.astype(BF)
 
 
-def moe_back_kernel(shares, *refs):
-    backs, (router, res, gains, misc, out_grad, rgrad, msg) = split_refs(refs, shares, 7)
+def moe_back_kernel(*refs):
+    backs, (router, res, gains, misc, out_grad, rgrad, msg) = split_refs(refs, 2, 7)
     own, width = res.shape
-    total = backs[0][...].astype(F32)
-    for back in backs[1:]:
-        total = total + back[...].astype(F32)
+    total = backs[0][...].astype(F32) + backs[1][...].astype(F32)
     upstream = total[:, :width]
     prob_grad = total[:, width:]
     probs = router[...]
@@ -336,7 +358,7 @@
 
 def attn_bwd_kernel(peers, shares, dims, *refs):
     n_q, n_kv = dims
-    ins, g_out, msg2, (sums, partial) = split_refs(refs, 13, peers, shares, 2)
+    ins, g_out, msg2, (sums, partial) = split_refs(refs, 13, 2, shares, 2)
     idx, msg, wall, qkv, att, logs, cos, sin, seg_c, seg_r, hid, rows2, x = ins
     length, width = x.shape
     own = length // shares
@@ -345,7 +367,10 @@
     all_w = (n_q + 2 * n_kv) * HD
     o_at = all_w + n_q * HD
     resid = jnp.concatenate([msg[s * span : s * span + own, :width] for s in range(shares)], 0)
-    logit = jnp.concatenate([msg[s * span : s * span + own, width:] for s in range(shares)], 0)
+    starts = [jnp.bitwise_xor(idx[1], s) * span for s in range(shares)]
+    logit = jnp.concatenate(
+        [msg[pl.ds(pl.multiple_of(at, 16), own), width:] for at in starts], 0
+    )
     gain_moe = jnp.zeros((1, width), F32)
     for s in range(shares):
         extra = msg[s * span + own : (s + 1) * span, :width].astype(F32)
@@ -386,11 +411,13 @@
     place = lax.broadcasted_iota(jnp.int32, (LANES, width), 0)
     gain_hi = gain_moe.astype(BF).astype(F32)
     rows = jnp.where(place == 32, gain_hi, jnp.where(place == 33, gain_moe - gain_hi, 0.0))
-    sums[:, o_at:] = mm(rows2[:, :width], logit, 0, 0) + jnp.transpose(rows)
-    depth = g_out[0].shape[0]
-    for m in range(peers):
+    sums[:, o_at:] = mm(rows2[...], logit, 0, 0) + jnp.transpose(rows)
+    depth = width // peers
+    for k, m in enumerate(visit_order(TOKEN_BITS)):
         at = pl.multiple_of(jnp.bitwise_xor(idx[0], m) * depth, depth)
-        g_out[m][...] = sums[pl.ds(at, depth), :].astype(BF)
+        out = g_out[k // (peers // 2)]
+        k = k % (peers // 2)
+        out[k * depth : (k + 1) * depth, :] = sums[pl.ds(at, depth), :].astype(BF)
     partial[...] = mm(low, wall[:, :all_w], 1, 1)
     normed, _ = norm_parts(x[...].astype(F32))
     extra = hi_lo_rows(jnp.sum(partial[...] * normed, axis=0, keepdims=True), span - own)
@@ -413,12 +440,9 @@
     gain_out[...] = jnp.broadcast_to(gain_sum, gain_out.shape)
 
 
-def layer_out_kernel(shares, *refs):
-    parts, (res, out) = split_refs(refs, shares, 2)
-    total = res[...]
-    for part in parts:
-        total = total + part[...].astype(F32)
-    out[...] = total.astype(BF)
+def layer_out_kernel(first, second, res, out):
+    total = first[...].astype(F32) + second[...].astype(F32)
+    out[...] = (res[...] + total).astype(BF)
 
 
 def swap(values, axis):
@@ -426,6 +450,45 @@
     for m in range(1, len(values)):
         got.append(lax.ppermute(values[m], axis, [(i, i ^ m) for i in range(len(values))]))
     return got
+
+
+def permute(value, axis, bit):
+    count = lax.axis_size(axis)
+    return lax.ppermute(value, axis, [(i, i ^ bit) for i in range(count)])
+
+
+def gather_dp(value, bits):
+    for at, bit in enumerate(bits):
+        got = permute(value, "dp", bit)
+        if at == len(bits) - 1:
+            return value, got
+        value = jnp.concatenate([value, got], 0)
+
+
+def gather_all(value):
+    first = jnp.concatenate(gather_dp(value, TOKEN_BITS), 0)
+    across = permute(first, "tensor", 2)
+    beside = permute(first, "tensor", 1)
+    return first, beside, across, permute(across, "tensor", 1)
+
+
+def reduce_dp(even, odd, other=None):
+    got = permute(odd, "dp", 1)
+    even = even + got if other is None else even + other + got
+    half = even.shape[0] // 2
+    even = even[:half] + permute(even[half:], "dp", 2)
+    half = half // 2
+    return even[:half], permute(even[half:], "dp", 4)
+
+
+def reduce_all(parts):
+    half = parts[0].shape[0] // 2
+    own = permute(parts[1], "tensor", 1)
+    far = permute(parts[3], "tensor", 1)
+    far_odd = permute(parts[2][half:] + far[half:], "tensor", 2)
+    far_even = permute(parts[2][:half] + far[:half], "tensor", 2)
+    odd = parts[0][half:] + own[half:] + far_odd
+    return reduce_dp(parts[0][:half] + own[:half], odd, far_even)
 
 
 def per_device(
@@ -460,22 +523,16 @@
     idx = jnp.stack([lax.axis_index("dp"), lax.axis_index("tensor")]).astype(jnp.int32)
 
     local = w_router.shape[0]
-    pack = jnp.concatenate(
-        [
-            w_query,
-            w_key,
-            w_value,
-            w_output.T,
-            w_router,
-            gain_attn[:, None],
-            gain_moe[:, None],
-            jnp.zeros((local, LANES - experts - 2), BF),
-        ],
-        axis=1,
-    )
+    pack_a = jnp.concatenate([w_query, w_key, w_value], axis=1)
+    tail = [w_router, gain_attn[:, None], gain_moe[:, None]]
+    tail.append(jnp.zeros((local, LANES - experts - 2), BF))
+    pack_b = jnp.concatenate([w_output.T] + tail, axis=1)
     if rep > 1:
-        pack = lax.all_gather(pack, "rep", axis=0, tiled=True)
-    packs = swap([pack] * peers, "dp")
+        pack_a = lax.all_gather(pack_a, "rep", axis=0, tiled=True)
+        pack_b = lax.all_gather(pack_b, "rep", axis=0, tiled=True)
+    packs = gather_dp(pack_a, QKV_BITS) + gather_dp(pack_b, REST_BITS)
+
+    x_all = lax.all_gather(layer_input, "tensor", axis=0, tiled=True)
 
     if rep > 1:
         w_gate = lax.all_gather(w_gate, "rep", axis=1, tiled=True)
@@ -486,9 +543,10 @@
         [((peers, 384, LANES), BF)] * shares,
         smem=1,
     )(idx, w_gate, w_up, w_down)
+    weight_parts, x_all = lax.optimization_barrier((weight_parts, x_all))
     weight_parts = swap(weight_parts, "tensor")
-
-    x_all = lax.all_gather(layer_input, "tensor", axis=0, tiled=True)
+    grads_in = gather_all(out_grad)
+
     segment = seq_ids[0]
     before = jnp.sum((segment[None, :] < segment[:, None]).astype(jnp.int32), axis=1)
     position = (jnp.arange(length, dtype=jnp.int32) - before).astype(F32)
@@ -500,15 +558,6 @@
     sine = jnp.where(lane[None, :] < half, -1.0, 1.0) * jnp.sin(angles)
     seg_c = segment[:, None]
     seg_r = segment[None, :]
-
-    grads_all = lax.all_gather(out_grad, "tensor", axis=0, tiled=True)
-    gt, *grad_slots = call(
-        functools.partial(onehot_kernel, peers, shares),
-        [((length, slots), BF)] + [((CAP, width), BF)] * peers,
-        smem=1,
-    )(idx, expert_ids, grads_all)
-    x_all, grad_slots = lax.optimization_barrier((x_all, grad_slots))
-    grad_in = swap(grad_slots, "dp")
 
     *parts, wall, gains, qkv, att, logs, hid = call(
         functools.partial(attn_fwd_kernel, peers, shares, dims),
@@ -526,6 +575,7 @@
     )(idx, x_all, *packs, cosine, sine, seg_c, seg_r)
 
     misc = wall[:, all_w + q_w :]
+    ids_own = lax.dynamic_slice_in_dim(expert_ids, lax.axis_index("tensor") * own, own, 0)
     parts = swap(parts, "tensor")
     weight_parts = call(
         functools.partial(regroup_kernel, peers, shares), [((shares, 384, LANES), BF)] * peers
@@ -534,63 +584,54 @@
     res, router, msg = call(
         functools.partial(post_attn_kernel, experts, shares),
         [((own, width), F32), ((own, LANES), F32), ((own, wide), BF)],
-    )(*parts, layer_input, gains, misc)
-    rows_all = lax.all_gather(msg, "tensor", axis=0, tiled=True)
-    row_slots = call(
-        functools.partial(dispatch_kernel, peers), [((CAP, wide), BF)] * peers
-    )(gt, rows_all)
-    rows_in = swap(row_slots, "dp")
+    )(*parts, layer_input, ids_own, gains, misc)
+    rows_in = gather_all(msg)
 
     ff = w_gate.shape[2] * shares
-    *row_back, hidden, gate_up = call(
-        functools.partial(expert_main_kernel, peers, shares, 256),
-        [((CAP, wide), BF)] * peers + [((slots, ff), BF), ((slots, 2 * ff), BF)],
-        scratch=[
-            ((slots, wide), BF),
+    outs = call(
+        functools.partial(expert_main_kernel, peers, shares, experts),
+        [((peers * own, wide), BF)] * shares
+        + [
             ((slots, width), BF),
-            ((width, 2 * ff), BF),
-            ((ff, width), BF),
-            ((slots, wide), BF),
+            ((slots, width), BF),
+            ((slots, ff), BF),
+            ((slots, 2 * ff), BF),
+            ((peers * length, CAP), BF),
+            ((slots, LANES), F32),
+            ((length, width), BF),
         ],
+        scratch=[((width, 2 * ff), BF), ((ff, width), BF)],
         smem=1,
-    )(idx, *rows_in, *grad_in, *pieces)
-    back_in = swap(row_back, "dp")
+    )(idx, *rows_in, *grads_in, *pieces)
+    row_back, saved, rows_near = outs[:shares], outs[shares:-1], outs[-1]
+    back = reduce_all(row_back)
     rest = call(
         functools.partial(expert_rest_kernel, peers, shares, 256),
-        [((CAP, width), BF)] * peers + [((peers, 384, LANES), BF)] * shares,
-        scratch=[((slots, width), BF), ((slots, width), BF), ((ff, width), BF)],
+        [((peers * own, width), BF)] * shares + [((peers, 384, LANES), BF)] * shares,
+        scratch=[((ff, width), BF)],
         smem=1,
-    )(idx, *rows_in, *grad_in, *pieces, hidden, gate_up)
-
-    y_slots, grad_parts = rest[:peers], rest[peers:]
+    )(idx, *pieces, *saved)
+    y_parts, grad_parts = rest[:shares], rest[shares:]
     grad_parts = swap(grad_parts, "tensor")
-    back_in, y_slots = lax.optimization_barrier((back_in, y_slots))
-    y_in = swap(y_slots, "dp")
-    row_grad = call(
-        functools.partial(combine_kernel, peers, shares),
-        [((own, wide), BF)] * shares,
-        scratch=[((slots, wide), BF), ((length, wide), F32)],
-        smem=1,
-    )(idx, gt, *back_in)
-    row_grad = swap(row_grad, "tensor")
+    mixed = reduce_all(y_parts)
     grad_parts = call(
         functools.partial(regroup_kernel, peers, shares), [((shares, 384, LANES), BF)] * peers
     )(*grad_parts)
     grad_parts = swap(grad_parts, "dp")
     rgrad, msg = call(
-        functools.partial(moe_back_kernel, shares), [((own, width), F32), ((own + 16, wide), BF)]
-    )(*row_grad, router, res, gains, misc, out_grad)
+        moe_back_kernel, [((own, width), F32), ((own + 16, wide), BF)]
+    )(*back, router, res, gains, misc, out_grad)
     msg_all = lax.all_gather(msg, "tensor", axis=0, tiled=True)
 
     outs = call(
         functools.partial(attn_bwd_kernel, peers, shares, dims),
-        [((depth, pack_w), BF)] * peers + [((own + 16, width), BF)] * shares,
+        [((width // 2, pack_w), BF)] * 2 + [((own + 16, width), BF)] * shares,
         scratch=[((width, pack_w), F32), ((length, width), F32)],
         smem=1,
-    )(idx, msg_all, wall, qkv, att, logs, cosine, sine, seg_c, seg_r, hid, rows_all, x_all)
-    w_grads, msg2 = outs[:peers], outs[peers:]
-    w_sums = swap(w_grads, "dp")
-    total = sum(piece.astype(F32) for piece in w_sums)
+    )(idx, msg_all, wall, qkv, att, logs, cosine, sine, seg_c, seg_r, hid, rows_near, x_all)
+    msg2 = outs[2:]
+    w_sums = reduce_dp(outs[0], outs[1])
+    total = w_sums[0].astype(F32) + w_sums[1].astype(F32)
     if rep > 1:
         total = lax.psum_scatter(total, "rep", scatter_dimension=0, tiled=True)
 
@@ -604,16 +645,7 @@
     if rep > 1:
         gain_attn_grad = lax.psum_scatter(gain_attn_grad, "rep", scatter_dimension=0, tiled=True)
 
-    mixed = call(
-        functools.partial(combine_kernel, peers, shares),
-        [((own, width), BF)] * shares,
-        scratch=[((slots, width), BF), ((length, width), F32)],
-        smem=1,
-    )(idx, gt, *y_in)
-    mixed = swap(mixed, "tensor")
-    (layer_output,) = call(
-        functools.partial(layer_out_kernel, shares), [((own, width), BF)]
-    )(*mixed, res)
+    (layer_output,) = call(layer_out_kernel, [((own, width), BF)])(*mixed, res)
 
     gate_grad, up_grad, down_grad = call(
         functools.partial(weight_grad_kernel, peers, shares),

time: 534 us -> 456 us (0.85)
  the two profiles are of different devices: /device:TPU:8 before, /device:TPU:0 now
where the time goes in v1:
time: 456 us; the launch traced here: 455 us
  waiting for transfers between devices  242 us (53%)
  starting transfers between devices  80.1 us (18%)
  Pallas kernels  74.1 us (16%)
  local copies, waits for them, and re-layouts  28 us (6%)
  blocking collectives  16.9 us (4%)
  other arithmetic  13.5 us (3%)
    ppermute x26, waiting for transfers between devices, swap(): lax.ppermute(values[m], axis, [(i, i ^ m) for i in range(len(values))])  128 us
    ppermute x35, waiting for transfers between devices, permute(): return lax.ppermute(value, axis, [(i, i ^ bit) for i in range(count)])  112 us
    pallas_call x12, Pallas kernels, run(): pl.pallas_call(kernel, out_shape=[jax.ShapeDtypeStruct(s, d) for s, d in...  74.1 us
    ppermute x35, starting transfers between devices, permute(): return lax.ppermute(value, axis, [(i, i ^ bit) for i in range(count)])  47 us
    ppermute x26, starting transfers between devices, swap(): lax.ppermute(values[m], axis, [(i, i ^ m) for i in range(len(values))])  28.7 us
    unnamed x93, local copies, waits for them, and re-layouts  17 us
    all_gather x1, blocking collectives, per_device(): msg_all = lax.all_gather(msg, 'tensor', axis=0, tiled=True)  9.26 us
  transfers between devices with their start and end apart: 62, of which 29 were waited for; matrix products, arithmetic and copies ran while one was open for 6% of the time, Pallas kernels for 10%

profile of v1, /device:TPU:0, one launch (start us, length us, event | category | flops | bytes accessed | tf_op | source)
XLA Modules:
  0.0 455.5 jit_solution(1598449954303941849)
XLA Ops:
  13.2 5.1 %collective-permute-done.10 = bf16[128,512]{1,0:T(8,128)(2,1)S(1)} collective-permute-done((bf16[128,512]{1,0:T(8,128)(2,1)S(1)}, bf16[128,512]{1,0:T(8,128)(2,1)S(1)}, u32[]{:S(2)}, u32[]{:S(2)}) %collective-permute-start.10) | collective-permute-done | bytes 131104 | tf_op jit(solution)/shard_map/ppermute | solution.py:457
  19.1 3.4 collective-permute-start.14
  22.6 7.6 %all_gather.6.refs_1_.refs_12_ = bf16[256,1024]{1,0:T(8,128)(2,1)} all-gather(bf16[64,1024]{1,0:T(8,128)(2,1)S(1)} %copy-done.13), channel_id=1, replica_groups=mesh['dp'=8,'tensor'=4] {'tensor'}, dimensions={0}, use_global_device_ids=true | all-gather | bytes 655360 | tf_op jit(solution)/shard_map/all_gather | solution.py:535
  34.7 3.7 shard_map.229
  45.3 5.3 %shard_map.231 = (bf16[64,1024]{1,0:T(8,128)(2,1)}, bf16[64,1024]{1,0:T(8,128)(2,1)}, bf16[64,1024]{1,0:T(8,128)(2,1)}, bf16[64,1024]{1,0:T(8,128)(2,1)}, bf16[1...) custom-call(s32[2]{0:T(128)} %pad_add_fusion.idx.refs_0_, ...), custom_call_target="tpu_custom_call" | custom-call | tf_op jit(solution)/shard_map/pallas_call | solution.py:36
  65.2 7.6 %collective-permute-done.19 = bf16[64,1152]{1,0:T(8,128)(2,1)S(1)} collective-permute-done((bf16[64,1152]{1,0:T(8,128)(2,1)}, bf16[64,1152]{1,0:T(8,128)(2,1)S(1)}, u32[]{:S(2)}, u32[]{:S(2)}) %collective-permute-start.19) | collective-permute-done | bytes 147488 | tf_op jit(solution)/shard_map/ppermute | solution.py:457
  77.0 5.7 %collective-permute-done.20 = bf16[128,1152]{1,0:T(8,128)(2,1)S(1)} collective-permute-done((bf16[128,1152]{1,0:T(8,128)(2,1)S(1)}, bf16[128,1152]{1,0:T(8,128)(2,1)S(1)}, u32[]{:S(2)}, u32[]{:S(2)}) %collective-permute-start.20) | collective-permute-done | bytes 294944 | tf_op jit(solution)/shard_map/ppermute | solution.py:457
  85.4 17.9 %collective-permute-done.21 = bf16[256,1152]{1,0:T(8,128)(2,1)S(1)} collective-permute-done((bf16[256,1152]{1,0:T(8,128)(2,1)S(1)}, bf16[256,1152]{1,0:T(8,128)(2,1)S(1)}, u32[]{:S(2)}, u32[]{:S(2)}) %collective-permute-start.21) | collective-permute-done | bytes 589856 | tf_op jit(solution)/shard_map/ppermute | solution.py:457
  111.2 3.5 shard_map.230
  118.2 8.6 %collective-permute-done.3.refs_10_.refs_2_ = bf16[4,384,128]{2,1,0:T(8,128)(2,1)S(1)} collective-permute-done((bf16[4,384,128]{2,1,0:T(8,128)(2,1)}, bf16[4,384,128]{2,1,0:T(8,128)(2,1)S(1)}, u32[]{:S(2)}, u32[]{:S(2)}) %collective-permute-start.3) | collective-permute-done | bytes 393248 | tf_op jit(solution)/shard_map/ppermute | solution.py:451
  130.4 13.3 %collective-permute-done.5.refs_12_.refs_4_ = bf16[4,384,128]{2,1,0:T(8,128)(2,1)S(1)} collective-permute-done((bf16[4,384,128]{2,1,0:T(8,128)(2,1)}, bf16[4,384,128]{2,1,0:T(8,128)(2,1)S(1)}, u32[]{:S(2)}, u32[]{:S(2)}) %collective-permute-start.5) | collective-permute-done | bytes 393248 | tf_op jit(solution)/shard_map/ppermute | solution.py:451
  144.2 12.6 %collective-permute-done.6.refs_13_.refs_5_ = bf16[4,384,128]{2,1,0:T(8,128)(2,1)S(1)} collective-permute-done((bf16[4,384,128]{2,1,0:T(8,128)(2,1)}, bf16[4,384,128]{2,1,0:T(8,128)(2,1)S(1)}, u32[]{:S(2)}, u32[]{:S(2)}) %collective-permute-start.6) | collective-permute-done | bytes 393248 | tf_op jit(solution)/shard_map/ppermute | solution.py:451
  158.7 5.7 %collective-permute-done.7.refs_14_.refs_6_ = bf16[4,384,128]{2,1,0:T(8,128)(2,1)S(1)} collective-permute-done((bf16[4,384,128]{2,1,0:T(8,128)(2,1)}, bf16[4,384,128]{2,1,0:T(8,128)(2,1)S(1)}, u32[]{:S(2)}, u32[]{:S(2)}) %collective-permute-start.7) | collective-permute-done | bytes 393248 | tf_op jit(solution)/shard_map/ppermute | solution.py:451
  165.9 11.0 %collective-permute-done.8.refs_15_.refs_7_ = bf16[4,384,128]{2,1,0:T(8,128)(2,1)S(1)} collective-permute-done((bf16[4,384,128]{2,1,0:T(8,128)(2,1)}, bf16[4,384,128]{2,1,0:T(8,128)(2,1)S(1)}, u32[]{:S(2)}, u32[]{:S(2)}) %collective-permute-start.8) | collective-permute-done | bytes 393248 | tf_op jit(solution)/shard_map/ppermute | solution.py:451
  179.2 10.1 %collective-permute-done.9.refs_16_.refs_8_ = bf16[4,384,128]{2,1,0:T(8,128)(2,1)S(1)} collective-permute-done((bf16[4,384,128]{2,1,0:T(8,128)(2,1)}, bf16[4,384,128]{2,1,0:T(8,128)(2,1)S(1)}, u32[]{:S(2)}, u32[]{:S(2)}) %collective-permute-start.9) | collective-permute-done | bytes 393248 | tf_op jit(solution)/shard_map/ppermute | solution.py:451
  190.0 22.5 %shard_map.233 = (bf16[512,1152]{1,0:T(8,128)(2,1)}, bf16[512,1152]{1,0:T(8,128)(2,1)}, bf16[512,1152]{1,0:T(8,128)(2,1)}, bf16[512,1152]{1,0:T(8,128)(2,1)}, bf...) custom-call(s32[2]{0:T(128)} %pad_add_fusion.idx.refs_0_, ...), custom_call_target="tpu_custom_call" | custom-call | tf_op jit(solution)/shard_map/pallas_call | solution.py:36
  219.2 14.2 %collective-permute-done.41 = bf16[256,1152]{1,0:T(8,128)(2,1)S(1)} collective-permute-done((bf16[256,1152]{1,0:T(8,128)(2,1)S(1)}, bf16[256,1152]{1,0:T(8,128)(2,1)S(1)}, u32[]{:S(2)}, u32[]{:S(2)}) %collective-permute-start.41) | collective-permute-done | bytes 589856 | tf_op jit(solution)/shard_map/ppermute | solution.py:457
  235.8 14.9 %shard_map.234 = (bf16[512,1024]{1,0:T(8,128)(2,1)}, bf16[512,1024]{1,0:T(8,128)(2,1)}, bf16[512,1024]{1,0:T(8,128)(2,1)}, bf16[512,1024]{1,0:T(8,128)(2,1)}, bf...) custom-call(s32[2]{0:T(128)} %pad_add_fusion.idx.refs_0_, ...), custom_call_target="tpu_custom_call" | custom-call | tf_op jit(solution)/shard_map/pallas_call | solution.py:36
  252.2 10.3 %collective-permute-start.43 = (bf16[128,1152]{1,0:T(8,128)(2,1)S(1)}, bf16[128,1152]{1,0:T(8,128)(2,1)S(1)}, u32[]{:S(2)}, u32[]{:S(2)}) collective-permute-start(bf16[128,1152]{1,0:T(8,128)(2,1)S(1)} %slice.161), channel_id=1, source_target_pairs={{0,8},{4,12},{8,0},{12,4},{16,24},{20,28},{24,16},{28,20},{1,9},{5... | collective-permute-start | bytes 884744 | tf_op jit(solution)/shard_map/ppermute | solution.py:457
  266.0 4.1 collective-permute-done.43
  273.9 15.3 %collective-permute-done.34 = bf16[256,1024]{1,0:T(8,128)(2,1)S(1)} collective-permute-done((bf16[256,1024]{1,0:T(8,128)(2,1)S(1)}, bf16[256,1024]{1,0:T(8,128)(2,1)S(1)}, u32[]{:S(2)}, u32[]{:S(2)}) %collective-permute-start.34) | collective-permute-done | bytes 524320 | tf_op jit(solution)/shard_map/ppermute | solution.py:457
  294.5 9.3 %all_gather.7.refs_1_ = bf16[320,1152]{1,0:T(8,128)(2,1)} all-gather(bf16[80,1152]{1,0:T(8,128)(2,1)} %get-tuple-element.122), channel_id=1, replica_groups=mesh['dp'=8,'tensor'=4] {'tensor'}, dimensions={0}, use_global_device_ids=true | all-gather | bytes 921600 | tf_op jit(solution)/shard_map/all_gather | solution.py:624
  303.7 6.9 %shard_map.237 = (bf16[512,896]{1,0:T(8,128)(2,1)}, bf16[512,896]{1,0:T(8,128)(2,1)}, bf16[80,1024]{1,0:T(8,128)(2,1)}, bf16[80,1024]{1,0:T(8,128)(2,1)}, bf16[8...) custom-call(s32[2]{0:T(128)} %pad_add_fusion.idx.refs_0_, bf16[320,1152]{1,0:T(8,128)(2,1)} %all_gather.7.refs_1_, ...), custom_call_target="tpu_custom_call" | custom-call | tf_op jit(solution)/shard_map/pallas_call | solution.py:36
  315.5 16.3 %collective-permute-done.52.refs_2_ = bf16[8,384,128]{2,1,0:T(8,128)(2,1)S(1)} collective-permute-done((bf16[8,384,128]{2,1,0:T(8,128)(2,1)}, bf16[8,384,128]{2,1,0:T(8,128)(2,1)S(1)}, u32[]{:S(2)}, u32[]{:S(2)}) %collective-permute-start.52) | collective-permute-done | bytes 786464 | tf_op jit(solution)/shard_map/ppermute | solution.py:451
  331.8 15.1 %collective-permute-done.53.refs_3_ = bf16[8,384,128]{2,1,0:T(8,128)(2,1)S(1)} collective-permute-done((bf16[8,384,128]{2,1,0:T(8,128)(2,1)}, bf16[8,384,128]{2,1,0:T(8,128)(2,1)S(1)}, u32[]{:S(2)}, u32[]{:S(2)}) %collective-permute-start.53) | collective-permute-done | bytes 786464 | tf_op jit(solution)/shard_map/ppermute | solution.py:451
  347.8 3.6 shard_map.239
  371.5 18.7 %collective-permute-done.49 = bf16[256,896]{1,0:T(8,128)(2,1)S(1)} collective-permute-done((bf16[256,896]{1,0:T(8,128)(2,1)S(1)}, bf16[256,896]{1,0:T(8,128)(2,1)S(1)}, u32[]{:S(2)}, u32[]{:S(2)}) %collective-permute-start.49) | collective-permute-done | bytes 458784 | tf_op jit(solution)/shard_map/ppermute | solution.py:457
  392.4 5.6 %collective-permute-done.56.refs_3_ = bf16[4,384,128]{2,1,0:T(8,128)(2,1)S(1)} collective-permute-done((bf16[4,384,128]{2,1,0:T(8,128)(2,1)}, bf16[4,384,128]{2,1,0:T(8,128)(2,1)S(1)}, u32[]{:S(2)}, u32[]{:S(2)}) %collective-permute-start.56) | collective-permute-done | bytes 393248 | tf_op jit(solution)/shard_map/ppermute | solution.py:451
  402.3 4.4 all-to-all-start
  406.6 20.2 %collective-permute-done.58.refs_5_ = bf16[4,384,128]{2,1,0:T(8,128)(2,1)S(1)} collective-permute-done((bf16[4,384,128]{2,1,0:T(8,128)(2,1)}, bf16[4,384,128]{2,1,0:T(8,128)(2,1)S(1)}, u32[]{:S(2)}, u32[]{:S(2)}) %collective-permute-start.58) | collective-permute-done | bytes 393248 | tf_op jit(solution)/shard_map/ppermute | solution.py:451
  427.6 4.9 %shard_map.240 = (f32[32,128,128]{2,1,0:T(8,128)}, f32[32,128,128]{2,1,0:T(8,128)}, f32[32,128,128]{2,1,0:T(8,128)}) custom-call(s32[2]{0:T(128)} %pad_add_fusion.idx.refs_0_, bf16[4,384,128]{2,1,0:T(8,128)(2,1)} %get-tuple-element.141.refs_0_, bf16[4,384,128]{2,1,0:T(8,128)(2,1)} %collective-permute-done.54.refs_1_, ...), custom_call_target="tpu_custom_call" | custom-call | tf_op jit(solution)/shard_map/pallas_call | solution.py:36
  432.5 13.8 %collective-permute-done.37.second = bf16[64,1024]{1,0:T(8,128)(2,1)S(1)} collective-permute-done((bf16[64,1024]{1,0:T(8,128)(2,1)S(1)}, bf16[64,1024]{1,0:T(8,128)(2,1)S(1)}, u32[]{:S(2)}, u32[]{:S(2)}) %collective-permute-start.37) | collective-permute-done | bytes 131104 | tf_op jit(solution)/shard_map/ppermute | solution.py:457
  (245 shorter events, 133.1 us)
Async XLA Ops:
  73.7 34.7 %collective-permute-start = (bf16[8,384,128]{2,1,0:T(8,128)(2,1)}, bf16[8,384,128]{2,1,0:T(8,128)(2,1)S(1)}, u32[]{:S(2)}, u32[]{:S(2)}) collective-permute-start(bf16[8,384,128]{2,1,0:T(8,128)(2,1)} %get-tuple-element.87), channel_id=1, source_target_pairs={{0,1},{1,0},{2,3},{3,2},{4,5},{5,4},{6,7},{7,6},{8,9},{9,8},{10,11... | collective-permute-start | bytes 2359304 | tf_op jit(solution)/shard_map/ppermute | solution.py:451
  73.8 34.6 %collective-permute-start.1 = (bf16[8,384,128]{2,1,0:T(8,128)(2,1)}, bf16[8,384,128]{2,1,0:T(8,128)(2,1)S(1)}, u32[]{:S(2)}, u32[]{:S(2)}) collective-permute-start(bf16[8,384,128]{2,1,0:T(8,128)(2,1)} %get-tuple-element.88), channel_id=1, source_target_pairs={{0,2},{1,3},{2,0},{3,1},{4,6},{5,7},{6,4},{7,5},{8,10},{9,11},{10,... | collective-permute-start | bytes 2359304 | tf_op jit(solution)/shard_map/ppermute | solution.py:451
  74.6 35.7 %collective-permute-start.2 = (bf16[8,384,128]{2,1,0:T(8,128)(2,1)S(1)}, bf16[8,384,128]{2,1,0:T(8,128)(2,1)S(1)}, u32[]{:S(2)}, u32[]{:S(2)}) collective-permute-start(bf16[8,384,128]{2,1,0:T(8,128)(2,1)S(1)} %copy-done.38), channel_id=1, source_target_pairs={{0,3},{1,2},{2,1},{3,0},{4,7},{5,6},{6,5},{7,4},{8,11},{9,10},{10,... | collective-permute-start | bytes 2359304 | tf_op jit(solution)/shard_map/ppermute | solution.py:451
  76.4 29.9 %collective-permute-start.27 = (bf16[256,1024]{1,0:T(8,128)(2,1)S(1)}, bf16[256,1024]{1,0:T(8,128)(2,1)S(1)}, u32[]{:S(2)}, u32[]{:S(2)}) collective-permute-start(bf16[256,1024]{1,0:T(8,128)(2,1)S(1)} %pad_maximum_fusion.2), channel_id=1, source_target_pairs={{0,4},{4,0},{8,12},{12,8},{16,20},{20,16},{24,28},{28,24},{1,5},{5... | collective-permute-start | bytes 1572872 | tf_op jit(solution)/shard_map/ppermute | solution.py:457
  104.2 39.5 %collective-permute-start.23 = (bf16[512,1152]{1,0:T(8,128)(2,1)}, bf16[512,1152]{1,0:T(8,128)(2,1)}, u32[]{:S(2)}, u32[]{:S(2)}) collective-permute-start(bf16[512,1152]{1,0:T(8,128)(2,1)} %constant_dynamic-update-slice_fusion.3.refs_1_), channel_id=1, source_target_pairs={{0,2},{1,3},{2,0},{3,1},{4,6},{5,7},{6,4},{7,5},{8,10},{9,11},{10,... | collective-permute-start | bytes 3538952 | tf_op jit(solution)/shard_map/ppermute | solution.py:457
  107.1 51.6 %collective-permute-start.29 = (bf16[512,1024]{1,0:T(8,128)(2,1)}, bf16[512,1024]{1,0:T(8,128)(2,1)}, u32[]{:S(2)}, u32[]{:S(2)}) collective-permute-start(bf16[512,1024]{1,0:T(8,128)(2,1)} %constant_dynamic-update-slice_fusion.7.refs_5_), channel_id=1, source_target_pairs={{0,2},{1,3},{2,0},{3,1},{4,6},{5,7},{6,4},{7,5},{8,10},{9,11},{10,... | collective-permute-start | bytes 3145736 | tf_op jit(solution)/shard_map/ppermute | solution.py:457
  117.2 26.5 %collective-permute-start.5 = (bf16[4,384,128]{2,1,0:T(8,128)(2,1)}, bf16[4,384,128]{2,1,0:T(8,128)(2,1)S(1)}, u32[]{:S(2)}, u32[]{:S(2)}) collective-permute-start(bf16[4,384,128]{2,1,0:T(8,128)(2,1)} %get-tuple-element.93), channel_id=1, source_target_pairs={{0,12},{4,8},{8,4},{12,0},{16,28},{20,24},{24,20},{28,16},{1,13},{... | collective-permute-start | bytes 1179656 | tf_op jit(solution)/shard_map/ppermute | solution.py:451
  126.8 30.0 %collective-permute-start.6 = (bf16[4,384,128]{2,1,0:T(8,128)(2,1)}, bf16[4,384,128]{2,1,0:T(8,128)(2,1)S(1)}, u32[]{:S(2)}, u32[]{:S(2)}) collective-permute-start(bf16[4,384,128]{2,1,0:T(8,128)(2,1)} %get-tuple-element.94), channel_id=1, source_target_pairs={{0,16},{4,20},{8,24},{12,28},{16,0},{20,4},{24,8},{28,12},{1,17},{... | collective-permute-start | bytes 1179656 | tf_op jit(solution)/shard_map/ppermute | solution.py:451
  128.7 35.7 %collective-permute-start.7 = (bf16[4,384,128]{2,1,0:T(8,128)(2,1)}, bf16[4,384,128]{2,1,0:T(8,128)(2,1)S(1)}, u32[]{:S(2)}, u32[]{:S(2)}) collective-permute-start(bf16[4,384,128]{2,1,0:T(8,128)(2,1)} %get-tuple-element.95), channel_id=1, source_target_pairs={{0,20},{4,16},{8,28},{12,24},{16,4},{20,0},{24,12},{28,8},{1,21},{... | collective-permute-start | bytes 1179656 | tf_op jit(solution)/shard_map/ppermute | solution.py:451
  143.7 45.6 %collective-permute-start.22 = (bf16[512,1152]{1,0:T(8,128)(2,1)}, bf16[512,1152]{1,0:T(8,128)(2,1)}, u32[]{:S(2)}, u32[]{:S(2)}) collective-permute-start(bf16[512,1152]{1,0:T(8,128)(2,1)} %constant_dynamic-update-slice_fusion.3.refs_1_), channel_id=1, source_target_pairs={{0,1},{1,0},{2,3},{3,2},{4,5},{5,4},{6,7},{7,6},{8,9},{9,8},{10,11... | collective-permute-start | bytes 3538952 | tf_op jit(solution)/shard_map/ppermute | solution.py:457
  143.7 45.6 %collective-permute-start.24 = (bf16[512,1152]{1,0:T(8,128)(2,1)}, bf16[512,1152]{1,0:T(8,128)(2,1)}, u32[]{:S(2)}, u32[]{:S(2)}) collective-permute-start(bf16[512,1152]{1,0:T(8,128)(2,1)} %collective-permute-done.23.refs_3_), channel_id=1, source_target_pairs={{0,1},{1,0},{2,3},{3,2},{4,5},{5,4},{6,7},{7,6},{8,9},{9,8},{10,11... | collective-permute-start | bytes 3538952 | tf_op jit(solution)/shard_map/ppermute | solution.py:457
  156.8 32.5 %collective-permute-start.28 = (bf16[512,1024]{1,0:T(8,128)(2,1)}, bf16[512,1024]{1,0:T(8,128)(2,1)}, u32[]{:S(2)}, u32[]{:S(2)}) collective-permute-start(bf16[512,1024]{1,0:T(8,128)(2,1)} %constant_dynamic-update-slice_fusion.7.refs_5_), channel_id=1, source_target_pairs={{0,1},{1,0},{2,3},{3,2},{4,5},{5,4},{6,7},{7,6},{8,9},{9,8},{10,11... | collective-permute-start | bytes 3145736 | tf_op jit(solution)/shard_map/ppermute | solution.py:457
  158.7 30.6 %collective-permute-start.30 = (bf16[512,1024]{1,0:T(8,128)(2,1)}, bf16[512,1024]{1,0:T(8,128)(2,1)}, u32[]{:S(2)}, u32[]{:S(2)}) collective-permute-start(bf16[512,1024]{1,0:T(8,128)(2,1)} %collective-permute-done.29.refs_7_), channel_id=1, source_target_pairs={{0,1},{1,0},{2,3},{3,2},{4,5},{5,4},{6,7},{7,6},{8,9},{9,8},{10,11... | collective-permute-start | bytes 3145736 | tf_op jit(solution)/shard_map/ppermute | solution.py:457
  217.9 32.9 %collective-permute-start.40 = (bf16[256,1152]{1,0:T(8,128)(2,1)S(1)}, bf16[256,1152]{1,0:T(8,128)(2,1)S(1)}, u32[]{:S(2)}, u32[]{:S(2)}) collective-permute-start(bf16[256,1152]{1,0:T(8,128)(2,1)S(1)} %get-tuple-element.200), channel_id=1, source_target_pairs={{0,2},{1,3},{2,0},{3,1},{4,6},{5,7},{6,4},{7,5},{8,10},{9,11},{10,... | collective-permute-start | bytes 1769480 | tf_op jit(solution)/shard_map/ppermute | solution.py:457
  262.5 52.5 %collective-permute-start.51 = (bf16[8,384,128]{2,1,0:T(8,128)(2,1)}, bf16[8,384,128]{2,1,0:T(8,128)(2,1)}, u32[]{:S(2)}, u32[]{:S(2)}) collective-permute-start(bf16[8,384,128]{2,1,0:T(8,128)(2,1)} %get-tuple-element.138), channel_id=1, source_target_pairs={{0,1},{1,0},{2,3},{3,2},{4,5},{5,4},{6,7},{7,6},{8,9},{9,8},{10,11... | collective-permute-start | bytes 2359304 | tf_op jit(solution)/shard_map/ppermute | solution.py:451
  263.9 47.7 %collective-permute-start.33 = (bf16[256,1024]{1,0:T(8,128)(2,1)}, bf16[256,1024]{1,0:T(8,128)(2,1)S(1)}, u32[]{:S(2)}, u32[]{:S(2)}) collective-permute-start(bf16[256,1024]{1,0:T(8,128)(2,1)} %get-tuple-element.202), channel_id=1, source_target_pairs={{0,2},{1,3},{2,0},{3,1},{4,6},{5,7},{6,4},{7,5},{8,10},{9,11},{10,... | collective-permute-start | bytes 1572872 | tf_op jit(solution)/shard_map/ppermute | solution.py:457
  265.5 23.8 %collective-permute-start.34 = (bf16[256,1024]{1,0:T(8,128)(2,1)S(1)}, bf16[256,1024]{1,0:T(8,128)(2,1)S(1)}, u32[]{:S(2)}, u32[]{:S(2)}) collective-permute-start(bf16[256,1024]{1,0:T(8,128)(2,1)S(1)} %get-tuple-element.203), channel_id=1, source_target_pairs={{0,2},{1,3},{2,0},{3,1},{4,6},{5,7},{6,4},{7,5},{8,10},{9,11},{10,... | collective-permute-start | bytes 1572872 | tf_op jit(solution)/shard_map/ppermute | solution.py:457
  270.8 20.7 %collective-permute-start.44 = (bf16[64,1152]{1,0:T(8,128)(2,1)S(1)}, bf16[64,1152]{1,0:T(8,128)(2,1)S(1)}, u32[]{:S(2)}, u32[]{:S(2)}) collective-permute-start(bf16[64,1152]{1,0:T(8,128)(2,1)S(1)} %get-tuple-element.208), channel_id=1, source_target_pairs={{0,16},{4,20},{8,24},{12,28},{16,0},{20,4},{24,8},{28,12},{1,17},{... | collective-permute-start | bytes 442376 | tf_op jit(solution)/shard_map/ppermute | solution.py:457
  290.2 22.4 %collective-permute-start.35 = (bf16[256,1024]{1,0:T(8,128)(2,1)}, bf16[256,1024]{1,0:T(8,128)(2,1)}, u32[]{:S(2)}, u32[]{:S(2)}) collective-permute-start(bf16[256,1024]{1,0:T(8,128)(2,1)} %fusion.3), channel_id=1, source_target_pairs={{0,4},{4,0},{8,12},{12,8},{16,20},{20,16},{24,28},{28,24},{1,5},{5... | collective-permute-start | bytes 1572872 | tf_op jit(solution)/shard_map/ppermute | solution.py:457
  310.6 43.3 %collective-permute-start.48 = (bf16[512,896]{1,0:T(8,128)(2,1)}, bf16[512,896]{1,0:T(8,128)(2,1)S(1)}, u32[]{:S(2)}, u32[]{:S(2)}) collective-permute-start(bf16[512,896]{1,0:T(8,128)(2,1)} %get-tuple-element.136), channel_id=1, source_target_pairs={{0,4},{4,0},{8,12},{12,8},{16,20},{20,16},{24,28},{28,24},{1,5},{5... | collective-permute-start | bytes 2752520 | tf_op jit(solution)/shard_map/ppermute | solution.py:457
  311.7 35.2 %collective-permute-start.53 = (bf16[8,384,128]{2,1,0:T(8,128)(2,1)}, bf16[8,384,128]{2,1,0:T(8,128)(2,1)S(1)}, u32[]{:S(2)}, u32[]{:S(2)}) collective-permute-start(bf16[8,384,128]{2,1,0:T(8,128)(2,1)} %get-tuple-element.140), channel_id=1, source_target_pairs={{0,3},{1,2},{2,1},{3,0},{4,7},{5,6},{6,5},{7,4},{8,11},{9,10},{10,... | collective-permute-start | bytes 2359304 | tf_op jit(solution)/shard_map/ppermute | solution.py:451
  314.0 40.7 %collective-permute-start.36 = (bf16[128,1024]{1,0:T(8,128)(2,1)S(1)}, bf16[128,1024]{1,0:T(8,128)(2,1)}, u32[]{:S(2)}, u32[]{:S(2)}) collective-permute-start(bf16[128,1024]{1,0:T(8,128)(2,1)S(1)} %slice.153), channel_id=1, source_target_pairs={{0,8},{4,12},{8,0},{12,4},{16,24},{20,28},{24,16},{28,20},{1,9},{5... | collective-permute-start | bytes 786440 | tf_op jit(solution)/shard_map/ppermute | solution.py:457
  315.0 41.3 %collective-permute-start.45 = (bf16[80,1024]{1,0:T(8,128)(2,1)}, bf16[80,1024]{1,0:T(8,128)(2,1)}, u32[]{:S(2)}, u32[]{:S(2)}) collective-permute-start(bf16[80,1024]{1,0:T(8,128)(2,1)} %get-tuple-element.129), channel_id=1, source_target_pairs={{0,1},{1,0},{2,3},{3,2},{4,5},{5,4},{6,7},{7,6},{8,9},{9,8},{10,11... | collective-permute-start | bytes 491528 | tf_op jit(solution)/shard_map/ppermute | solution.py:451
  356.3 33.9 %collective-permute-start.49 = (bf16[256,896]{1,0:T(8,128)(2,1)S(1)}, bf16[256,896]{1,0:T(8,128)(2,1)S(1)}, u32[]{:S(2)}, u32[]{:S(2)}) collective-permute-start(bf16[256,896]{1,0:T(8,128)(2,1)S(1)} %slice.165), channel_id=1, source_target_pairs={{0,8},{4,12},{8,0},{12,4},{16,24},{20,28},{24,16},{28,20},{1,9},{5... | collective-permute-start | bytes 1376264 | tf_op jit(solution)/shard_map/ppermute | solution.py:457
  361.2 36.8 %collective-permute-start.56 = (bf16[4,384,128]{2,1,0:T(8,128)(2,1)}, bf16[4,384,128]{2,1,0:T(8,128)(2,1)S(1)}, u32[]{:S(2)}, u32[]{:S(2)}) collective-permute-start(bf16[4,384,128]{2,1,0:T(8,128)(2,1)} %get-tuple-element.144), channel_id=1, source_target_pairs={{0,12},{4,8},{8,4},{12,0},{16,28},{20,24},{24,20},{28,16},{1,13},{... | collective-permute-start | bytes 1179656 | tf_op jit(solution)/shard_map/ppermute | solution.py:451
  363.7 34.6 %collective-permute-start.57 = (bf16[4,384,128]{2,1,0:T(8,128)(2,1)}, bf16[4,384,128]{2,1,0:T(8,128)(2,1)S(1)}, u32[]{:S(2)}, u32[]{:S(2)}) collective-permute-start(bf16[4,384,128]{2,1,0:T(8,128)(2,1)} %get-tuple-element.145), channel_id=1, source_target_pairs={{0,16},{4,20},{8,24},{12,28},{16,0},{20,4},{24,8},{28,12},{1,17},{... | collective-permute-start | bytes 1179656 | tf_op jit(solution)/shard_map/ppermute | solution.py:451
  368.0 58.9 %collective-permute-start.58 = (bf16[4,384,128]{2,1,0:T(8,128)(2,1)}, bf16[4,384,128]{2,1,0:T(8,128)(2,1)S(1)}, u32[]{:S(2)}, u32[]{:S(2)}) collective-permute-start(bf16[4,384,128]{2,1,0:T(8,128)(2,1)} %get-tuple-element.146), channel_id=1, source_target_pairs={{0,20},{4,16},{8,28},{12,24},{16,4},{20,0},{24,12},{28,8},{1,21},{... | collective-permute-start | bytes 1179656 | tf_op jit(solution)/shard_map/ppermute | solution.py:451
  369.6 57.3 %collective-permute-start.59 = (bf16[4,384,128]{2,1,0:T(8,128)(2,1)}, bf16[4,384,128]{2,1,0:T(8,128)(2,1)}, u32[]{:S(2)}, u32[]{:S(2)}) collective-permute-start(bf16[4,384,128]{2,1,0:T(8,128)(2,1)} %get-tuple-element.147), channel_id=1, source_target_pairs={{0,24},{4,28},{8,16},{12,20},{16,8},{20,12},{24,0},{28,4},{1,25},{... | collective-permute-start | bytes 1179656 | tf_op jit(solution)/shard_map/ppermute | solution.py:451
  390.2 36.7 %collective-permute-start.60 = (bf16[4,384,128]{2,1,0:T(8,128)(2,1)}, bf16[4,384,128]{2,1,0:T(8,128)(2,1)}, u32[]{:S(2)}, u32[]{:S(2)}) collective-permute-start(bf16[4,384,128]{2,1,0:T(8,128)(2,1)} %get-tuple-element.148), channel_id=1, source_target_pairs={{0,28},{4,24},{8,20},{12,16},{16,12},{20,8},{24,4},{28,0},{1,29},{... | collective-permute-start | bytes 1179656 | tf_op jit(solution)/shard_map/ppermute | solution.py:451
  398.0 48.4 %collective-permute-start.37 = (bf16[64,1024]{1,0:T(8,128)(2,1)S(1)}, bf16[64,1024]{1,0:T(8,128)(2,1)S(1)}, u32[]{:S(2)}, u32[]{:S(2)}) collective-permute-start(bf16[64,1024]{1,0:T(8,128)(2,1)S(1)} %get-tuple-element.210), channel_id=1, source_target_pairs={{0,16},{4,20},{8,24},{12,28},{16,0},{20,4},{24,8},{28,12},{1,17},{... | collective-permute-start | bytes 393224 | tf_op jit(solution)/shard_map/ppermute | solution.py:457
  398.4 53.6 %collective-permute-start.50 = (bf16[128,896]{1,0:T(8,128)(2,1)S(1)}, bf16[128,896]{1,0:T(8,128)(2,1)S(1)}, u32[]{:S(2)}, u32[]{:S(2)}) collective-permute-start(bf16[128,896]{1,0:T(8,128)(2,1)S(1)} %slice.167), channel_id=1, source_target_pairs={{0,16},{4,20},{8,24},{12,28},{16,0},{20,4},{24,8},{28,12},{1,17},{... | collective-permute-start | bytes 688136 | tf_op jit(solution)/shard_map/ppermute | solution.py:457
  402.3 49.2 %all-to-all-start = ((f32[8,1,128]{2,1,0:T(1,128)}), f32[8,1,128]{2,1,0:T(1,128)S(1)}, u32[]{:S(2)}, u32[]{:S(2)}) async-start(f32[8,1,128]{2,1,0:T(1,128)} %slice_bitcast_fusion.1), calls=%async_computation | async-start | bytes 8192 | tf_op jit(solution)/shard_map/all_to_all | solution.py:643
  (70 other events, 929.1 us)

commit v2 on v1

--- a/solution.py
+++ b/solution.py
@@ -97,10 +97,14 @@
 
 def attn_fwd_kernel(peers, shares, dims, *refs):
     n_q, n_kv = dims
-    (idx,), (x,), w_in, (cos, sin, seg_c, seg_r), parts, outs, (part,) = split_refs(
-        refs, 1, 1, 4, 4, shares, 6, 1
-    )
-    wall, gains, qkv, att, log_out, hid = outs
+    (idx,), x_in, w_in, (cos, sin, seg_c, seg_r), parts, outs, (part,) = split_refs(
+        refs, 1, shares, 4, 4, shares, 8, 1
+    )
+    wall, gains, qkv, att, log_out, hid, x, misc = outs
+    own = x_in[0].shape[0]
+    for s, got in enumerate(x_in):
+        at = pl.multiple_of(jnp.bitwise_xor(idx[1], s) * own, own)
+        x[pl.ds(at, own), :] = got[...]
     rows = wall.shape[0] // peers
     column = 0
     for pair, bits in ((w_in[:2], QKV_BITS), (w_in[2:], REST_BITS)):
@@ -114,6 +118,7 @@
     qk_w = (n_q + n_kv) * HD
     all_w = (n_q + 2 * n_kv) * HD
     o_at = all_w + n_q * HD
+    misc[...] = wall[:, o_at : o_at + LANES]
     misc_t = jnp.transpose(wall[:, o_at : o_at + LANES].astype(F32))
     gains[...] = misc_t[32:40, :]
     gain = misc_t[32:33, :]
@@ -532,7 +537,7 @@
         pack_b = lax.all_gather(pack_b, "rep", axis=0, tiled=True)
     packs = gather_dp(pack_a, QKV_BITS) + gather_dp(pack_b, REST_BITS)
 
-    x_all = lax.all_gather(layer_input, "tensor", axis=0, tiled=True)
+    x_in = swap([layer_input] * shares, "tensor")
 
     if rep > 1:
         w_gate = lax.all_gather(w_gate, "rep", axis=1, tiled=True)
@@ -543,7 +548,6 @@
         [((peers, 384, LANES), BF)] * shares,
         smem=1,
     )(idx, w_gate, w_up, w_down)
-    weight_parts, x_all = lax.optimization_barrier((weight_parts, x_all))
     weight_parts = swap(weight_parts, "tensor")
     grads_in = gather_all(out_grad)
 
@@ -559,7 +563,7 @@
     seg_c = segment[:, None]
     seg_r = segment[None, :]
 
-    *parts, wall, gains, qkv, att, logs, hid = call(
+    *parts, wall, gains, qkv, att, logs, hid, x_all, misc = call(
         functools.partial(attn_fwd_kernel, peers, shares, dims),
         [((own, width), BF)] * shares
         + [
@@ -569,12 +573,13 @@
             ((length, q_w), BF),
             ((length, LANES), F32),
             ((length, width), BF),
+            ((length, width), BF),
+            ((width, LANES), BF),
         ],
         scratch=[((length, width), F32)],
         smem=1,
-    )(idx, x_all, *packs, cosine, sine, seg_c, seg_r)
-
-    misc = wall[:, all_w + q_w :]
+    )(idx, *x_in, *packs, cosine, sine, seg_c, seg_r)
+
     ids_own = lax.dynamic_slice_in_dim(expert_ids, lax.axis_index("tensor") * own, own, 0)
     parts = swap(parts, "tensor")
     weight_parts = call(
@@ -613,7 +618,6 @@
     )(idx, *pieces, *saved)
     y_parts, grad_parts = rest[:shares], rest[shares:]
     grad_parts = swap(grad_parts, "tensor")
-    mixed = reduce_all(y_parts)
     grad_parts = call(
         functools.partial(regroup_kernel, peers, shares), [((shares, 384, LANES), BF)] * peers
     )(*grad_parts)
@@ -622,6 +626,8 @@
         moe_back_kernel, [((own, width), F32), ((own + 16, wide), BF)]
     )(*back, router, res, gains, misc, out_grad)
     msg_all = lax.all_gather(msg, "tensor", axis=0, tiled=True)
+    y_parts, msg_all = lax.optimization_barrier((y_parts, msg_all))
+    mixed = reduce_all(y_parts)
 
     outs = call(
         functools.partial(attn_bwd_kernel, peers, shares, dims),

time: 456 us -> 456 us (level)
  waiting for transfers between devices: 242 us -> 250 us
  blocking collectives: 16.9 us -> 9.12 us
    ppermute x26 -> x29, waiting for transfers between devices: 128 us -> 148 us  [swap(): lax.ppermute(values[m], axis, [(i, i ^ m) for i in range(len(values))])]
    ppermute x35, waiting for transfers between devices: 112 us -> 101 us  [permute(): return lax.ppermute(value, axis, [(i, i ^ bit) for i in range(count)])]
    all_gather x1 -> x0, blocking collectives: 7.63 us -> none  [per_device(): x_all = lax.all_gather(layer_input, 'tensor', axis=0, tiled=True)]
    ppermute x26 -> x29, starting transfers between devices: 28.7 us -> 27 us  [swap(): lax.ppermute(values[m], axis, [(i, i ^ m) for i in range(len(values))])]
    unnamed x93 -> x107, local copies, waits for them, and re-layouts: 17 us -> 15.4 us
  transfers between devices with their start and end apart: 62 -> 65, of which waited for: 29 -> 36; matrix products, arithmetic and copies ran while one was open for 6% -> 7% of each run, Pallas kernels for 10% -> 9%
where the time goes in v2:
time: 456 us; the launch traced here: 455 us
  waiting for transfers between devices  250 us (55%)
  starting transfers between devices  81 us (18%)
  Pallas kernels  74.2 us (16%)
  local copies, waits for them, and re-layouts  25.4 us (6%)
  other arithmetic  14.1 us (3%)
  blocking collectives  9.12 us (2%)
    ppermute x29, waiting for transfers between devices, swap(): lax.ppermute(values[m], axis, [(i, i ^ m) for i in range(len(values))])  148 us
    ppermute x35, waiting for transfers between devices, permute(): return lax.ppermute(value, axis, [(i, i ^ bit) for i in range(count)])  101 us
    pallas_call x12, Pallas kernels, run(): pl.pallas_call(kernel, out_shape=[jax.ShapeDtypeStruct(s, d) for s, d in...  74.2 us
    ppermute x35, starting transfers between devices, permute(): return lax.ppermute(value, axis, [(i, i ^ bit) for i in range(count)])  47.9 us
    ppermute x29, starting transfers between devices, swap(): lax.ppermute(values[m], axis, [(i, i ^ m) for i in range(len(values))])  27 us
    unnamed x107, local copies, waits for them, and re-layouts  15.4 us
  transfers between devices with their start and end apart: 65, of which 36 were waited for; matrix products, arithmetic and copies ran while one was open for 7% of the time, Pallas kernels for 9%

profile of v2, /device:TPU:0, one launch (start us, length us, event | category | flops | bytes accessed | tf_op | source)
XLA Modules:
  0.0 454.8 jit_solution(14977913853807473316)
XLA Ops:
  3.0 4.1 collective-permute-start.13
  17.9 8.7 %collective-permute-done.14 = bf16[256,512]{1,0:T(8,128)(2,1)S(1)} collective-permute-done((bf16[256,512]{1,0:T(8,128)(2,1)S(1)}, bf16[256,512]{1,0:T(8,128)(2,1)S(1)}, u32[]{:S(2)}, u32[]{:S(2)}) %collective-permute-start.14) | collective-permute-done | bytes 262176 | tf_op jit(solution)/shard_map/ppermute | solution.py:462
  31.6 5.6 %collective-permute-done.18.refs_8_ = bf16[512,384]{1,0:T(8,128)(2,1)S(1)} collective-permute-done((bf16[512,384]{1,0:T(8,128)(2,1)S(1)}, bf16[512,384]{1,0:T(8,128)(2,1)S(1)}, u32[]{:S(2)}, u32[]{:S(2)}) %collective-permute-start.18) | collective-permute-done | bytes 393248 | tf_op jit(solution)/shard_map/ppermute | solution.py:462
  40.3 5.4 %shard_map.231 = (bf16[64,1024]{1,0:T(8,128)(2,1)}, bf16[64,1024]{1,0:T(8,128)(2,1)}, bf16[64,1024]{1,0:T(8,128)(2,1)}, bf16[64,1024]{1,0:T(8,128)(2,1)}, bf16[1...) custom-call(s32[2]{0:T(128)} %pad_add_fusion.idx.refs_0_, ...), custom_call_target="tpu_custom_call" | custom-call | tf_op jit(solution)/shard_map/pallas_call | solution.py:36
  61.7 6.3 %collective-permute-done.22 = bf16[64,1152]{1,0:T(8,128)(2,1)S(1)} collective-permute-done((bf16[64,1152]{1,0:T(8,128)(2,1)}, bf16[64,1152]{1,0:T(8,128)(2,1)S(1)}, u32[]{:S(2)}, u32[]{:S(2)}) %collective-permute-start.22) | collective-permute-done | bytes 147488 | tf_op jit(solution)/shard_map/ppermute | solution.py:462
  69.6 3.7 shard_map.229
  81.2 21.6 %collective-permute-done.24 = bf16[256,1152]{1,0:T(8,128)(2,1)S(1)} collective-permute-done((bf16[256,1152]{1,0:T(8,128)(2,1)S(1)}, bf16[256,1152]{1,0:T(8,128)(2,1)S(1)}, u32[]{:S(2)}, u32[]{:S(2)}) %collective-permute-start.24) | collective-permute-done | bytes 589856 | tf_op jit(solution)/shard_map/ppermute | solution.py:462
  118.0 8.4 %collective-permute-done.3.refs_10_.refs_2_ = bf16[4,384,128]{2,1,0:T(8,128)(2,1)S(1)} collective-permute-done((bf16[4,384,128]{2,1,0:T(8,128)(2,1)}, bf16[4,384,128]{2,1,0:T(8,128)(2,1)S(1)}, u32[]{:S(2)}, u32[]{:S(2)}) %collective-permute-start.3) | collective-permute-done | bytes 393248 | tf_op jit(solution)/shard_map/ppermute | solution.py:456
  130.5 13.3 %collective-permute-done.5.refs_12_.refs_4_ = bf16[4,384,128]{2,1,0:T(8,128)(2,1)S(1)} collective-permute-done((bf16[4,384,128]{2,1,0:T(8,128)(2,1)}, bf16[4,384,128]{2,1,0:T(8,128)(2,1)S(1)}, u32[]{:S(2)}, u32[]{:S(2)}) %collective-permute-start.5) | collective-permute-done | bytes 393248 | tf_op jit(solution)/shard_map/ppermute | solution.py:456
  144.3 12.0 %collective-permute-done.6.refs_13_.refs_5_ = bf16[4,384,128]{2,1,0:T(8,128)(2,1)S(1)} collective-permute-done((bf16[4,384,128]{2,1,0:T(8,128)(2,1)}, bf16[4,384,128]{2,1,0:T(8,128)(2,1)S(1)}, u32[]{:S(2)}, u32[]{:S(2)}) %collective-permute-start.6) | collective-permute-done | bytes 393248 | tf_op jit(solution)/shard_map/ppermute | solution.py:456
  158.3 5.8 %collective-permute-done.7.refs_14_.refs_6_ = bf16[4,384,128]{2,1,0:T(8,128)(2,1)S(1)} collective-permute-done((bf16[4,384,128]{2,1,0:T(8,128)(2,1)}, bf16[4,384,128]{2,1,0:T(8,128)(2,1)S(1)}, u32[]{:S(2)}, u32[]{:S(2)}) %collective-permute-start.7) | collective-permute-done | bytes 393248 | tf_op jit(solution)/shard_map/ppermute | solution.py:456
  166.1 10.2 %collective-permute-done.8.refs_15_.refs_7_ = bf16[4,384,128]{2,1,0:T(8,128)(2,1)S(1)} collective-permute-done((bf16[4,384,128]{2,1,0:T(8,128)(2,1)}, bf16[4,384,128]{2,1,0:T(8,128)(2,1)S(1)}, u32[]{:S(2)}, u32[]{:S(2)}) %collective-permute-start.8) | collective-permute-done | bytes 393248 | tf_op jit(solution)/shard_map/ppermute | solution.py:456
  178.7 10.0 %collective-permute-done.9.refs_16_.refs_8_ = bf16[4,384,128]{2,1,0:T(8,128)(2,1)S(1)} collective-permute-done((bf16[4,384,128]{2,1,0:T(8,128)(2,1)}, bf16[4,384,128]{2,1,0:T(8,128)(2,1)S(1)}, u32[]{:S(2)}, u32[]{:S(2)}) %collective-permute-start.9) | collective-permute-done | bytes 393248 | tf_op jit(solution)/shard_map/ppermute | solution.py:456
  189.5 22.5 %shard_map.233 = (bf16[512,1152]{1,0:T(8,128)(2,1)}, bf16[512,1152]{1,0:T(8,128)(2,1)}, bf16[512,1152]{1,0:T(8,128)(2,1)}, bf16[512,1152]{1,0:T(8,128)(2,1)}, bf...) custom-call(s32[2]{0:T(128)} %pad_add_fusion.idx.refs_0_, ...), custom_call_target="tpu_custom_call" | custom-call | tf_op jit(solution)/shard_map/pallas_call | solution.py:36
  219.4 14.1 %collective-permute-done.37 = bf16[256,1152]{1,0:T(8,128)(2,1)S(1)} collective-permute-done((bf16[256,1152]{1,0:T(8,128)(2,1)S(1)}, bf16[256,1152]{1,0:T(8,128)(2,1)S(1)}, u32[]{:S(2)}, u32[]{:S(2)}) %collective-permute-start.37) | collective-permute-done | bytes 589856 | tf_op jit(solution)/shard_map/ppermute | solution.py:462
  234.0 11.6 %collective-permute-done.36 = bf16[256,1152]{1,0:T(8,128)(2,1)S(1)} collective-permute-done((bf16[256,1152]{1,0:T(8,128)(2,1)S(1)}, bf16[256,1152]{1,0:T(8,128)(2,1)S(1)}, u32[]{:S(2)}, u32[]{:S(2)}) %collective-permute-start.36) | collective-permute-done | bytes 589856 | tf_op jit(solution)/shard_map/ppermute | solution.py:462
  248.1 10.3 %collective-permute-start.39 = (bf16[128,1152]{1,0:T(8,128)(2,1)S(1)}, bf16[128,1152]{1,0:T(8,128)(2,1)S(1)}, u32[]{:S(2)}, u32[]{:S(2)}) collective-permute-start(bf16[128,1152]{1,0:T(8,128)(2,1)S(1)} %slice.149), channel_id=1, source_target_pairs={{0,8},{4,12},{8,0},{12,4},{16,24},{20,28},{24,16},{28,20},{1,9},{5... | collective-permute-start | bytes 884744 | tf_op jit(solution)/shard_map/ppermute | solution.py:462
  258.3 4.8 %collective-permute-done.39 = bf16[128,1152]{1,0:T(8,128)(2,1)S(1)} collective-permute-done((bf16[128,1152]{1,0:T(8,128)(2,1)S(1)}, bf16[128,1152]{1,0:T(8,128)(2,1)S(1)}, u32[]{:S(2)}, u32[]{:S(2)}) %collective-permute-start.39) | collective-permute-done | bytes 294944 | tf_op jit(solution)/shard_map/ppermute | solution.py:462
  266.5 14.9 %shard_map.234 = (bf16[512,1024]{1,0:T(8,128)(2,1)}, bf16[512,1024]{1,0:T(8,128)(2,1)}, bf16[512,1024]{1,0:T(8,128)(2,1)}, bf16[512,1024]{1,0:T(8,128)(2,1)}, bf...) custom-call(s32[2]{0:T(128)} %pad_add_fusion.idx.refs_0_, ...), custom_call_target="tpu_custom_call" | custom-call | tf_op jit(solution)/shard_map/pallas_call | solution.py:36
  284.5 9.1 %all_gather.3.refs_1_ = bf16[320,1152]{1,0:T(8,128)(2,1)} all-gather(bf16[80,1152]{1,0:T(8,128)(2,1)} %get-tuple-element.119), channel_id=1, replica_groups=mesh['dp'=8,'tensor'=4] {'tensor'}, dimensions={0}, use_global_device_ids=true | all-gather | bytes 921600 | tf_op jit(solution)/shard_map/all_gather | solution.py:628
  295.8 6.9 %shard_map.237 = (bf16[512,896]{1,0:T(8,128)(2,1)}, bf16[512,896]{1,0:T(8,128)(2,1)}, bf16[80,1024]{1,0:T(8,128)(2,1)}, bf16[80,1024]{1,0:T(8,128)(2,1)}, bf16[8...) custom-call(s32[2]{0:T(128)} %pad_add_fusion.idx.refs_0_, bf16[320,1152]{1,0:T(8,128)(2,1)} %all_gather.3.refs_1_, ...), custom_call_target="tpu_custom_call" | custom-call | tf_op jit(solution)/shard_map/pallas_call | solution.py:36
  304.8 10.0 %collective-permute-done.55.refs_2_ = bf16[8,384,128]{2,1,0:T(8,128)(2,1)} collective-permute-done((bf16[8,384,128]{2,1,0:T(8,128)(2,1)}, bf16[8,384,128]{2,1,0:T(8,128)(2,1)}, u32[]{:S(2)}, u32[]{:S(2)}) %collective-permute-start.55) | collective-permute-done | bytes 786464 | tf_op jit(solution)/shard_map/ppermute | solution.py:456
  314.8 15.6 %collective-permute-done.56.refs_3_ = bf16[8,384,128]{2,1,0:T(8,128)(2,1)} collective-permute-done((bf16[8,384,128]{2,1,0:T(8,128)(2,1)}, bf16[8,384,128]{2,1,0:T(8,128)(2,1)}, u32[]{:S(2)}, u32[]{:S(2)}) %collective-permute-start.56) | collective-permute-done | bytes 786464 | tf_op jit(solution)/shard_map/ppermute | solution.py:456
  338.6 7.4 %collective-permute-done.57.refs_1_ = bf16[4,384,128]{2,1,0:T(8,128)(2,1)S(1)} collective-permute-done((bf16[4,384,128]{2,1,0:T(8,128)(2,1)}, bf16[4,384,128]{2,1,0:T(8,128)(2,1)S(1)}, u32[]{:S(2)}, u32[]{:S(2)}) %collective-permute-start.57) | collective-permute-done | bytes 393248 | tf_op jit(solution)/shard_map/ppermute | solution.py:456
  348.2 12.2 %collective-permute-done.59.refs_3_ = bf16[4,384,128]{2,1,0:T(8,128)(2,1)S(1)} collective-permute-done((bf16[4,384,128]{2,1,0:T(8,128)(2,1)}, bf16[4,384,128]{2,1,0:T(8,128)(2,1)S(1)}, u32[]{:S(2)}, u32[]{:S(2)}) %collective-permute-start.59) | collective-permute-done | bytes 393248 | tf_op jit(solution)/shard_map/ppermute | solution.py:456
  363.8 18.4 %collective-permute-done.60.refs_4_ = bf16[4,384,128]{2,1,0:T(8,128)(2,1)S(1)} collective-permute-done((bf16[4,384,128]{2,1,0:T(8,128)(2,1)S(1)}, bf16[4,384,128]{2,1,0:T(8,128)(2,1)S(1)}, u32[]{:S(2)}, u32[]{:S(2)}) %collective-permute-start.60) | collective-permute-done | bytes 393248 | tf_op jit(solution)/shard_map/ppermute | solution.py:456
  382.2 12.2 %collective-permute-done.61.refs_5_ = bf16[4,384,128]{2,1,0:T(8,128)(2,1)S(1)} collective-permute-done((bf16[4,384,128]{2,1,0:T(8,128)(2,1)S(1)}, bf16[4,384,128]{2,1,0:T(8,128)(2,1)S(1)}, u32[]{:S(2)}, u32[]{:S(2)}) %collective-permute-start.61) | collective-permute-done | bytes 393248 | tf_op jit(solution)/shard_map/ppermute | solution.py:456
  412.5 6.0 %all-to-all-start = ((f32[8,1,128]{2,1,0:T(1,128)}), f32[8,1,128]{2,1,0:T(1,128)S(1)}, u32[]{:S(2)}, u32[]{:S(2)}) async-start(f32[8,1,128]{2,1,0:T(1,128)} %slice_bitcast_fusion.1), calls=%async_computation | async-start | bytes 8192 | tf_op jit(solution)/shard_map/all_to_all | solution.py:649
  419.3 4.9 %shard_map.240 = (f32[32,128,128]{2,1,0:T(8,128)}, f32[32,128,128]{2,1,0:T(8,128)}, f32[32,128,128]{2,1,0:T(8,128)}) custom-call(s32[2]{0:T(128)} %pad_add_fusion.idx.refs_0_, bf16[4,384,128]{2,1,0:T(8,128)(2,1)} %get-tuple-element.145.refs_0_, bf16[4,384,128]{2,1,0:T(8,128)(2,1)} %copy-done.22, bf16[4,384,128]{2,1,0:T(8,128)(2,1)} %copy-done.23, ...), custom_call_target="tpu_custom_call" | custom-call | tf_op jit(solution)/shard_map/pallas_call | solution.py:36
  426.6 4.3 collective-permute-start.53
  432.4 9.4 %collective-permute-done.53 = bf16[128,896]{1,0:T(8,128)(2,1)S(1)} collective-permute-done((bf16[128,896]{1,0:T(8,128)(2,1)S(1)}, bf16[128,896]{1,0:T(8,128)(2,1)S(1)}, u32[]{:S(2)}, u32[]{:S(2)}) %collective-permute-start.53) | collective-permute-done | bytes 229408 | tf_op jit(solution)/shard_map/ppermute | solution.py:462
  448.4 4.0 collective-permute-done.47.second
  (263 shorter events, 139.7 us)
Async XLA Ops:
  7.2 24.4 %collective-permute-start.12 = (bf16[64,1024]{1,0:T(8,128)(2,1)}, bf16[64,1024]{1,0:T(8,128)(2,1)S(1)}, u32[]{:S(2)}, u32[]{:S(2)}) collective-permute-start(bf16[64,1024]{1,0:T(8,128)(2,1)} %refs_4_.3), channel_id=1, source_target_pairs={{0,3},{1,2},{2,1},{3,0},{4,7},{5,6},{6,5},{7,4},{8,11},{9,10},{10,... | collective-permute-start | bytes 393224 | tf_op jit(solution)/shard_map/ppermute | solution.py:456
  7.9 23.7 %collective-permute-start.11 = (bf16[64,1024]{1,0:T(8,128)(2,1)}, bf16[64,1024]{1,0:T(8,128)(2,1)S(1)}, u32[]{:S(2)}, u32[]{:S(2)}) collective-permute-start(bf16[64,1024]{1,0:T(8,128)(2,1)} %refs_4_.3), channel_id=1, source_target_pairs={{0,2},{1,3},{2,0},{3,1},{4,6},{5,7},{6,4},{7,5},{8,10},{9,11},{10,... | collective-permute-start | bytes 393224 | tf_op jit(solution)/shard_map/ppermute | solution.py:456
  8.7 22.9 %collective-permute-start.10 = (bf16[64,1024]{1,0:T(8,128)(2,1)}, bf16[64,1024]{1,0:T(8,128)(2,1)S(1)}, u32[]{:S(2)}, u32[]{:S(2)}) collective-permute-start(bf16[64,1024]{1,0:T(8,128)(2,1)} %refs_4_.3), channel_id=1, source_target_pairs={{0,1},{1,0},{2,3},{3,2},{4,5},{5,4},{6,7},{7,6},{8,9},{9,8},{10,11... | collective-permute-start | bytes 393224 | tf_op jit(solution)/shard_map/ppermute | solution.py:456
  73.4 34.6 %collective-permute-start = (bf16[8,384,128]{2,1,0:T(8,128)(2,1)}, bf16[8,384,128]{2,1,0:T(8,128)(2,1)S(1)}, u32[]{:S(2)}, u32[]{:S(2)}) collective-permute-start(bf16[8,384,128]{2,1,0:T(8,128)(2,1)} %get-tuple-element.85), channel_id=1, source_target_pairs={{0,1},{1,0},{2,3},{3,2},{4,5},{5,4},{6,7},{7,6},{8,9},{9,8},{10,11... | collective-permute-start | bytes 2359304 | tf_op jit(solution)/shard_map/ppermute | solution.py:456
  73.4 34.6 %collective-permute-start.1 = (bf16[8,384,128]{2,1,0:T(8,128)(2,1)}, bf16[8,384,128]{2,1,0:T(8,128)(2,1)S(1)}, u32[]{:S(2)}, u32[]{:S(2)}) collective-permute-start(bf16[8,384,128]{2,1,0:T(8,128)(2,1)} %get-tuple-element.86), channel_id=1, source_target_pairs={{0,2},{1,3},{2,0},{3,1},{4,6},{5,7},{6,4},{7,5},{8,10},{9,11},{10,... | collective-permute-start | bytes 2359304 | tf_op jit(solution)/shard_map/ppermute | solution.py:456
  75.0 35.1 %collective-permute-start.2 = (bf16[8,384,128]{2,1,0:T(8,128)(2,1)}, bf16[8,384,128]{2,1,0:T(8,128)(2,1)S(1)}, u32[]{:S(2)}, u32[]{:S(2)}) collective-permute-start(bf16[8,384,128]{2,1,0:T(8,128)(2,1)} %get-tuple-element.87), channel_id=1, source_target_pairs={{0,3},{1,2},{2,1},{3,0},{4,7},{5,6},{6,5},{7,4},{8,11},{9,10},{10,... | collective-permute-start | bytes 2359304 | tf_op jit(solution)/shard_map/ppermute | solution.py:456
  75.9 30.7 %collective-permute-start.30 = (bf16[256,1024]{1,0:T(8,128)(2,1)S(1)}, bf16[256,1024]{1,0:T(8,128)(2,1)S(1)}, u32[]{:S(2)}, u32[]{:S(2)}) collective-permute-start(bf16[256,1024]{1,0:T(8,128)(2,1)S(1)} %pad_maximum_fusion.2), channel_id=1, source_target_pairs={{0,4},{4,0},{8,12},{12,8},{16,20},{20,16},{24,28},{28,24},{1,5},{5... | collective-permute-start | bytes 1572872 | tf_op jit(solution)/shard_map/ppermute | solution.py:462
  78.6 24.2 %collective-permute-start.24 = (bf16[256,1152]{1,0:T(8,128)(2,1)S(1)}, bf16[256,1152]{1,0:T(8,128)(2,1)S(1)}, u32[]{:S(2)}, u32[]{:S(2)}) collective-permute-start(bf16[256,1152]{1,0:T(8,128)(2,1)S(1)} %pad_maximum_fusion), channel_id=1, source_target_pairs={{0,4},{4,0},{8,12},{12,8},{16,20},{20,16},{24,28},{28,24},{1,5},{5... | collective-permute-start | bytes 1769480 | tf_op jit(solution)/shard_map/ppermute | solution.py:462
  103.7 40.1 %collective-permute-start.26 = (bf16[512,1152]{1,0:T(8,128)(2,1)}, bf16[512,1152]{1,0:T(8,128)(2,1)}, u32[]{:S(2)}, u32[]{:S(2)}) collective-permute-start(bf16[512,1152]{1,0:T(8,128)(2,1)} %constant_dynamic-update-slice_fusion.3.refs_1_), channel_id=1, source_target_pairs={{0,2},{1,3},{2,0},{3,1},{4,6},{5,7},{6,4},{7,5},{8,10},{9,11},{10,... | collective-permute-start | bytes 3538952 | tf_op jit(solution)/shard_map/ppermute | solution.py:462
  107.4 50.8 %collective-permute-start.32 = (bf16[512,1024]{1,0:T(8,128)(2,1)}, bf16[512,1024]{1,0:T(8,128)(2,1)}, u32[]{:S(2)}, u32[]{:S(2)}) collective-permute-start(bf16[512,1024]{1,0:T(8,128)(2,1)} %constant_dynamic-update-slice_fusion.7.refs_5_), channel_id=1, source_target_pairs={{0,2},{1,3},{2,0},{3,1},{4,6},{5,7},{6,4},{7,5},{8,10},{9,11},{10,... | collective-permute-start | bytes 3145736 | tf_op jit(solution)/shard_map/ppermute | solution.py:462
  117.0 26.8 %collective-permute-start.5 = (bf16[4,384,128]{2,1,0:T(8,128)(2,1)}, bf16[4,384,128]{2,1,0:T(8,128)(2,1)S(1)}, u32[]{:S(2)}, u32[]{:S(2)}) collective-permute-start(bf16[4,384,128]{2,1,0:T(8,128)(2,1)} %get-tuple-element.91), channel_id=1, source_target_pairs={{0,12},{4,8},{8,4},{12,0},{16,28},{20,24},{24,20},{28,16},{1,13},{... | collective-permute-start | bytes 1179656 | tf_op jit(solution)/shard_map/ppermute | solution.py:456
  126.4 29.9 %collective-permute-start.6 = (bf16[4,384,128]{2,1,0:T(8,128)(2,1)}, bf16[4,384,128]{2,1,0:T(8,128)(2,1)S(1)}, u32[]{:S(2)}, u32[]{:S(2)}) collective-permute-start(bf16[4,384,128]{2,1,0:T(8,128)(2,1)} %get-tuple-element.92), channel_id=1, source_target_pairs={{0,16},{4,20},{8,24},{12,28},{16,0},{20,4},{24,8},{28,12},{1,17},{... | collective-permute-start | bytes 1179656 | tf_op jit(solution)/shard_map/ppermute | solution.py:456
  128.8 35.3 %collective-permute-start.7 = (bf16[4,384,128]{2,1,0:T(8,128)(2,1)}, bf16[4,384,128]{2,1,0:T(8,128)(2,1)S(1)}, u32[]{:S(2)}, u32[]{:S(2)}) collective-permute-start(bf16[4,384,128]{2,1,0:T(8,128)(2,1)} %get-tuple-element.93), channel_id=1, source_target_pairs={{0,20},{4,16},{8,28},{12,24},{16,4},{20,0},{24,12},{28,8},{1,21},{... | collective-permute-start | bytes 1179656 | tf_op jit(solution)/shard_map/ppermute | solution.py:456
  143.8 44.9 %collective-permute-start.25 = (bf16[512,1152]{1,0:T(8,128)(2,1)}, bf16[512,1152]{1,0:T(8,128)(2,1)}, u32[]{:S(2)}, u32[]{:S(2)}) collective-permute-start(bf16[512,1152]{1,0:T(8,128)(2,1)} %constant_dynamic-update-slice_fusion.3.refs_1_), channel_id=1, source_target_pairs={{0,1},{1,0},{2,3},{3,2},{4,5},{5,4},{6,7},{7,6},{8,9},{9,8},{10,11... | collective-permute-start | bytes 3538952 | tf_op jit(solution)/shard_map/ppermute | solution.py:462
  143.8 44.9 %collective-permute-start.27 = (bf16[512,1152]{1,0:T(8,128)(2,1)}, bf16[512,1152]{1,0:T(8,128)(2,1)}, u32[]{:S(2)}, u32[]{:S(2)}) collective-permute-start(bf16[512,1152]{1,0:T(8,128)(2,1)} %collective-permute-done.26.refs_3_), channel_id=1, source_target_pairs={{0,1},{1,0},{2,3},{3,2},{4,5},{5,4},{6,7},{7,6},{8,9},{9,8},{10,11... | collective-permute-start | bytes 3538952 | tf_op jit(solution)/shard_map/ppermute | solution.py:462
  156.3 32.4 %collective-permute-start.31 = (bf16[512,1024]{1,0:T(8,128)(2,1)}, bf16[512,1024]{1,0:T(8,128)(2,1)}, u32[]{:S(2)}, u32[]{:S(2)}) collective-permute-start(bf16[512,1024]{1,0:T(8,128)(2,1)} %constant_dynamic-update-slice_fusion.7.refs_5_), channel_id=1, source_target_pairs={{0,1},{1,0},{2,3},{3,2},{4,5},{5,4},{6,7},{7,6},{8,9},{9,8},{10,11... | collective-permute-start | bytes 3145736 | tf_op jit(solution)/shard_map/ppermute | solution.py:462
  158.3 30.5 %collective-permute-start.33 = (bf16[512,1024]{1,0:T(8,128)(2,1)}, bf16[512,1024]{1,0:T(8,128)(2,1)}, u32[]{:S(2)}, u32[]{:S(2)}) collective-permute-start(bf16[512,1024]{1,0:T(8,128)(2,1)} %collective-permute-done.32.refs_7_), channel_id=1, source_target_pairs={{0,1},{1,0},{2,3},{3,2},{4,5},{5,4},{6,7},{7,6},{8,9},{9,8},{10,11... | collective-permute-start | bytes 3145736 | tf_op jit(solution)/shard_map/ppermute | solution.py:462
  219.3 26.3 %collective-permute-start.36 = (bf16[256,1152]{1,0:T(8,128)(2,1)S(1)}, bf16[256,1152]{1,0:T(8,128)(2,1)S(1)}, u32[]{:S(2)}, u32[]{:S(2)}) collective-permute-start(bf16[256,1152]{1,0:T(8,128)(2,1)S(1)} %get-tuple-element.204), channel_id=1, source_target_pairs={{0,2},{1,3},{2,0},{3,1},{4,6},{5,7},{6,4},{7,5},{8,10},{9,11},{10,... | collective-permute-start | bytes 1769480 | tf_op jit(solution)/shard_map/ppermute | solution.py:462
  293.6 42.4 %collective-permute-start.42 = (bf16[512,1024]{1,0:T(8,128)(2,1)}, bf16[512,1024]{1,0:T(8,128)(2,1)S(1)}, u32[]{:S(2)}, u32[]{:S(2)}) collective-permute-start(bf16[512,1024]{1,0:T(8,128)(2,1)} %get-tuple-element.123), channel_id=1, source_target_pairs={{0,1},{1,0},{2,3},{3,2},{4,5},{5,4},{6,7},{7,6},{8,9},{9,8},{10,11... | collective-permute-start | bytes 3145736 | tf_op jit(solution)/shard_map/ppermute | solution.py:462
  294.5 35.9 %collective-permute-start.56 = (bf16[8,384,128]{2,1,0:T(8,128)(2,1)}, bf16[8,384,128]{2,1,0:T(8,128)(2,1)}, u32[]{:S(2)}, u32[]{:S(2)}) collective-permute-start(bf16[8,384,128]{2,1,0:T(8,128)(2,1)} %get-tuple-element.144), channel_id=1, source_target_pairs={{0,3},{1,2},{2,1},{3,0},{4,7},{5,6},{6,5},{7,4},{8,11},{9,10},{10,... | collective-permute-start | bytes 2359304 | tf_op jit(solution)/shard_map/ppermute | solution.py:456
  302.7 58.6 %collective-permute-start.51 = (bf16[512,896]{1,0:T(8,128)(2,1)}, bf16[512,896]{1,0:T(8,128)(2,1)}, u32[]{:S(2)}, u32[]{:S(2)}) collective-permute-start(bf16[512,896]{1,0:T(8,128)(2,1)} %get-tuple-element.140), channel_id=1, source_target_pairs={{0,4},{4,0},{8,12},{12,8},{16,20},{20,16},{24,28},{28,24},{1,5},{5... | collective-permute-start | bytes 2752520 | tf_op jit(solution)/shard_map/ppermute | solution.py:462
  304.7 92.8 %collective-permute-start.41 = (bf16[512,1024]{1,0:T(8,128)(2,1)}, bf16[512,1024]{1,0:T(8,128)(2,1)S(1)}, u32[]{:S(2)}, u32[]{:S(2)}) collective-permute-start(bf16[512,1024]{1,0:T(8,128)(2,1)} %get-tuple-element.121), channel_id=1, source_target_pairs={{0,1},{1,0},{2,3},{3,2},{4,5},{5,4},{6,7},{7,6},{8,9},{9,8},{10,11... | collective-permute-start | bytes 3145736 | tf_op jit(solution)/shard_map/ppermute | solution.py:462
  336.1 24.4 %collective-permute-start.59 = (bf16[4,384,128]{2,1,0:T(8,128)(2,1)}, bf16[4,384,128]{2,1,0:T(8,128)(2,1)S(1)}, u32[]{:S(2)}, u32[]{:S(2)}) collective-permute-start(bf16[4,384,128]{2,1,0:T(8,128)(2,1)} %get-tuple-element.148), channel_id=1, source_target_pairs={{0,12},{4,8},{8,4},{12,0},{16,28},{20,24},{24,20},{28,16},{1,13},{... | collective-permute-start | bytes 1179656 | tf_op jit(solution)/shard_map/ppermute | solution.py:456
  346.0 51.5 %collective-permute-start.44 = (bf16[256,1024]{1,0:T(8,128)(2,1)S(1)}, bf16[256,1024]{1,0:T(8,128)(2,1)S(1)}, u32[]{:S(2)}, u32[]{:S(2)}) collective-permute-start(bf16[256,1024]{1,0:T(8,128)(2,1)S(1)} %get-tuple-element.207), channel_id=1, source_target_pairs={{0,2},{1,3},{2,0},{3,1},{4,6},{5,7},{6,4},{7,5},{8,10},{9,11},{10,... | collective-permute-start | bytes 1572872 | tf_op jit(solution)/shard_map/ppermute | solution.py:462
  348.2 34.0 %collective-permute-start.60 = (bf16[4,384,128]{2,1,0:T(8,128)(2,1)S(1)}, bf16[4,384,128]{2,1,0:T(8,128)(2,1)S(1)}, u32[]{:S(2)}, u32[]{:S(2)}) collective-permute-start(bf16[4,384,128]{2,1,0:T(8,128)(2,1)S(1)} %copy-done.43), channel_id=1, source_target_pairs={{0,16},{4,20},{8,24},{12,28},{16,0},{20,4},{24,8},{28,12},{1,17},{... | collective-permute-start | bytes 1179656 | tf_op jit(solution)/shard_map/ppermute | solution.py:456
  360.4 33.9 %collective-permute-start.61 = (bf16[4,384,128]{2,1,0:T(8,128)(2,1)S(1)}, bf16[4,384,128]{2,1,0:T(8,128)(2,1)S(1)}, u32[]{:S(2)}, u32[]{:S(2)}) collective-permute-start(bf16[4,384,128]{2,1,0:T(8,128)(2,1)S(1)} %copy-done.42), channel_id=1, source_target_pairs={{0,20},{4,16},{8,28},{12,24},{16,4},{20,0},{24,12},{28,8},{1,21},{... | collective-permute-start | bytes 1179656 | tf_op jit(solution)/shard_map/ppermute | solution.py:456
  361.4 34.4 %collective-permute-start.48 = (bf16[80,1024]{1,0:T(8,128)(2,1)S(1)}, bf16[80,1024]{1,0:T(8,128)(2,1)S(1)}, u32[]{:S(2)}, u32[]{:S(2)}) collective-permute-start(bf16[80,1024]{1,0:T(8,128)(2,1)S(1)} %copy-done.46), channel_id=1, source_target_pairs={{0,1},{1,0},{2,3},{3,2},{4,5},{5,4},{6,7},{7,6},{8,9},{9,8},{10,11... | collective-permute-start | bytes 491528 | tf_op jit(solution)/shard_map/ppermute | solution.py:456
  382.2 36.3 %collective-permute-start.62 = (bf16[4,384,128]{2,1,0:T(8,128)(2,1)}, bf16[4,384,128]{2,1,0:T(8,128)(2,1)S(1)}, u32[]{:S(2)}, u32[]{:S(2)}) collective-permute-start(bf16[4,384,128]{2,1,0:T(8,128)(2,1)} %get-tuple-element.151), channel_id=1, source_target_pairs={{0,24},{4,28},{8,16},{12,20},{16,8},{20,12},{24,0},{28,4},{1,25},{... | collective-permute-start | bytes 1179656 | tf_op jit(solution)/shard_map/ppermute | solution.py:456
  394.4 24.2 %collective-permute-start.63 = (bf16[4,384,128]{2,1,0:T(8,128)(2,1)}, bf16[4,384,128]{2,1,0:T(8,128)(2,1)}, u32[]{:S(2)}, u32[]{:S(2)}) collective-permute-start(bf16[4,384,128]{2,1,0:T(8,128)(2,1)} %get-tuple-element.152), channel_id=1, source_target_pairs={{0,28},{4,24},{8,20},{12,16},{16,12},{20,8},{24,4},{28,0},{1,29},{... | collective-permute-start | bytes 1179656 | tf_op jit(solution)/shard_map/ppermute | solution.py:456
  397.4 28.0 %collective-permute-start.52 = (bf16[256,896]{1,0:T(8,128)(2,1)}, bf16[256,896]{1,0:T(8,128)(2,1)}, u32[]{:S(2)}, u32[]{:S(2)}) collective-permute-start(bf16[256,896]{1,0:T(8,128)(2,1)} %slice.161), channel_id=1, source_target_pairs={{0,8},{4,12},{8,0},{12,4},{16,24},{20,28},{24,16},{28,20},{1,9},{5... | collective-permute-start | bytes 1376264 | tf_op jit(solution)/shard_map/ppermute | solution.py:462
  402.0 28.9 %collective-permute-start.43 = (bf16[256,1024]{1,0:T(8,128)(2,1)}, bf16[256,1024]{1,0:T(8,128)(2,1)}, u32[]{:S(2)}, u32[]{:S(2)}) collective-permute-start(bf16[256,1024]{1,0:T(8,128)(2,1)} %get-tuple-element.206), channel_id=1, source_target_pairs={{0,2},{1,3},{2,0},{3,1},{4,6},{5,7},{6,4},{7,5},{8,10},{9,11},{10,... | collective-permute-start | bytes 1572872 | tf_op jit(solution)/shard_map/ppermute | solution.py:462
  406.2 24.8 %collective-permute-start.45 = (bf16[256,1024]{1,0:T(8,128)(2,1)}, bf16[256,1024]{1,0:T(8,128)(2,1)}, u32[]{:S(2)}, u32[]{:S(2)}) collective-permute-start(bf16[256,1024]{1,0:T(8,128)(2,1)} %fusion.3), channel_id=1, source_target_pairs={{0,4},{4,0},{8,12},{12,8},{16,20},{20,16},{24,28},{28,24},{1,5},{5... | collective-permute-start | bytes 1572872 | tf_op jit(solution)/shard_map/ppermute | solution.py:462
  (80 other events, 1081.8 us)

commit v3 on v2

--- a/solution.py
+++ b/solution.py
@@ -17,6 +17,7 @@
 score_scale = 0.125
 rope_base = 10000.0
 
+CHUNKS = ((0, 1, 4, 5), (2, 3, 6, 7))
 TOKEN_BITS = (4, 2, 1)
 QKV_BITS = (4, 2, 1)
 REST_BITS = (1, 4, 2)
@@ -190,19 +191,20 @@
             down[t * 128 : (t + 1) * 128, at] = piece[t, 256:384, :]
 
 
-def weight_pack_kernel(peers, shares, idx, gate, up, down, *outs):
-    for s in range(shares):
-        for m in range(peers):
-            e = jnp.bitwise_xor(idx[0], m) * shares + jnp.bitwise_xor(idx[1], s)
-            for k, w in enumerate((gate, up, down)):
-                outs[s][m, k * 128 : (k + 1) * 128, :] = w[e]
-
-
-def regroup_kernel(peers, shares, *refs):
-    ins, outs = split_refs(refs, shares, peers)
-    for m in range(peers):
+def weight_pack_kernel(shares, idx, gate, up, down, *outs):
+    for c, chunk in enumerate(CHUNKS):
         for s in range(shares):
-            outs[m][s] = ins[s][m]
+            for j, m in enumerate(chunk):
+                e = jnp.bitwise_xor(idx[0], m) * shares + jnp.bitwise_xor(idx[1], s)
+                for k, w in enumerate((gate, up, down)):
+                    outs[c * shares + s][j, k * 128 : (k + 1) * 128, :] = w[e]
+
+
+def regroup_kernel(shares, *refs):
+    ins, outs = split_refs(refs, shares, len(refs) - shares)
+    for j, out in enumerate(outs):
+        for s in range(shares):
+            out[s] = ins[s][j]
 
 
 def weight_grad_kernel(peers, shares, idx, *refs):
@@ -296,10 +298,9 @@
 
 def expert_rest_kernel(peers, shares, step, *refs):
     (idx,), pieces, ins, y_out, grad_out, (down,) = split_refs(
-        refs, 1, peers, 6, shares, shares, 1
+        refs, 1, peers, 6, shares, len(CHUNKS) * shares, 1
     )
     rows, scaled, hid, gpu, hot_in, gate_in = ins
-    width = rows.shape[1]
     span = y_out[0].shape[0] // peers
     block = shares * span
     load_down(idx[0], pieces, down, shares)
@@ -317,21 +318,25 @@
 
     lax.fori_loop(0, peers, out_rows, 0)
 
-    def body(c, carry):
-        at = pl.ds(pl.multiple_of(c * step, step), step)
-        both = mm(rows[:, at], gpu[...], 0, 0).astype(BF)
-        down_g = mm(hid[...], scaled[:, at], 0, 0).astype(BF)
-        for s in range(step // 128):
-            for t in range(shares):
-                m = jnp.bitwise_xor(c * (step // 128) + s, idx[0])
+    for c in range(len(CHUNKS)):
+        outs = grad_out[c * shares : (c + 1) * shares]
+
+        def body(pair, carry):
+            q = jnp.bitwise_xor(pair * 2 + c, idx[0] // 2)
+            at = pl.ds(pl.multiple_of(q * step, step), step)
+            both = mm(rows[:, at], gpu[...], 0, 0).astype(BF)
+            down_g = mm(hid[...], scaled[:, at], 0, 0).astype(BF)
+            for s in range(2):
+                j = pair * 2 + jnp.bitwise_xor(idx[0] % 2, s)
                 r = slice(s * 128, (s + 1) * 128)
-                out = grad_out[t]
-                out[m, 0:128, :] = both[r, t * 128 : (t + 1) * 128]
-                out[m, 128:256, :] = both[r, (shares + t) * 128 : (shares + t + 1) * 128]
-                out[m, 256:384, :] = down_g[t * 128 : (t + 1) * 128, r]
-        return carry
-
-    lax.fori_loop(0, width // step, body, 0)
+                for t in range(shares):
+                    out = outs[t]
+                    out[j, 0:128, :] = both[r, t * 128 : (t + 1) * 128]
+                    out[j, 128:256, :] = both[r, (shares + t) * 128 : (shares + t + 1) * 128]
+                    out[j, 256:384, :] = down_g[t * 128 : (t + 1) * 128, r]
+            return carry
+
+        lax.fori_loop(0, 2, body, 0)
 
 
 def hi_lo_rows(row, count):
@@ -363,24 +368,25 @@
 
 def attn_bwd_kernel(peers, shares, dims, *refs):
     n_q, n_kv = dims
-    ins, g_out, msg2, (sums, partial) = split_refs(refs, 13, 2, shares, 2)
-    idx, msg, wall, qkv, att, logs, cos, sin, seg_c, seg_r, hid, rows2, x = ins
+    (idx,), msgs, ins, g_out, msg2, (sums, partial, resid) = split_refs(
+        refs, 1, shares, 11, 2, shares, 3
+    )
+    wall, qkv, att, logs, cos, sin, seg_c, seg_r, hid, rows2, x = ins
     length, width = x.shape
     own = length // shares
-    span = msg.shape[0] // shares
+    span = msgs[0].shape[0]
     qk_w = (n_q + n_kv) * HD
     all_w = (n_q + 2 * n_kv) * HD
     o_at = all_w + n_q * HD
-    resid = jnp.concatenate([msg[s * span : s * span + own, :width] for s in range(shares)], 0)
-    starts = [jnp.bitwise_xor(idx[1], s) * span for s in range(shares)]
-    logit = jnp.concatenate(
-        [msg[pl.ds(pl.multiple_of(at, 16), own), width:] for at in starts], 0
-    )
+    for s, msg in enumerate(msgs):
+        at = pl.multiple_of(jnp.bitwise_xor(idx[1], s) * own, own)
+        resid[pl.ds(at, own), :] = msg[0:own, :width]
+    logit = jnp.concatenate([msg[0:own, width:] for msg in msgs], 0)
     gain_moe = jnp.zeros((1, width), F32)
-    for s in range(shares):
-        extra = msg[s * span + own : (s + 1) * span, :width].astype(F32)
+    for msg in msgs:
+        extra = msg[own:, :width].astype(F32)
         gain_moe = gain_moe + jnp.sum(extra, axis=0, keepdims=True)
-    att_grad = jnp.dot(resid, wall[:, all_w:o_at], preferred_element_type=F32).astype(BF)
+    att_grad = jnp.dot(resid[...], wall[:, all_w:o_at], preferred_element_type=F32).astype(BF)
     allowed = allowed_pairs(seg_c[...], seg_r[...], length)
     group = n_q // n_kv
     lane = lax.broadcasted_iota(jnp.int32, (length, LANES), 1)
@@ -412,7 +418,7 @@
     qk_low = rotate_lanes(qk_grad, cos[...], -sin[...]).astype(BF)
     low = jnp.concatenate([qk_low, jnp.concatenate(v_grads, 1).astype(BF)], 1)
     sums[:, :all_w] = mm(hid[...], low, 0, 0)
-    sums[:, all_w:o_at] = mm(resid, att[...], 0, 0)
+    sums[:, all_w:o_at] = mm(resid[...], att[...], 0, 0)
     place = lax.broadcasted_iota(jnp.int32, (LANES, width), 0)
     gain_hi = gain_moe.astype(BF).astype(F32)
     rows = jnp.where(place == 32, gain_hi, jnp.where(place == 33, gain_moe - gain_hi, 0.0))
@@ -445,6 +451,23 @@
     gain_out[...] = jnp.broadcast_to(gain_sum, gain_out.shape)
 
 
+def attn_grad_kernel(terms, widths, *refs):
+    ins, (query, key, value, output, router, gain) = split_refs(refs, terms, 6)
+    q_w, kv_w, experts = widths
+    total = ins[0][...].astype(F32)
+    for ref in ins[1:]:
+        total = total + ref[...].astype(F32)
+    all_w = q_w + 2 * kv_w
+    query[...] = total[:, :q_w]
+    key[...] = total[:, q_w : q_w + kv_w]
+    value[...] = total[:, q_w + kv_w : all_w]
+    output[...] = jnp.transpose(total[:, all_w : all_w + q_w])
+    tail = total[:, all_w + q_w :]
+    router[...] = tail[:, :experts]
+    tail_t = jnp.transpose(tail)
+    gain[...] = tail_t[experts : experts + 1, :] + tail_t[experts + 1 : experts + 2, :]
+
+
 def layer_out_kernel(first, second, res, out):
     total = first[...].astype(F32) + second[...].astype(F32)
     out[...] = (res[...] + total).astype(BF)
@@ -494,6 +517,19 @@
     far_even = permute(parts[2][:half] + far[:half], "tensor", 2)
     odd = parts[0][half:] + own[half:] + far_odd
     return reduce_dp(parts[0][:half] + own[:half], odd, far_even)
+
+
+def move_chunks(parts):
+    pieces = {}
+    for c, chunk in enumerate(CHUNKS):
+        shape = parts[c][0].shape
+        groups = call(
+            functools.partial(regroup_kernel, len(parts[c])),
+            [((len(parts[c]),) + shape[1:], BF)] * len(chunk),
+        )(*parts[c])
+        for m, group in zip(chunk, groups):
+            pieces[m] = permute(group, "dp", m) if m else group
+    return [pieces[m] for m in sorted(pieces)]
 
 
 def per_device(
@@ -544,11 +580,13 @@
         w_up = lax.all_gather(w_up, "rep", axis=1, tiled=True)
         w_down = lax.all_gather(w_down, "rep", axis=2, tiled=True)
     weight_parts = call(
-        functools.partial(weight_pack_kernel, peers, shares),
-        [((peers, 384, LANES), BF)] * shares,
+        functools.partial(weight_pack_kernel, shares),
+        [((peers // 2, 384, LANES), BF)] * (2 * shares),
         smem=1,
     )(idx, w_gate, w_up, w_down)
-    weight_parts = swap(weight_parts, "tensor")
+    pieces = move_chunks(
+        [swap(weight_parts[c * shares : (c + 1) * shares], "tensor") for c in range(len(CHUNKS))],
+    )
     grads_in = gather_all(out_grad)
 
     segment = seq_ids[0]
@@ -582,10 +620,7 @@
 
     ids_own = lax.dynamic_slice_in_dim(expert_ids, lax.axis_index("tensor") * own, own, 0)
     parts = swap(parts, "tensor")
-    weight_parts = call(
-        functools.partial(regroup_kernel, peers, shares), [((shares, 384, LANES), BF)] * peers
-    )(*weight_parts)
-    pieces = swap(weight_parts, "dp")
+    ids_own = lax.dynamic_slice_in_dim(expert_ids, lax.axis_index("tensor") * own, own, 0)
     res, router, msg = call(
         functools.partial(post_attn_kernel, experts, shares),
         [((own, width), F32), ((own, LANES), F32), ((own, wide), BF)],
@@ -612,34 +647,47 @@
     back = reduce_all(row_back)
     rest = call(
         functools.partial(expert_rest_kernel, peers, shares, 256),
-        [((peers * own, width), BF)] * shares + [((peers, 384, LANES), BF)] * shares,
+        [((peers * own, width), BF)] * shares
+        + [((peers // 2, 384, LANES), BF)] * (2 * shares),
         scratch=[((ff, width), BF)],
         smem=1,
     )(idx, *pieces, *saved)
     y_parts, grad_parts = rest[:shares], rest[shares:]
-    grad_parts = swap(grad_parts, "tensor")
-    grad_parts = call(
-        functools.partial(regroup_kernel, peers, shares), [((shares, 384, LANES), BF)] * peers
-    )(*grad_parts)
-    grad_parts = swap(grad_parts, "dp")
+    grad_parts = [
+        swap(grad_parts[c * shares : (c + 1) * shares], "tensor")
+        for c in range(len(CHUNKS))
+    ]
+    grad_parts = move_chunks(grad_parts)
     rgrad, msg = call(
         moe_back_kernel, [((own, width), F32), ((own + 16, wide), BF)]
     )(*back, router, res, gains, misc, out_grad)
-    msg_all = lax.all_gather(msg, "tensor", axis=0, tiled=True)
-    y_parts, msg_all = lax.optimization_barrier((y_parts, msg_all))
-    mixed = reduce_all(y_parts)
+    msgs = swap([msg] * shares, "tensor")
 
     outs = call(
         functools.partial(attn_bwd_kernel, peers, shares, dims),
         [((width // 2, pack_w), BF)] * 2 + [((own + 16, width), BF)] * shares,
-        scratch=[((width, pack_w), F32), ((length, width), F32)],
+        scratch=[((width, pack_w), F32), ((length, width), F32), ((length, width), BF)],
         smem=1,
-    )(idx, msg_all, wall, qkv, att, logs, cosine, sine, seg_c, seg_r, hid, rows_near, x_all)
+    )(idx, *msgs, wall, qkv, att, logs, cosine, sine, seg_c, seg_r, hid, rows_near, x_all)
     msg2 = outs[2:]
-    w_sums = reduce_dp(outs[0], outs[1])
-    total = w_sums[0].astype(F32) + w_sums[1].astype(F32)
+    y_parts, msg2 = lax.optimization_barrier((y_parts, msg2))
+    mixed = reduce_all(y_parts)
+    terms = reduce_dp(outs[0], outs[1])
     if rep > 1:
-        total = lax.psum_scatter(total, "rep", scatter_dimension=0, tiled=True)
+        total = terms[0].astype(F32) + terms[1].astype(F32)
+        terms = (lax.psum_scatter(total, "rep", scatter_dimension=0, tiled=True),)
+    rows_own = terms[0].shape[0]
+    q_grad, k_grad, v_grad, o_grad, router_grad, gain_moe_grad = call(
+        functools.partial(attn_grad_kernel, len(terms), (q_w, kv_w, experts)),
+        [
+            ((rows_own, q_w), F32),
+            ((rows_own, kv_w), F32),
+            ((rows_own, kv_w), F32),
+            ((q_w, rows_own), F32),
+            ((rows_own, experts), F32),
+            ((1, rows_own), F32),
+        ],
+    )(*terms)
 
     msg2 = swap(msg2, "tensor")
     input_grad, gain_rows = call(
@@ -662,17 +710,16 @@
         gate_grad = lax.psum_scatter(gate_grad, "rep", scatter_dimension=1, tiled=True)
         up_grad = lax.psum_scatter(up_grad, "rep", scatter_dimension=1, tiled=True)
         down_grad = lax.psum_scatter(down_grad, "rep", scatter_dimension=2, tiled=True)
-    o_at = all_w + q_w
     return (
         layer_output,
         input_grad,
         gain_attn_grad,
-        total[:, o_at + experts] + total[:, o_at + experts + 1],
-        total[:, :q_w],
-        total[:, q_w : q_w + kv_w],
-        total[:, q_w + kv_w : all_w],
-        total[:, all_w:o_at].T,
-        total[:, o_at : o_at + experts],
+        gain_moe_grad.reshape(-1),
+        q_grad,
+        k_grad,
+        v_grad,
+        o_grad,
+        router_grad,
         gate_grad,
         up_grad,
         down_grad,

time: 456 us -> 521 us (1.14)
  waiting for transfers between devices: 250 us -> 318 us
  blocking collectives: 9.12 us -> 0 us
  Pallas kernels: 74.2 us -> 79.9 us
    ppermute x35 -> x49, waiting for transfers between devices: 101 us -> 190 us  [permute(): return lax.ppermute(value, axis, [(i, i ^ bit) for i in range(count)])]
    ppermute x29 -> x24, waiting for transfers between devices: 148 us -> 110 us  [swap(): lax.ppermute(values[m], axis, [(i, i ^ m) for i in range(len(values))])]
    all_to_all x1, waiting for transfers between devices: 0.72 us -> 18 us  [per_device(): lax.all_to_all(gain_cut, 'dp', split_axis=0, concat_axis=0, tiled=True)]
    ppermute x35 -> x49, starting transfers between devices: 47.9 us -> 64 us  [permute(): return lax.ppermute(value, axis, [(i, i ^ bit) for i in range(count)])]
    ppermute x29 -> x24, starting transfers between devices: 27 us -> 15.1 us  [swap(): lax.ppermute(values[m], axis, [(i, i ^ m) for i in range(len(values))])]
    all_gather x1 -> x0, blocking collectives: 9.12 us -> none  [per_device(): msg_all = lax.all_gather(msg, 'tensor', axis=0, tiled=True)]
    pallas_call x12 -> x15, Pallas kernels: 74.2 us -> 79.9 us  [run(): pl.pallas_call(kernel, out_shape=[jax.ShapeDtypeStruct(s, d) for s, d in...]
    unnamed x107 -> x124, local copies, waits for them, and re-layouts: 15.4 us -> 16.8 us
  transfers between devices with their start and end apart: 65 -> 74, of which waited for: 36 -> 36; matrix products, arithmetic and copies ran while one was open for 7% -> 5% of each run, Pallas kernels for 9% -> 8%
where the time goes in v3:
time: 521 us; the launch traced here: 520 us
  waiting for transfers between devices  318 us (61%)
  starting transfers between devices  83 us (16%)
  Pallas kernels  79.9 us (15%)
  local copies, waits for them, and re-layouts  26.2 us (5%)
  other arithmetic  10.7 us (2%)
    ppermute x49, waiting for transfers between devices, permute(): return lax.ppermute(value, axis, [(i, i ^ bit) for i in range(count)])  190 us
    ppermute x24, waiting for transfers between devices, swap(): lax.ppermute(values[m], axis, [(i, i ^ m) for i in range(len(values))])  110 us
    pallas_call x15, Pallas kernels, run(): pl.pallas_call(kernel, out_shape=[jax.ShapeDtypeStruct(s, d) for s, d in...  79.9 us
    ppermute x49, starting transfers between devices, permute(): return lax.ppermute(value, axis, [(i, i ^ bit) for i in range(count)])  64 us
    all_to_all x1, waiting for transfers between devices, per_device(): lax.all_to_all(gain_cut, 'dp', split_axis=0, concat_axis=0, tiled=True)  18 us
    unnamed x124, local copies, waits for them, and re-layouts  16.8 us
    ppermute x24, starting transfers between devices, swap(): lax.ppermute(values[m], axis, [(i, i ^ m) for i in range(len(values))])  15.1 us
  transfers between devices with their start and end apart: 74, of which 36 were waited for; matrix products, arithmetic and copies ran while one was open for 5% of the time, Pallas kernels for 8%

profile of v3, /device:TPU:0, one launch (start us, length us, event | category | flops | bytes accessed | tf_op | source)
XLA Modules:
  0.0 519.5 jit_solution(11437530326609380873)
XLA Ops:
  3.0 4.1 collective-permute-start.16
  17.9 8.7 %collective-permute-done.17 = bf16[256,512]{1,0:T(8,128)(2,1)S(1)} collective-permute-done((bf16[256,512]{1,0:T(8,128)(2,1)S(1)}, bf16[256,512]{1,0:T(8,128)(2,1)S(1)}, u32[]{:S(2)}, u32[]{:S(2)}) %collective-permute-start.17) | collective-permute-done | bytes 262176 | tf_op jit(solution)/shard_map/ppermute | solution.py:485
  31.6 5.6 %collective-permute-done.21.refs_8_ = bf16[512,384]{1,0:T(8,128)(2,1)S(1)} collective-permute-done((bf16[512,384]{1,0:T(8,128)(2,1)S(1)}, bf16[512,384]{1,0:T(8,128)(2,1)S(1)}, u32[]{:S(2)}, u32[]{:S(2)}) %collective-permute-start.21) | collective-permute-done | bytes 393248 | tf_op jit(solution)/shard_map/ppermute | solution.py:485
  40.3 5.4 %shard_map.232 = (bf16[64,1024]{1,0:T(8,128)(2,1)}, bf16[64,1024]{1,0:T(8,128)(2,1)}, bf16[64,1024]{1,0:T(8,128)(2,1)}, bf16[64,1024]{1,0:T(8,128)(2,1)}, bf16[1...) custom-call(s32[2]{0:T(128)} %pad_add_fusion.idx.refs_0_, ...), custom_call_target="tpu_custom_call" | custom-call | tf_op jit(solution)/shard_map/pallas_call | solution.py:37
  61.0 7.0 %collective-permute-done.25 = bf16[64,1152]{1,0:T(8,128)(2,1)S(1)} collective-permute-done((bf16[64,1152]{1,0:T(8,128)(2,1)}, bf16[64,1152]{1,0:T(8,128)(2,1)S(1)}, u32[]{:S(2)}, u32[]{:S(2)}) %collective-permute-start.25) | collective-permute-done | bytes 147488 | tf_op jit(solution)/shard_map/ppermute | solution.py:485
  69.0 3.7 shard_map.229
  80.4 21.8 %collective-permute-done.27 = bf16[256,1152]{1,0:T(8,128)(2,1)S(1)} collective-permute-done((bf16[256,1152]{1,0:T(8,128)(2,1)S(1)}, bf16[256,1152]{1,0:T(8,128)(2,1)S(1)}, u32[]{:S(2)}, u32[]{:S(2)}) %collective-permute-start.27) | collective-permute-done | bytes 589856 | tf_op jit(solution)/shard_map/ppermute | solution.py:485
  112.8 50.2 %collective-permute-done.5.refs_2_ = bf16[4,384,128]{2,1,0:T(8,128)(2,1)S(1)} collective-permute-done((bf16[4,384,128]{2,1,0:T(8,128)(2,1)}, bf16[4,384,128]{2,1,0:T(8,128)(2,1)S(1)}, u32[]{:S(2)}, u32[]{:S(2)}) %collective-permute-start.5) | collective-permute-done | bytes 393248 | tf_op jit(solution)/shard_map/ppermute | solution.py:479
  174.9 15.9 %collective-permute-done.9.refs_13_.refs_5_ = bf16[4,384,128]{2,1,0:T(8,128)(2,1)S(1)} collective-permute-done((bf16[4,384,128]{2,1,0:T(8,128)(2,1)}, bf16[4,384,128]{2,1,0:T(8,128)(2,1)S(1)}, u32[]{:S(2)}, u32[]{:S(2)}) %collective-permute-start.9) | collective-permute-done | bytes 393248 | tf_op jit(solution)/shard_map/ppermute | solution.py:485
  190.8 7.3 %collective-permute-done.10.refs_14_.refs_6_ = bf16[4,384,128]{2,1,0:T(8,128)(2,1)S(1)} collective-permute-done((bf16[4,384,128]{2,1,0:T(8,128)(2,1)}, bf16[4,384,128]{2,1,0:T(8,128)(2,1)S(1)}, u32[]{:S(2)}, u32[]{:S(2)}) %collective-permute-start.10) | collective-permute-done | bytes 393248 | tf_op jit(solution)/shard_map/ppermute | solution.py:485
  201.6 7.3 %collective-permute-done.8.refs_12_.refs_4_ = bf16[4,384,128]{2,1,0:T(8,128)(2,1)S(1)} collective-permute-done((bf16[4,384,128]{2,1,0:T(8,128)(2,1)}, bf16[4,384,128]{2,1,0:T(8,128)(2,1)S(1)}, u32[]{:S(2)}, u32[]{:S(2)}) %collective-permute-start.8) | collective-permute-done | bytes 393248 | tf_op jit(solution)/shard_map/ppermute | solution.py:485
  211.1 10.8 %collective-permute-done.11.refs_15_.refs_7_ = bf16[4,384,128]{2,1,0:T(8,128)(2,1)S(1)} collective-permute-done((bf16[4,384,128]{2,1,0:T(8,128)(2,1)}, bf16[4,384,128]{2,1,0:T(8,128)(2,1)S(1)}, u32[]{:S(2)}, u32[]{:S(2)}) %collective-permute-start.11) | collective-permute-done | bytes 393248 | tf_op jit(solution)/shard_map/ppermute | solution.py:485
  223.5 11.5 %collective-permute-done.12.refs_16_.refs_8_ = bf16[4,384,128]{2,1,0:T(8,128)(2,1)S(1)} collective-permute-done((bf16[4,384,128]{2,1,0:T(8,128)(2,1)}, bf16[4,384,128]{2,1,0:T(8,128)(2,1)S(1)}, u32[]{:S(2)}, u32[]{:S(2)}) %collective-permute-start.12) | collective-permute-done | bytes 393248 | tf_op jit(solution)/shard_map/ppermute | solution.py:485
  235.8 22.4 %shard_map.234 = (bf16[512,1152]{1,0:T(8,128)(2,1)}, bf16[512,1152]{1,0:T(8,128)(2,1)}, bf16[512,1152]{1,0:T(8,128)(2,1)}, bf16[512,1152]{1,0:T(8,128)(2,1)}, bf...) custom-call(s32[2]{0:T(128)} %pad_add_fusion.idx.refs_0_, ...), custom_call_target="tpu_custom_call" | custom-call | tf_op jit(solution)/shard_map/pallas_call | solution.py:37
  264.9 14.2 %collective-permute-done.40 = bf16[256,1152]{1,0:T(8,128)(2,1)S(1)} collective-permute-done((bf16[256,1152]{1,0:T(8,128)(2,1)S(1)}, bf16[256,1152]{1,0:T(8,128)(2,1)S(1)}, u32[]{:S(2)}, u32[]{:S(2)}) %collective-permute-start.40) | collective-permute-done | bytes 589856 | tf_op jit(solution)/shard_map/ppermute | solution.py:485
  280.9 10.2 %collective-permute-done.39 = bf16[256,1152]{1,0:T(8,128)(2,1)S(1)} collective-permute-done((bf16[256,1152]{1,0:T(8,128)(2,1)S(1)}, bf16[256,1152]{1,0:T(8,128)(2,1)S(1)}, u32[]{:S(2)}, u32[]{:S(2)}) %collective-permute-start.39) | collective-permute-done | bytes 589856 | tf_op jit(solution)/shard_map/ppermute | solution.py:485
  293.6 13.7 %collective-permute-start.42 = (bf16[128,1152]{1,0:T(8,128)(2,1)S(1)}, bf16[128,1152]{1,0:T(8,128)(2,1)S(1)}, u32[]{:S(2)}, u32[]{:S(2)}) collective-permute-start(bf16[128,1152]{1,0:T(8,128)(2,1)S(1)} %slice.121), channel_id=1, source_target_pairs={{0,8},{4,12},{8,0},{12,4},{16,24},{20,28},{24,16},{28,20},{1,9},{5... | collective-permute-start | bytes 884744 | tf_op jit(solution)/shard_map/ppermute | solution.py:485
  307.3 5.3 %collective-permute-done.42 = bf16[128,1152]{1,0:T(8,128)(2,1)S(1)} collective-permute-done((bf16[128,1152]{1,0:T(8,128)(2,1)S(1)}, bf16[128,1152]{1,0:T(8,128)(2,1)S(1)}, u32[]{:S(2)}, u32[]{:S(2)}) %collective-permute-start.42) | collective-permute-done | bytes 294944 | tf_op jit(solution)/shard_map/ppermute | solution.py:485
  315.1 5.9 %collective-permute-done.43.refs_1_ = bf16[64,1152]{1,0:T(8,128)(2,1)S(1)} collective-permute-done((bf16[64,1152]{1,0:T(8,128)(2,1)S(1)}, bf16[64,1152]{1,0:T(8,128)(2,1)S(1)}, u32[]{:S(2)}, u32[]{:S(2)}) %collective-permute-start.43) | collective-permute-done | bytes 147488 | tf_op jit(solution)/shard_map/ppermute | solution.py:485
  325.9 15.5 %shard_map.235 = (bf16[512,1024]{1,0:T(8,128)(2,1)}, bf16[512,1024]{1,0:T(8,128)(2,1)}, bf16[512,1024]{1,0:T(8,128)(2,1)}, bf16[512,1024]{1,0:T(8,128)(2,1)}, bf...) custom-call(s32[2]{0:T(128)} %pad_add_fusion.idx.refs_0_, ...), custom_call_target="tpu_custom_call" | custom-call | tf_op jit(solution)/shard_map/pallas_call | solution.py:37
  342.2 7.1 %shard_map.237 = (bf16[512,896]{1,0:T(8,128)(2,1)}, bf16[512,896]{1,0:T(8,128)(2,1)}, bf16[80,1024]{1,0:T(8,128)(2,1)}, bf16[80,1024]{1,0:T(8,128)(2,1)}, bf16[8...) custom-call(s32[2]{0:T(128)} %pad_add_fusion.idx.refs_0_, bf16[80,1152]{1,0:T(8,128)(2,1)} %get-tuple-element.140.refs_1_, ...), custom_call_target="tpu_custom_call" | custom-call | tf_op jit(solution)/shard_map/pallas_call | solution.py:37
  355.5 20.8 %collective-permute-done.61.refs_2_ = bf16[4,384,128]{2,1,0:T(8,128)(2,1)S(1)} collective-permute-done((bf16[4,384,128]{2,1,0:T(8,128)(2,1)}, bf16[4,384,128]{2,1,0:T(8,128)(2,1)S(1)}, u32[]{:S(2)}, u32[]{:S(2)}) %collective-permute-start.61) | collective-permute-done | bytes 393248 | tf_op jit(solution)/shard_map/ppermute | solution.py:479
  376.3 6.8 %collective-permute-done.62.refs_3_ = bf16[4,384,128]{2,1,0:T(8,128)(2,1)S(1)} collective-permute-done((bf16[4,384,128]{2,1,0:T(8,128)(2,1)S(1)}, bf16[4,384,128]{2,1,0:T(8,128)(2,1)S(1)}, u32[]{:S(2)}, u32[]{:S(2)}) %collective-permute-start.62) | collective-permute-done | bytes 393248 | tf_op jit(solution)/shard_map/ppermute | solution.py:479
  388.2 6.9 %collective-permute-done.65.refs_2_ = bf16[4,384,128]{2,1,0:T(8,128)(2,1)} collective-permute-done((bf16[4,384,128]{2,1,0:T(8,128)(2,1)S(1)}, bf16[4,384,128]{2,1,0:T(8,128)(2,1)}, u32[]{:S(2)}, u32[]{:S(2)}) %collective-permute-start.65) | collective-permute-done | bytes 393248 | tf_op jit(solution)/shard_map/ppermute | solution.py:479
  395.4 7.6 %collective-permute-done.66.refs_3_ = bf16[4,384,128]{2,1,0:T(8,128)(2,1)} collective-permute-done((bf16[4,384,128]{2,1,0:T(8,128)(2,1)S(1)}, bf16[4,384,128]{2,1,0:T(8,128)(2,1)}, u32[]{:S(2)}, u32[]{:S(2)}) %collective-permute-start.66) | collective-permute-done | bytes 393248 | tf_op jit(solution)/shard_map/ppermute | solution.py:479
  410.1 8.1 %collective-permute-done.55.refs_2_ = bf16[80,1024]{1,0:T(8,128)(2,1)S(1)} collective-permute-done((bf16[80,1024]{1,0:T(8,128)(2,1)}, bf16[80,1024]{1,0:T(8,128)(2,1)S(1)}, u32[]{:S(2)}, u32[]{:S(2)}) %collective-permute-start.55) | collective-permute-done | bytes 163872 | tf_op jit(solution)/shard_map/ppermute | solution.py:479
  431.4 27.8 %collective-permute-done.52 = bf16[128,1024]{1,0:T(8,128)(2,1)S(1)} collective-permute-done((bf16[128,1024]{1,0:T(8,128)(2,1)S(1)}, bf16[128,1024]{1,0:T(8,128)(2,1)S(1)}, u32[]{:S(2)}, u32[]{:S(2)}) %collective-permute-start.52) | collective-permute-done | bytes 262176 | tf_op jit(solution)/shard_map/ppermute | solution.py:485
  470.1 3.8 all-to-all-start
  473.9 7.1 %collective-permute-done.68.refs_3_ = bf16[4,384,128]{2,1,0:T(8,128)(2,1)S(1)} collective-permute-done((bf16[4,384,128]{2,1,0:T(8,128)(2,1)}, bf16[4,384,128]{2,1,0:T(8,128)(2,1)S(1)}, u32[]{:S(2)}, u32[]{:S(2)}) %collective-permute-start.68) | collective-permute-done | bytes 393248 | tf_op jit(solution)/shard_map/ppermute | solution.py:485
  481.5 7.2 %collective-permute-done.72.refs_7_ = bf16[4,384,128]{2,1,0:T(8,128)(2,1)S(1)} collective-permute-done((bf16[4,384,128]{2,1,0:T(8,128)(2,1)S(1)}, bf16[4,384,128]{2,1,0:T(8,128)(2,1)S(1)}, u32[]{:S(2)}, u32[]{:S(2)}) %collective-permute-start.72) | collective-permute-done | bytes 393248 | tf_op jit(solution)/shard_map/ppermute | solution.py:485
  489.5 4.9 shard_map.243
  494.5 18.0 %all-to-all-done = f32[8,1,128]{2,1,0:T(1,128)S(1)} async-done(((f32[8,1,128]{2,1,0:T(1,128)}), f32[8,1,128]{2,1,0:T(1,128)S(1)}, u32[]{:S(2)}, u32[]{:S(2)}) %all-to-all-start) | async-done | bytes 4128 | tf_op jit(solution)/shard_map/all_to_all | solution.py:697
  (295 shorter events, 145.6 us)
Async XLA Ops:
  72.7 34.1 %collective-permute-start = (bf16[4,384,128]{2,1,0:T(8,128)(2,1)}, bf16[4,384,128]{2,1,0:T(8,128)(2,1)S(1)}, u32[]{:S(2)}, u32[]{:S(2)}) collective-permute-start(bf16[4,384,128]{2,1,0:T(8,128)(2,1)} %get-tuple-element.102), channel_id=1, source_target_pairs={{0,1},{1,0},{2,3},{3,2},{4,5},{5,4},{6,7},{7,6},{8,9},{9,8},{10,11... | collective-permute-start | bytes 1179656 | tf_op jit(solution)/shard_map/ppermute | solution.py:479
  72.7 34.6 %collective-permute-start.1 = (bf16[4,384,128]{2,1,0:T(8,128)(2,1)}, bf16[4,384,128]{2,1,0:T(8,128)(2,1)S(1)}, u32[]{:S(2)}, u32[]{:S(2)}) collective-permute-start(bf16[4,384,128]{2,1,0:T(8,128)(2,1)} %get-tuple-element.103), channel_id=1, source_target_pairs={{0,2},{1,3},{2,0},{3,1},{4,6},{5,7},{6,4},{7,5},{8,10},{9,11},{10,... | collective-permute-start | bytes 1179656 | tf_op jit(solution)/shard_map/ppermute | solution.py:479
  74.3 34.6 %collective-permute-start.2 = (bf16[4,384,128]{2,1,0:T(8,128)(2,1)}, bf16[4,384,128]{2,1,0:T(8,128)(2,1)S(1)}, u32[]{:S(2)}, u32[]{:S(2)}) collective-permute-start(bf16[4,384,128]{2,1,0:T(8,128)(2,1)} %get-tuple-element.104), channel_id=1, source_target_pairs={{0,3},{1,2},{2,1},{3,0},{4,7},{5,6},{6,5},{7,4},{8,11},{9,10},{10,... | collective-permute-start | bytes 1179656 | tf_op jit(solution)/shard_map/ppermute | solution.py:479
  75.3 30.0 %collective-permute-start.33 = (bf16[256,1024]{1,0:T(8,128)(2,1)S(1)}, bf16[256,1024]{1,0:T(8,128)(2,1)S(1)}, u32[]{:S(2)}, u32[]{:S(2)}) collective-permute-start(bf16[256,1024]{1,0:T(8,128)(2,1)S(1)} %pad_maximum_fusion.2), channel_id=1, source_target_pairs={{0,4},{4,0},{8,12},{12,8},{16,20},{20,16},{24,28},{28,24},{1,5},{5... | collective-permute-start | bytes 1572872 | tf_op jit(solution)/shard_map/ppermute | solution.py:485
  103.1 95.1 %collective-permute-start.29 = (bf16[512,1152]{1,0:T(8,128)(2,1)}, bf16[512,1152]{1,0:T(8,128)(2,1)}, u32[]{:S(2)}, u32[]{:S(2)}) collective-permute-start(bf16[512,1152]{1,0:T(8,128)(2,1)} %constant_dynamic-update-slice_fusion.3.refs_1_), channel_id=1, source_target_pairs={{0,2},{1,3},{2,0},{3,1},{4,6},{5,7},{6,4},{7,5},{8,10},{9,11},{10,... | collective-permute-start | bytes 3538952 | tf_op jit(solution)/shard_map/ppermute | solution.py:485
  106.9 94.2 %collective-permute-start.35 = (bf16[512,1024]{1,0:T(8,128)(2,1)}, bf16[512,1024]{1,0:T(8,128)(2,1)}, u32[]{:S(2)}, u32[]{:S(2)}) collective-permute-start(bf16[512,1024]{1,0:T(8,128)(2,1)} %constant_dynamic-update-slice_fusion.7.refs_5_), channel_id=1, source_target_pairs={{0,2},{1,3},{2,0},{3,1},{4,6},{5,7},{6,4},{7,5},{8,10},{9,11},{10,... | collective-permute-start | bytes 3145736 | tf_op jit(solution)/shard_map/ppermute | solution.py:485
  107.4 55.7 %collective-permute-start.5 = (bf16[4,384,128]{2,1,0:T(8,128)(2,1)}, bf16[4,384,128]{2,1,0:T(8,128)(2,1)S(1)}, u32[]{:S(2)}, u32[]{:S(2)}) collective-permute-start(bf16[4,384,128]{2,1,0:T(8,128)(2,1)} %get-tuple-element.109), channel_id=1, source_target_pairs={{0,2},{1,3},{2,0},{3,1},{4,6},{5,7},{6,4},{7,5},{8,10},{9,11},{10,... | collective-permute-start | bytes 1179656 | tf_op jit(solution)/shard_map/ppermute | solution.py:479
  108.9 60.1 %collective-permute-start.6 = (bf16[4,384,128]{2,1,0:T(8,128)(2,1)S(1)}, bf16[4,384,128]{2,1,0:T(8,128)(2,1)S(1)}, u32[]{:S(2)}, u32[]{:S(2)}) collective-permute-start(bf16[4,384,128]{2,1,0:T(8,128)(2,1)S(1)} %copy-done.53), channel_id=1, source_target_pairs={{0,3},{1,2},{2,1},{3,0},{4,7},{5,6},{6,5},{7,4},{8,11},{9,10},{10,... | collective-permute-start | bytes 1179656 | tf_op jit(solution)/shard_map/ppermute | solution.py:479
  112.2 62.6 %collective-permute-start.3 = (bf16[4,384,128]{2,1,0:T(8,128)(2,1)}, bf16[4,384,128]{2,1,0:T(8,128)(2,1)S(1)}, u32[]{:S(2)}, u32[]{:S(2)}) collective-permute-start(bf16[4,384,128]{2,1,0:T(8,128)(2,1)} %get-tuple-element.106), channel_id=1, source_target_pairs={{0,4},{4,0},{8,12},{12,8},{16,20},{20,16},{24,28},{28,24},{1,5},{5... | collective-permute-start | bytes 1179656 | tf_op jit(solution)/shard_map/ppermute | solution.py:485
  163.0 27.8 %collective-permute-start.9 = (bf16[4,384,128]{2,1,0:T(8,128)(2,1)}, bf16[4,384,128]{2,1,0:T(8,128)(2,1)S(1)}, u32[]{:S(2)}, u32[]{:S(2)}) collective-permute-start(bf16[4,384,128]{2,1,0:T(8,128)(2,1)} %get-tuple-element.113), channel_id=1, source_target_pairs={{0,16},{4,20},{8,24},{12,28},{16,0},{20,4},{24,8},{28,12},{1,17},{... | collective-permute-start | bytes 1179656 | tf_op jit(solution)/shard_map/ppermute | solution.py:485
  169.0 29.1 %collective-permute-start.10 = (bf16[4,384,128]{2,1,0:T(8,128)(2,1)}, bf16[4,384,128]{2,1,0:T(8,128)(2,1)S(1)}, u32[]{:S(2)}, u32[]{:S(2)}) collective-permute-start(bf16[4,384,128]{2,1,0:T(8,128)(2,1)} %get-tuple-element.114), channel_id=1, source_target_pairs={{0,20},{4,16},{8,28},{12,24},{16,4},{20,0},{24,12},{28,8},{1,21},{... | collective-permute-start | bytes 1179656 | tf_op jit(solution)/shard_map/ppermute | solution.py:485
  174.9 26.2 %collective-permute-start.7 = (bf16[4,384,128]{2,1,0:T(8,128)(2,1)}, bf16[4,384,128]{2,1,0:T(8,128)(2,1)S(1)}, u32[]{:S(2)}, u32[]{:S(2)}) collective-permute-start(bf16[4,384,128]{2,1,0:T(8,128)(2,1)} %get-tuple-element.111), channel_id=1, source_target_pairs={{0,8},{4,12},{8,0},{12,4},{16,24},{20,28},{24,16},{28,20},{1,9},{5... | collective-permute-start | bytes 1179656 | tf_op jit(solution)/shard_map/ppermute | solution.py:485
  198.2 36.9 %collective-permute-start.28 = (bf16[512,1152]{1,0:T(8,128)(2,1)}, bf16[512,1152]{1,0:T(8,128)(2,1)}, u32[]{:S(2)}, u32[]{:S(2)}) collective-permute-start(bf16[512,1152]{1,0:T(8,128)(2,1)} %constant_dynamic-update-slice_fusion.3.refs_1_), channel_id=1, source_target_pairs={{0,1},{1,0},{2,3},{3,2},{4,5},{5,4},{6,7},{7,6},{8,9},{9,8},{10,11... | collective-permute-start | bytes 3538952 | tf_op jit(solution)/shard_map/ppermute | solution.py:485
  198.2 36.9 %collective-permute-start.30 = (bf16[512,1152]{1,0:T(8,128)(2,1)}, bf16[512,1152]{1,0:T(8,128)(2,1)}, u32[]{:S(2)}, u32[]{:S(2)}) collective-permute-start(bf16[512,1152]{1,0:T(8,128)(2,1)} %collective-permute-done.29.refs_3_), channel_id=1, source_target_pairs={{0,1},{1,0},{2,3},{3,2},{4,5},{5,4},{6,7},{7,6},{8,9},{9,8},{10,11... | collective-permute-start | bytes 3538952 | tf_op jit(solution)/shard_map/ppermute | solution.py:485
  201.1 34.0 %collective-permute-start.34 = (bf16[512,1024]{1,0:T(8,128)(2,1)}, bf16[512,1024]{1,0:T(8,128)(2,1)}, u32[]{:S(2)}, u32[]{:S(2)}) collective-permute-start(bf16[512,1024]{1,0:T(8,128)(2,1)} %constant_dynamic-update-slice_fusion.7.refs_5_), channel_id=1, source_target_pairs={{0,1},{1,0},{2,3},{3,2},{4,5},{5,4},{6,7},{7,6},{8,9},{9,8},{10,11... | collective-permute-start | bytes 3145736 | tf_op jit(solution)/shard_map/ppermute | solution.py:485
  201.1 34.0 %collective-permute-start.36 = (bf16[512,1024]{1,0:T(8,128)(2,1)}, bf16[512,1024]{1,0:T(8,128)(2,1)}, u32[]{:S(2)}, u32[]{:S(2)}) collective-permute-start(bf16[512,1024]{1,0:T(8,128)(2,1)} %collective-permute-done.35.refs_7_), channel_id=1, source_target_pairs={{0,1},{1,0},{2,3},{3,2},{4,5},{5,4},{6,7},{7,6},{8,9},{9,8},{10,11... | collective-permute-start | bytes 3145736 | tf_op jit(solution)/shard_map/ppermute | solution.py:485
  264.8 26.3 %collective-permute-start.39 = (bf16[256,1152]{1,0:T(8,128)(2,1)S(1)}, bf16[256,1152]{1,0:T(8,128)(2,1)S(1)}, u32[]{:S(2)}, u32[]{:S(2)}) collective-permute-start(bf16[256,1152]{1,0:T(8,128)(2,1)S(1)} %get-tuple-element.238), channel_id=1, source_target_pairs={{0,2},{1,3},{2,0},{3,1},{4,6},{5,7},{6,4},{7,5},{8,10},{9,11},{10,... | collective-permute-start | bytes 1769480 | tf_op jit(solution)/shard_map/ppermute | solution.py:485
  349.3 34.6 %collective-permute-start.47 = (bf16[512,1024]{1,0:T(8,128)(2,1)}, bf16[512,1024]{1,0:T(8,128)(2,1)S(1)}, u32[]{:S(2)}, u32[]{:S(2)}) collective-permute-start(bf16[512,1024]{1,0:T(8,128)(2,1)} %get-tuple-element.153), channel_id=1, source_target_pairs={{0,1},{1,0},{2,3},{3,2},{4,5},{5,4},{6,7},{7,6},{8,9},{9,8},{10,11... | collective-permute-start | bytes 3145736 | tf_op jit(solution)/shard_map/ppermute | solution.py:485
  353.1 32.0 %collective-permute-start.50 = (bf16[256,1024]{1,0:T(8,128)(2,1)S(1)}, bf16[256,1024]{1,0:T(8,128)(2,1)S(1)}, u32[]{:S(2)}, u32[]{:S(2)}) collective-permute-start(bf16[256,1024]{1,0:T(8,128)(2,1)S(1)} %get-tuple-element.241), channel_id=1, source_target_pairs={{0,2},{1,3},{2,0},{3,1},{4,6},{5,7},{6,4},{7,5},{8,10},{9,11},{10,... | collective-permute-start | bytes 1572872 | tf_op jit(solution)/shard_map/ppermute | solution.py:485
  355.1 32.0 %collective-permute-start.57 = (bf16[512,896]{1,0:T(8,128)(2,1)S(1)}, bf16[512,896]{1,0:T(8,128)(2,1)S(1)}, u32[]{:S(2)}, u32[]{:S(2)}) collective-permute-start(bf16[512,896]{1,0:T(8,128)(2,1)S(1)} %copy-done.47), channel_id=1, source_target_pairs={{0,4},{4,0},{8,12},{12,8},{16,20},{20,16},{24,28},{28,24},{1,5},{5... | collective-permute-start | bytes 2752520 | tf_op jit(solution)/shard_map/ppermute | solution.py:485
  355.4 27.7 %collective-permute-start.62 = (bf16[4,384,128]{2,1,0:T(8,128)(2,1)S(1)}, bf16[4,384,128]{2,1,0:T(8,128)(2,1)S(1)}, u32[]{:S(2)}, u32[]{:S(2)}) collective-permute-start(bf16[4,384,128]{2,1,0:T(8,128)(2,1)S(1)} %copy-done.54), channel_id=1, source_target_pairs={{0,3},{1,2},{2,1},{3,0},{4,7},{5,6},{6,5},{7,4},{8,11},{9,10},{10,... | collective-permute-start | bytes 1179656 | tf_op jit(solution)/shard_map/ppermute | solution.py:479
  385.1 38.6 %collective-permute-start.49 = (bf16[256,1024]{1,0:T(8,128)(2,1)}, bf16[256,1024]{1,0:T(8,128)(2,1)}, u32[]{:S(2)}, u32[]{:S(2)}) collective-permute-start(bf16[256,1024]{1,0:T(8,128)(2,1)} %get-tuple-element.240), channel_id=1, source_target_pairs={{0,2},{1,3},{2,0},{3,1},{4,6},{5,7},{6,4},{7,5},{8,10},{9,11},{10,... | collective-permute-start | bytes 1572872 | tf_op jit(solution)/shard_map/ppermute | solution.py:485
  386.5 39.5 %collective-permute-start.51 = (bf16[256,1024]{1,0:T(8,128)(2,1)}, bf16[256,1024]{1,0:T(8,128)(2,1)}, u32[]{:S(2)}, u32[]{:S(2)}) collective-permute-start(bf16[256,1024]{1,0:T(8,128)(2,1)} %fusion.3), channel_id=1, source_target_pairs={{0,4},{4,0},{8,12},{12,8},{16,20},{20,16},{24,28},{28,24},{1,5},{5... | collective-permute-start | bytes 1572872 | tf_op jit(solution)/shard_map/ppermute | solution.py:485
  395.1 32.5 %collective-permute-start.58 = (bf16[256,896]{1,0:T(8,128)(2,1)}, bf16[256,896]{1,0:T(8,128)(2,1)}, u32[]{:S(2)}, u32[]{:S(2)}) collective-permute-start(bf16[256,896]{1,0:T(8,128)(2,1)} %slice.133), channel_id=1, source_target_pairs={{0,8},{4,12},{8,0},{12,4},{16,24},{20,28},{24,16},{28,20},{1,9},{5... | collective-permute-start | bytes 1376264 | tf_op jit(solution)/shard_map/ppermute | solution.py:485
  418.9 41.9 %collective-permute-start.63 = (bf16[4,384,128]{2,1,0:T(8,128)(2,1)}, bf16[4,384,128]{2,1,0:T(8,128)(2,1)S(1)}, u32[]{:S(2)}, u32[]{:S(2)}) collective-permute-start(bf16[4,384,128]{2,1,0:T(8,128)(2,1)} %get-tuple-element.176), channel_id=1, source_target_pairs={{0,4},{4,0},{8,12},{12,8},{16,20},{20,16},{24,28},{28,24},{1,5},{5... | collective-permute-start | bytes 1179656 | tf_op jit(solution)/shard_map/ppermute | solution.py:485
  421.2 41.8 %collective-permute-start.69 = (bf16[4,384,128]{2,1,0:T(8,128)(2,1)}, bf16[4,384,128]{2,1,0:T(8,128)(2,1)}, u32[]{:S(2)}, u32[]{:S(2)}) collective-permute-start(bf16[4,384,128]{2,1,0:T(8,128)(2,1)} %get-tuple-element.183), channel_id=1, source_target_pairs={{0,16},{4,20},{8,24},{12,28},{16,0},{20,4},{24,8},{28,12},{1,17},{... | collective-permute-start | bytes 1179656 | tf_op jit(solution)/shard_map/ppermute | solution.py:485
  423.6 42.2 %collective-permute-start.70 = (bf16[4,384,128]{2,1,0:T(8,128)(2,1)}, bf16[4,384,128]{2,1,0:T(8,128)(2,1)}, u32[]{:S(2)}, u32[]{:S(2)}) collective-permute-start(bf16[4,384,128]{2,1,0:T(8,128)(2,1)} %get-tuple-element.184), channel_id=1, source_target_pairs={{0,20},{4,16},{8,28},{12,24},{16,4},{20,0},{24,12},{28,8},{1,21},{... | collective-permute-start | bytes 1179656 | tf_op jit(solution)/shard_map/ppermute | solution.py:485
  426.0 41.1 %collective-permute-start.67 = (bf16[4,384,128]{2,1,0:T(8,128)(2,1)}, bf16[4,384,128]{2,1,0:T(8,128)(2,1)}, u32[]{:S(2)}, u32[]{:S(2)}) collective-permute-start(bf16[4,384,128]{2,1,0:T(8,128)(2,1)} %get-tuple-element.181), channel_id=1, source_target_pairs={{0,8},{4,12},{8,0},{12,4},{16,24},{20,28},{24,16},{28,20},{1,9},{5... | collective-permute-start | bytes 1179656 | tf_op jit(solution)/shard_map/ppermute | solution.py:485
  427.7 31.5 %collective-permute-start.52 = (bf16[128,1024]{1,0:T(8,128)(2,1)S(1)}, bf16[128,1024]{1,0:T(8,128)(2,1)S(1)}, u32[]{:S(2)}, u32[]{:S(2)}) collective-permute-start(bf16[128,1024]{1,0:T(8,128)(2,1)S(1)} %slice.129), channel_id=1, source_target_pairs={{0,8},{4,12},{8,0},{12,4},{16,24},{20,28},{24,16},{28,20},{1,9},{5... | collective-permute-start | bytes 786440 | tf_op jit(solution)/shard_map/ppermute | solution.py:485
  465.8 47.2 %collective-permute-start.59 = (bf16[128,896]{1,0:T(8,128)(2,1)S(1)}, bf16[128,896]{1,0:T(8,128)(2,1)S(1)}, u32[]{:S(2)}, u32[]{:S(2)}) collective-permute-start(bf16[128,896]{1,0:T(8,128)(2,1)S(1)} %get-tuple-element.242), channel_id=1, source_target_pairs={{0,16},{4,20},{8,24},{12,28},{16,0},{20,4},{24,8},{28,12},{1,17},{... | collective-permute-start | bytes 688136 | tf_op jit(solution)/shard_map/ppermute | solution.py:485
  467.1 49.9 %collective-permute-start.53 = (bf16[64,1024]{1,0:T(8,128)(2,1)S(1)}, bf16[64,1024]{1,0:T(8,128)(2,1)S(1)}, u32[]{:S(2)}, u32[]{:S(2)}) collective-permute-start(bf16[64,1024]{1,0:T(8,128)(2,1)S(1)} %get-tuple-element.246), channel_id=1, source_target_pairs={{0,16},{4,20},{8,24},{12,28},{16,0},{20,4},{24,8},{28,12},{1,17},{... | collective-permute-start | bytes 393224 | tf_op jit(solution)/shard_map/ppermute | solution.py:485
  470.1 42.3 %all-to-all-start = ((f32[8,1,128]{2,1,0:T(1,128)}), f32[8,1,128]{2,1,0:T(1,128)S(1)}, u32[]{:S(2)}, u32[]{:S(2)}) async-start(f32[8,1,128]{2,1,0:T(1,128)} %slice_bitcast_fusion), calls=%async_computation | async-start | bytes 8192 | tf_op jit(solution)/shard_map/all_to_all | solution.py:697
  (98 other events, 1446.2 us)

commit v4 on v3

--- a/solution.py
+++ b/solution.py
@@ -157,7 +157,7 @@
 
 
 def post_attn_kernel(experts, shares, *refs):
-    parts, (x, ids, gains, misc, res, router, msg) = split_refs(refs, shares, 7)
+    parts, (x, gains, misc, res, router, msg) = split_refs(refs, shares, 6)
     width = x.shape[1]
     total = x[...].astype(F32)
     for part in parts:
@@ -171,11 +171,7 @@
     probs = exponent / jnp.sum(exponent, axis=-1, keepdims=True)
     router[...] = probs
     msg[:, :width] = h2
-    ids_v = ids[...]
-    member = jnp.zeros(probs.shape, F32)
-    for k in range(ids_v.shape[1]):
-        member = member + jnp.where(ids_v[:, k : k + 1] + experts == lane, 1.0, 0.0)
-    msg[:, width:] = (probs + member).astype(BF)
+    msg[:, width:] = probs.astype(BF)
 
 
 def gate_column(router_cols, expert):
@@ -207,23 +203,24 @@
             out[s] = ins[s][j]
 
 
-def weight_grad_kernel(peers, shares, idx, *refs):
-    ins, outs = split_refs(refs, peers, 3)
-    for m in range(peers):
-        for s in range(shares):
-            e = jnp.bitwise_xor(idx[0], m) * shares + jnp.bitwise_xor(idx[1], s)
-            for k in range(3):
-                outs[k][e] = ins[m][s, k * 128 : (k + 1) * 128, :].astype(F32)
-
-
-def expert_main_kernel(peers, shares, experts, *refs):
-    (idx,), rows_in, grads_in, pieces, back, outs, (wgu, down) = split_refs(
-        refs, 1, shares, shares, peers, shares, 7, 2
-    )
-    rows_out, scaled_out, hid, gpu, hot_out, gate_out, near_out = outs
+def weight_grad_kernel(shares, idx, *refs):
+    first, second, outs = split_refs(refs, shares, len(CHUNKS[1]), 3)
+    for c, chunk in enumerate(CHUNKS):
+        for j, m in enumerate(chunk):
+            for s in range(shares):
+                e = jnp.bitwise_xor(idx[0], m) * shares + jnp.bitwise_xor(idx[1], s)
+                got = first[s].at[j] if c == 0 else second[j].at[s]
+                for k in range(3):
+                    outs[k][e] = got[k * 128 : (k + 1) * 128, :].astype(F32)
+
+
+def expert_pre_kernel(peers, shares, *refs):
+    (idx,), grads_in, pieces, (hot_out, grads_out, raw, wgu, down) = split_refs(
+        refs, 1, shares, peers, 5
+    )
     ff = shares * 128
-    width = grads_in[0].shape[1]
-    span = rows_in[0].shape[0] // peers
+    width = grads_out.shape[1]
+    span = grads_in[0].shape[0] // peers
     block = shares * span
     for m, piece in enumerate(pieces):
         at = pl.ds(pl.multiple_of(jnp.bitwise_xor(idx[0], m) * 128, 128), 128)
@@ -231,42 +228,66 @@
             wgu[at, t * 128 : (t + 1) * 128] = piece[t, 0:128, :]
             wgu[at, ff + t * 128 : ff + (t + 1) * 128] = piece[t, 128:256, :]
     load_down(idx[0], pieces, down, shares)
-    for s in range(shares):
-        near_out[s * span : (s + 1) * span, :] = rows_in[s][0:span, :width]
     expert = idx[0] * shares + idx[1]
     r = lax.broadcasted_iota(jnp.int32, (block, block), 0)
     c = lax.broadcasted_iota(jnp.int32, (block, block), 1)
     lower = jnp.where(r > c, 1.0, 0.0).astype(BF)
     slot = lax.broadcasted_iota(jnp.int32, (block, CAP), 1)
+
+    def body(step, carry):
+        grads = []
+        for half in range(2):
+            k = step * 2 + half
+            at = pl.ds(pl.multiple_of(k * span, span), span)
+            tokens = jnp.concatenate([ref[at, :] for ref in grads_in], 0)
+            member = jnp.where(slot == expert, tokens[:, width:].astype(F32), 0.0)
+            rank = jnp.dot(lower, member.astype(BF), preferred_element_type=F32)
+            rank = jnp.sum(jnp.where(slot == expert, rank, 0.0), -1, keepdims=True)
+            is_member = jnp.sum(member, axis=-1, keepdims=True) > 0.0
+            place = jnp.where(is_member, rank, -1.0)
+            hot = jnp.where(place == slot.astype(F32), 1.0, 0.0).astype(BF)
+            hot_out[pl.ds(pl.multiple_of(k * block, block), block), :] = hot
+            grads.append(mm(hot, tokens[:, :width], 0, 0).astype(BF))
+        grad_rows = jnp.concatenate(grads, 0)
+        at = pl.ds(pl.multiple_of(step * 2 * CAP, 2 * CAP), 2 * CAP)
+        grads_out[at, :] = grad_rows
+        raw[at, :] = mm(grad_rows, down[...], 1, 1)
+        return carry
+
+    lax.fori_loop(0, peers // 2, body, 0)
+
+
+def expert_main_kernel(peers, shares, *refs):
+    (idx,), rows_in, (hot_in, raw_in, wgu), back, outs = split_refs(
+        refs, 1, shares, 3, shares, 5
+    )
+    rows_out, hid, gpu, gate_out, near_out = outs
+    ff = raw_in.shape[1]
+    width = rows_out.shape[1]
+    span = rows_in[0].shape[0] // peers
+    block = shares * span
+    for s in range(shares):
+        near_out[s * span : (s + 1) * span, :] = rows_in[s][0:span, :width]
+    expert = idx[0] * shares + idx[1]
     lane = lax.broadcasted_iota(jnp.int32, (2 * CAP, LANES), 1)
 
     def body(step, carry):
-        slots, grads = [], []
+        slots, hots = [], []
         for half in range(2):
             k = step * 2 + half
             at = pl.ds(pl.multiple_of(k * span, span), span)
             tokens = jnp.concatenate([ref[at, :] for ref in rows_in], 0)
-            cotangents = jnp.concatenate([ref[at, :] for ref in grads_in], 0)
-            tail = tokens[:, width:].astype(F32)
-            member = jnp.where(slot == expert + experts, tail, 0.0)
-            rank = jnp.dot(lower, member.astype(BF), preferred_element_type=F32)
-            rank = jnp.sum(jnp.where(slot == expert + experts, rank, 0.0), -1, keepdims=True)
-            is_member = jnp.sum(member, axis=-1, keepdims=True) > 0.0
-            place = jnp.where(is_member, rank, -1.0)
-            hot = jnp.where(place == slot.astype(F32), 1.0, 0.0).astype(BF)
-            hot_out[pl.ds(pl.multiple_of(k * block, block), block), :] = hot
+            hot = hot_in[pl.ds(pl.multiple_of(k * block, block), block), :]
+            hots.append(hot)
             slots.append(mm(hot, tokens, 0, 0).astype(BF))
-            grads.append(mm(hot, cotangents, 0, 0).astype(BF))
         rows = jnp.concatenate(slots, 0)
-        grad_rows = jnp.concatenate(grads, 0)
         at = pl.ds(pl.multiple_of(step * 2 * CAP, 2 * CAP), 2 * CAP)
         gate = gate_column(rows[:, width:], expert)
         rows = rows[:, :width]
         rows_out[at, :] = rows
-        scaled_out[at, :] = (grad_rows.astype(F32) * gate).astype(BF)
         gate_out[at, :] = jnp.broadcast_to(gate, (2 * CAP, LANES))
         pre = jnp.dot(rows, wgu[...], preferred_element_type=F32)
-        raw = mm(grad_rows, down[...], 1, 1)
+        raw = raw_in[at, :]
         gate_pre = pre[:, :ff]
         up_pre = pre[:, ff:]
         sig = jax.nn.sigmoid(gate_pre)
@@ -281,9 +302,8 @@
         gpu[at, :] = both
         row_grad = mm(both, wgu[...], 1, 1).astype(BF)
         tail_grad = jnp.where(lane == expert, gate_grad, 0.0).astype(BF)
-        for half in range(2):
+        for half, hot in enumerate(hots):
             k = step * 2 + half
-            hot = hot_out[pl.ds(pl.multiple_of(k * block, block), block), :]
             cut = slice(half * CAP, (half + 1) * CAP)
             to = pl.ds(pl.multiple_of(k * span, span), span)
             spread = jnp.dot(hot, row_grad[cut, :], preferred_element_type=F32).astype(BF)
@@ -297,13 +317,13 @@
 
 
 def expert_rest_kernel(peers, shares, step, *refs):
-    (idx,), pieces, ins, y_out, grad_out, (down,) = split_refs(
-        refs, 1, peers, 6, shares, len(CHUNKS) * shares, 1
-    )
-    rows, scaled, hid, gpu, hot_in, gate_in = ins
+    (idx,), ins, y_out, first_out, second_out, (scaled,) = split_refs(
+        refs, 1, 7, shares, len(CHUNKS[0]), shares, 1
+    )
+    rows, hid, gpu, gate_in, hot_in, grads, down = ins
     span = y_out[0].shape[0] // peers
     block = shares * span
-    load_down(idx[0], pieces, down, shares)
+    scaled[...] = (grads[...].astype(F32) * gate_in[:, 0:1]).astype(BF)
 
     def out_rows(k, carry):
         at = pl.ds(pl.multiple_of(k * CAP, CAP), CAP)
@@ -318,25 +338,38 @@
 
     lax.fori_loop(0, peers, out_rows, 0)
 
-    for c in range(len(CHUNKS)):
-        outs = grad_out[c * shares : (c + 1) * shares]
-
-        def body(pair, carry):
-            q = jnp.bitwise_xor(pair * 2 + c, idx[0] // 2)
-            at = pl.ds(pl.multiple_of(q * step, step), step)
-            both = mm(rows[:, at], gpu[...], 0, 0).astype(BF)
-            down_g = mm(hid[...], scaled[:, at], 0, 0).astype(BF)
-            for s in range(2):
-                j = pair * 2 + jnp.bitwise_xor(idx[0] % 2, s)
-                r = slice(s * 128, (s + 1) * 128)
-                for t in range(shares):
-                    out = outs[t]
-                    out[j, 0:128, :] = both[r, t * 128 : (t + 1) * 128]
-                    out[j, 128:256, :] = both[r, (shares + t) * 128 : (shares + t + 1) * 128]
-                    out[j, 256:384, :] = down_g[t * 128 : (t + 1) * 128, r]
-            return carry
-
-        lax.fori_loop(0, 2, body, 0)
+    def model_rows(p):
+        q = jnp.bitwise_xor(p, idx[0] // 2)
+        at = pl.ds(pl.multiple_of(q * step, step), step)
+        both = mm(rows[:, at], gpu[...], 0, 0).astype(BF)
+        return both, mm(hid[...], scaled[:, at], 0, 0).astype(BF)
+
+    def store(to, both, down_g, s, t):
+        r = slice(s * 128, (s + 1) * 128)
+        to[0:128, :] = both[r, t * 128 : (t + 1) * 128]
+        to[128:256, :] = both[r, (shares + t) * 128 : (shares + t + 1) * 128]
+        to[256:384, :] = down_g[t * 128 : (t + 1) * 128, r]
+
+    low = idx[0] % 2
+    for pair in range(2):
+        both, down_g = model_rows(CHUNKS[0][pair * 2] // 2)
+        for s in range(2):
+            for odd in range(2):
+
+                @pl.when(jnp.bitwise_xor(low, s) == odd)
+                def _():
+                    for t in range(shares):
+                        store(first_out[pair * 2 + odd].at[t], both, down_g, s, t)
+
+    def body(pair, carry):
+        both, down_g = model_rows(pair * 2 + 1)
+        for s in range(2):
+            j = pair * 2 + jnp.bitwise_xor(low, s)
+            for t in range(shares):
+                store(second_out[t].at[j], both, down_g, s, t)
+        return carry
+
+    lax.fori_loop(0, 2, body, 0)
 
 
 def hi_lo_rows(row, count):
@@ -374,7 +407,6 @@
     wall, qkv, att, logs, cos, sin, seg_c, seg_r, hid, rows2, x = ins
     length, width = x.shape
     own = length // shares
-    span = msgs[0].shape[0]
     qk_w = (n_q + n_kv) * HD
     all_w = (n_q + 2 * n_kv) * HD
     o_at = all_w + n_q * HD
@@ -421,7 +453,14 @@
     sums[:, all_w:o_at] = mm(resid[...], att[...], 0, 0)
     place = lax.broadcasted_iota(jnp.int32, (LANES, width), 0)
     gain_hi = gain_moe.astype(BF).astype(F32)
-    rows = jnp.where(place == 32, gain_hi, jnp.where(place == 33, gain_moe - gain_hi, 0.0))
+    partial[...] = mm(low, wall[:, :all_w], 1, 1)
+    normed, _ = norm_parts(x[...].astype(F32))
+    gain_attn = jnp.sum(partial[...] * normed, axis=0, keepdims=True)
+    attn_hi = gain_attn.astype(BF).astype(F32)
+    rows = jnp.zeros((LANES, width), F32)
+    gain_rows = (gain_hi, gain_moe - gain_hi, attn_hi, gain_attn - attn_hi)
+    for at, row in enumerate(gain_rows):
+        rows = jnp.where(place == 32 + at, row, rows)
     sums[:, o_at:] = mm(rows2[...], logit, 0, 0) + jnp.transpose(rows)
     depth = width // peers
     for k, m in enumerate(visit_order(TOKEN_BITS)):
@@ -429,30 +468,21 @@
         out = g_out[k // (peers // 2)]
         k = k % (peers // 2)
         out[k * depth : (k + 1) * depth, :] = sums[pl.ds(at, depth), :].astype(BF)
-    partial[...] = mm(low, wall[:, :all_w], 1, 1)
-    normed, _ = norm_parts(x[...].astype(F32))
-    extra = hi_lo_rows(jnp.sum(partial[...] * normed, axis=0, keepdims=True), span - own)
-    scatter_rows(partial, [out.at[0:own, :] for out in msg2], idx[1])
-    for out in msg2:
-        out[own:, :] = extra
+    scatter_rows(partial, msg2, idx[1])
 
 
 def input_grad_kernel(shares, *refs):
-    msgs, (x, gains, rgrad, out, gain_out) = split_refs(refs, shares, 5)
-    own, width = x.shape
-    upstream = jnp.zeros((own, width), F32)
-    gain_sum = jnp.zeros((1, width), F32)
-    for msg in msgs:
-        upstream = upstream + msg[0:own, :].astype(F32)
-        gain_sum = gain_sum + jnp.sum(msg[own:, :].astype(F32), axis=0, keepdims=True)
+    parts, (x, gains, rgrad, out) = split_refs(refs, shares, 4)
+    upstream = parts[0][...].astype(F32)
+    for part in parts[1:]:
+        upstream = upstream + part[...].astype(F32)
     normed, inverse = norm_parts(x[...].astype(F32))
     through = norm_backward(upstream, normed, inverse, gains[0:1, :])
     out[...] = (rgrad[...] + through).astype(BF)
-    gain_out[...] = jnp.broadcast_to(gain_sum, gain_out.shape)
 
 
 def attn_grad_kernel(terms, widths, *refs):
-    ins, (query, key, value, output, router, gain) = split_refs(refs, terms, 6)
+    ins, (query, key, value, output, router, gain, gain_part) = split_refs(refs, terms, 7)
     q_w, kv_w, experts = widths
     total = ins[0][...].astype(F32)
     for ref in ins[1:]:
@@ -466,6 +496,8 @@
     router[...] = tail[:, :experts]
     tail_t = jnp.transpose(tail)
     gain[...] = tail_t[experts : experts + 1, :] + tail_t[experts + 1 : experts + 2, :]
+    part = tail_t[experts + 2 : experts + 3, :] + tail_t[experts + 3 : experts + 4, :]
+    gain_part[...] = jnp.broadcast_to(part, gain_part.shape)
 
 
 def layer_out_kernel(first, second, res, out):
@@ -519,15 +551,17 @@
     return reduce_dp(parts[0][:half] + own[:half], odd, far_even)
 
 
+def regroup(parts):
+    shape = parts[0].shape
+    return call(
+        functools.partial(regroup_kernel, len(parts)), [((len(parts),) + shape[1:], BF)] * shape[0]
+    )(*parts)
+
+
 def move_chunks(parts):
     pieces = {}
     for c, chunk in enumerate(CHUNKS):
-        shape = parts[c][0].shape
-        groups = call(
-            functools.partial(regroup_kernel, len(parts[c])),
-            [((len(parts[c]),) + shape[1:], BF)] * len(chunk),
-        )(*parts[c])
-        for m, group in zip(chunk, groups):
+        for m, group in zip(chunk, regroup(parts[c])):
             pieces[m] = permute(group, "dp", m) if m else group
     return [pieces[m] for m in sorted(pieces)]
 
@@ -554,7 +588,6 @@
     own, width = layer_input.shape
     experts = w_gate.shape[0]
     length = seq_ids.shape[1]
-    depth = width // peers
     q_w, kv_w = w_query.shape[1], w_key.shape[1]
     dims = (q_w // HD, kv_w // HD)
     all_w = q_w + 2 * kv_w
@@ -587,7 +620,10 @@
     pieces = move_chunks(
         [swap(weight_parts[c * shares : (c + 1) * shares], "tensor") for c in range(len(CHUNKS))],
     )
-    grads_in = gather_all(out_grad)
+    ids_own = lax.dynamic_slice_in_dim(expert_ids, lax.axis_index("tensor") * own, own, 0)
+    lanes = jnp.arange(LANES, dtype=jnp.int32)
+    member = jnp.sum((ids_own[:, :, None] == lanes).astype(F32), axis=1).astype(BF)
+    grads_in = gather_all(jnp.concatenate([out_grad, member], axis=1))
 
     segment = seq_ids[0]
     before = jnp.sum((segment[None, :] < segment[:, None]).astype(jnp.int32), axis=1)
@@ -618,46 +654,53 @@
         smem=1,
     )(idx, *x_in, *packs, cosine, sine, seg_c, seg_r)
 
-    ids_own = lax.dynamic_slice_in_dim(expert_ids, lax.axis_index("tensor") * own, own, 0)
     parts = swap(parts, "tensor")
-    ids_own = lax.dynamic_slice_in_dim(expert_ids, lax.axis_index("tensor") * own, own, 0)
     res, router, msg = call(
         functools.partial(post_attn_kernel, experts, shares),
         [((own, width), F32), ((own, LANES), F32), ((own, wide), BF)],
-    )(*parts, layer_input, ids_own, gains, misc)
+    )(*parts, layer_input, gains, misc)
     rows_in = gather_all(msg)
 
     ff = w_gate.shape[2] * shares
+    hots, grad_rows, raw, wgu, down = call(
+        functools.partial(expert_pre_kernel, peers, shares),
+        [
+            ((peers * length, CAP), BF),
+            ((slots, width), BF),
+            ((slots, ff), F32),
+            ((width, 2 * ff), BF),
+            ((ff, width), BF),
+        ],
+        smem=1,
+    )(idx, *grads_in, *pieces)
     outs = call(
-        functools.partial(expert_main_kernel, peers, shares, experts),
+        functools.partial(expert_main_kernel, peers, shares),
         [((peers * own, wide), BF)] * shares
         + [
             ((slots, width), BF),
-            ((slots, width), BF),
             ((slots, ff), BF),
             ((slots, 2 * ff), BF),
-            ((peers * length, CAP), BF),
             ((slots, LANES), F32),
             ((length, width), BF),
         ],
-        scratch=[((width, 2 * ff), BF), ((ff, width), BF)],
         smem=1,
-    )(idx, *rows_in, *grads_in, *pieces)
+    )(idx, *rows_in, hots, raw, wgu)
     row_back, saved, rows_near = outs[:shares], outs[shares:-1], outs[-1]
     back = reduce_all(row_back)
     rest = call(
         functools.partial(expert_rest_kernel, peers, shares, 256),
         [((peers * own, width), BF)] * shares
-        + [((peers // 2, 384, LANES), BF)] * (2 * shares),
-        scratch=[((ff, width), BF)],
+        + [((shares, 384, LANES), BF)] * len(CHUNKS[0])
+        + [((len(CHUNKS[1]), 384, LANES), BF)] * shares,
+        scratch=[((slots, width), BF)],
         smem=1,
-    )(idx, *pieces, *saved)
-    y_parts, grad_parts = rest[:shares], rest[shares:]
-    grad_parts = [
-        swap(grad_parts[c * shares : (c + 1) * shares], "tensor")
-        for c in range(len(CHUNKS))
-    ]
-    grad_parts = move_chunks(grad_parts)
+    )(idx, *saved, hots, grad_rows, down)
+    y_parts, first, second = rest[:shares], rest[shares : shares + 4], rest[shares + 4 :]
+    first = [permute(v, "dp", m) if m else v for m, v in zip(CHUNKS[0], first)]
+    first = swap(regroup(first), "tensor")
+    second = regroup(swap(second, "tensor"))
+    second = [permute(v, "dp", m) for m, v in zip(CHUNKS[1], second)]
+    mixed = reduce_all(y_parts)
     rgrad, msg = call(
         moe_back_kernel, [((own, width), F32), ((own + 16, wide), BF)]
     )(*back, router, res, gains, misc, out_grad)
@@ -665,19 +708,17 @@
 
     outs = call(
         functools.partial(attn_bwd_kernel, peers, shares, dims),
-        [((width // 2, pack_w), BF)] * 2 + [((own + 16, width), BF)] * shares,
+        [((width // 2, pack_w), BF)] * 2 + [((own, width), BF)] * shares,
         scratch=[((width, pack_w), F32), ((length, width), F32), ((length, width), BF)],
         smem=1,
     )(idx, *msgs, wall, qkv, att, logs, cosine, sine, seg_c, seg_r, hid, rows_near, x_all)
     msg2 = outs[2:]
-    y_parts, msg2 = lax.optimization_barrier((y_parts, msg2))
-    mixed = reduce_all(y_parts)
     terms = reduce_dp(outs[0], outs[1])
     if rep > 1:
         total = terms[0].astype(F32) + terms[1].astype(F32)
         terms = (lax.psum_scatter(total, "rep", scatter_dimension=0, tiled=True),)
     rows_own = terms[0].shape[0]
-    q_grad, k_grad, v_grad, o_grad, router_grad, gain_moe_grad = call(
+    q_grad, k_grad, v_grad, o_grad, router_grad, gain_moe_grad, gain_part = call(
         functools.partial(attn_grad_kernel, len(terms), (q_w, kv_w, experts)),
         [
             ((rows_own, q_w), F32),
@@ -686,26 +727,21 @@
             ((q_w, rows_own), F32),
             ((rows_own, experts), F32),
             ((1, rows_own), F32),
+            ((8, rows_own), F32),
         ],
     )(*terms)
+    gain_attn_grad = sum(swap([gain_part] * shares, "tensor"))[0]
 
     msg2 = swap(msg2, "tensor")
-    input_grad, gain_rows = call(
-        functools.partial(input_grad_kernel, shares), [((own, width), BF), ((8, width), F32)]
+    (input_grad,) = call(
+        functools.partial(input_grad_kernel, shares), [((own, width), BF)]
     )(*msg2, layer_input, gains, rgrad)
-    gain_cut = gain_rows[:1].reshape(peers, depth)
-    gain_cut = lax.all_to_all(gain_cut, "dp", split_axis=0, concat_axis=0, tiled=True)
-    gain_attn_grad = jnp.sum(gain_cut, axis=0)
-    if rep > 1:
-        gain_attn_grad = lax.psum_scatter(gain_attn_grad, "rep", scatter_dimension=0, tiled=True)
 
     (layer_output,) = call(layer_out_kernel, [((own, width), BF)])(*mixed, res)
 
     gate_grad, up_grad, down_grad = call(
-        functools.partial(weight_grad_kernel, peers, shares),
-        [((experts, 128, LANES), F32)] * 3,
-        smem=1,
-    )(idx, *grad_parts)
+        functools.partial(weight_grad_kernel, shares), [((experts, 128, LANES), F32)] * 3, smem=1
+    )(idx, *first, *second)
     if rep > 1:
         gate_grad = lax.psum_scatter(gate_grad, "rep", scatter_dimension=1, tiled=True)
         up_grad = lax.psum_scatter(up_grad, "rep", scatter_dimension=1, tiled=True)

time: 521 us -> 508 us (0.975)
  waiting for transfers between devices: 318 us -> 305 us
  local copies, waits for them, and re-layouts: 26.2 us -> 18 us
    ppermute x49, waiting for transfers between devices: 190 us -> 227 us  [permute(): return lax.ppermute(value, axis, [(i, i ^ bit) for i in range(count)])]
    ppermute x24 -> x27, waiting for transfers between devices: 110 us -> 78.2 us  [swap(): lax.ppermute(values[m], axis, [(i, i ^ m) for i in range(len(values))])]
    all_to_all x1 -> x0, waiting for transfers between devices: 18 us -> none  [per_device(): lax.all_to_all(gain_cut, 'dp', split_axis=0, concat_axis=0, tiled=True)]
    ppermute x24 -> x27, starting transfers between devices: 15.1 us -> 21.6 us  [swap(): lax.ppermute(values[m], axis, [(i, i ^ m) for i in range(len(values))])]
    unnamed x124 -> x110, local copies, waits for them, and re-layouts: 16.8 us -> 11.1 us
    pallas_call x15 -> x16, Pallas kernels: 79.9 us -> 83.9 us  [run(): pl.pallas_call(kernel, out_shape=[jax.ShapeDtypeStruct(s, d) for s, d in...]
  transfers between devices with their start and end apart: 74 -> 76, of which waited for: 36 -> 34; matrix products, arithmetic and copies ran while one was open for 5% -> 4% of each run, Pallas kernels for 8% -> 13%
where the time goes in v4:
time: 508 us; the launch traced here: 507 us
  waiting for transfers between devices  305 us (60%)
  starting transfers between devices  86.3 us (17%)
  Pallas kernels  83.9 us (17%)
  local copies, waits for them, and re-layouts  18 us (4%)
  other arithmetic  12.2 us (2%)
    ppermute x49, waiting for transfers between devices, permute(): return lax.ppermute(value, axis, [(i, i ^ bit) for i in range(count)])  227 us
    pallas_call x16, Pallas kernels, run(): pl.pallas_call(kernel, out_shape=[jax.ShapeDtypeStruct(s, d) for s, d in...  83.9 us
    ppermute x27, waiting for transfers between devices, swap(): lax.ppermute(values[m], axis, [(i, i ^ m) for i in range(len(values))])  78.2 us
    ppermute x49, starting transfers between devices, permute(): return lax.ppermute(value, axis, [(i, i ^ bit) for i in range(count)])  64.7 us
    ppermute x27, starting transfers between devices, swap(): lax.ppermute(values[m], axis, [(i, i ^ m) for i in range(len(values))])  21.6 us
    unnamed x110, local copies, waits for them, and re-layouts  11.1 us
  transfers between devices with their start and end apart: 76, of which 34 were waited for; matrix products, arithmetic and copies ran while one was open for 4% of the time, Pallas kernels for 13%

profile of v4, /device:TPU:0, one launch (start us, length us, event | category | flops | bytes accessed | tf_op | source)
XLA Modules:
  0.0 506.8 jit_solution(5431481089313443756)
XLA Ops:
  18.4 10.3 %collective-permute-done.3 = bf16[128,512]{1,0:T(8,128)(2,1)S(1)} collective-permute-done((bf16[128,512]{1,0:T(8,128)(2,1)S(1)}, bf16[128,512]{1,0:T(8,128)(2,1)S(1)}, u32[]{:S(2)}, u32[]{:S(2)}) %collective-permute-start.3) | collective-permute-done | bytes 131104 | tf_op jit(solution)/shard_map/ppermute | solution.py:517
  36.0 4.9 collective-permute-done.4
  42.7 4.5 collective-permute-done.19
  49.2 6.3 %collective-permute-done.8.refs_8_ = bf16[512,384]{1,0:T(8,128)(2,1)S(1)} collective-permute-done((bf16[512,384]{1,0:T(8,128)(2,1)S(1)}, bf16[512,384]{1,0:T(8,128)(2,1)S(1)}, u32[]{:S(2)}, u32[]{:S(2)}) %collective-permute-start.8) | collective-permute-done | bytes 393248 | tf_op jit(solution)/shard_map/ppermute | solution.py:517
  56.2 5.3 %shard_map.229 = (bf16[64,1024]{1,0:T(8,128)(2,1)}, bf16[64,1024]{1,0:T(8,128)(2,1)}, bf16[64,1024]{1,0:T(8,128)(2,1)}, bf16[64,1024]{1,0:T(8,128)(2,1)}, bf16[1...) custom-call(s32[2]{0:T(128)} %pad_add_fusion.refs_0_.idx, ...), custom_call_target="tpu_custom_call" | custom-call | tf_op jit(solution)/shard_map/pallas_call | solution.py:37
  63.5 4.8 collective-permute-done.10.refs_2_
  74.6 8.8 %collective-permute-done.12 = bf16[64,1152]{1,0:T(8,128)(2,1)S(1)} collective-permute-done((bf16[64,1152]{1,0:T(8,128)(2,1)}, bf16[64,1152]{1,0:T(8,128)(2,1)S(1)}, u32[]{:S(2)}, u32[]{:S(2)}) %collective-permute-start.12) | collective-permute-done | bytes 147488 | tf_op jit(solution)/shard_map/ppermute | solution.py:517
  85.1 3.7 shard_map.231
  94.4 13.4 %collective-permute-done.14 = bf16[256,1152]{1,0:T(8,128)(2,1)S(1)} collective-permute-done((bf16[256,1152]{1,0:T(8,128)(2,1)S(1)}, bf16[256,1152]{1,0:T(8,128)(2,1)S(1)}, u32[]{:S(2)}, u32[]{:S(2)}) %collective-permute-start.14) | collective-permute-done | bytes 589856 | tf_op jit(solution)/shard_map/ppermute | solution.py:517
  114.6 55.9 %collective-permute-done.29.refs_2_ = bf16[4,384,128]{2,1,0:T(8,128)(2,1)} collective-permute-done((bf16[4,384,128]{2,1,0:T(8,128)(2,1)}, bf16[4,384,128]{2,1,0:T(8,128)(2,1)}, u32[]{:S(2)}, u32[]{:S(2)}) %collective-permute-start.29) | collective-permute-done | bytes 393248 | tf_op jit(solution)/shard_map/ppermute | solution.py:511
  182.1 15.0 %collective-permute-done.33.refs_9_ = bf16[4,384,128]{2,1,0:T(8,128)(2,1)} collective-permute-done((bf16[4,384,128]{2,1,0:T(8,128)(2,1)}, bf16[4,384,128]{2,1,0:T(8,128)(2,1)}, u32[]{:S(2)}, u32[]{:S(2)}) %collective-permute-start.33) | collective-permute-done | bytes 393248 | tf_op jit(solution)/shard_map/ppermute | solution.py:517
  197.1 7.1 %collective-permute-done.34.refs_10_ = bf16[4,384,128]{2,1,0:T(8,128)(2,1)} collective-permute-done((bf16[4,384,128]{2,1,0:T(8,128)(2,1)}, bf16[4,384,128]{2,1,0:T(8,128)(2,1)}, u32[]{:S(2)}, u32[]{:S(2)}) %collective-permute-start.34) | collective-permute-done | bytes 393248 | tf_op jit(solution)/shard_map/ppermute | solution.py:517
  207.7 7.7 %collective-permute-done.32.refs_8_ = bf16[4,384,128]{2,1,0:T(8,128)(2,1)S(1)} collective-permute-done((bf16[4,384,128]{2,1,0:T(8,128)(2,1)}, bf16[4,384,128]{2,1,0:T(8,128)(2,1)S(1)}, u32[]{:S(2)}, u32[]{:S(2)}) %collective-permute-start.32) | collective-permute-done | bytes 393248 | tf_op jit(solution)/shard_map/ppermute | solution.py:517
  216.9 11.5 %collective-permute-done.35.refs_11_ = bf16[4,384,128]{2,1,0:T(8,128)(2,1)S(1)} collective-permute-done((bf16[4,384,128]{2,1,0:T(8,128)(2,1)}, bf16[4,384,128]{2,1,0:T(8,128)(2,1)S(1)}, u32[]{:S(2)}, u32[]{:S(2)}) %collective-permute-start.35) | collective-permute-done | bytes 393248 | tf_op jit(solution)/shard_map/ppermute | solution.py:517
  230.9 10.7 %collective-permute-done.36.refs_12_ = bf16[4,384,128]{2,1,0:T(8,128)(2,1)S(1)} collective-permute-done((bf16[4,384,128]{2,1,0:T(8,128)(2,1)}, bf16[4,384,128]{2,1,0:T(8,128)(2,1)S(1)}, u32[]{:S(2)}, u32[]{:S(2)}) %collective-permute-start.36) | collective-permute-done | bytes 393248 | tf_op jit(solution)/shard_map/ppermute | solution.py:517
  243.8 11.2 %shard_map.234 = (bf16[2048,128]{1,0:T(8,128)(2,1)}, bf16[1024,1024]{1,0:T(8,128)(2,1)}, f32[1024,512]{1,0:T(8,128)}, bf16[1024,1024]{1,0:T(8,128)(2,1)}, bf16[512,1024]{1,0:T(8,128)(2,1)}) custom-call(s32[2]{0:T(128)} %pad_add_fusion.refs_0_.idx, bf16[512,1152]{1,0:T(8,128)(2,1)} %copy-done.2, bf16[512,1152]{1,0:T(8,128)(2,1)} %copy-done.11, ...), custom_call_target="tpu_custom_call" | custom-call | tf_op jit(solution)/shard_map/pallas_call | solution.py:37
  255.0 16.1 %shard_map.235 = (bf16[512,1152]{1,0:T(8,128)(2,1)}, bf16[512,1152]{1,0:T(8,128)(2,1)}, bf16[512,1152]{1,0:T(8,128)(2,1)}, bf16[512,1152]{1,0:T(8,128)(2,1)}, bf...) custom-call(s32[2]{0:T(128)} %pad_add_fusion.refs_0_.idx, ...), custom_call_target="tpu_custom_call" | custom-call | tf_op jit(solution)/shard_map/pallas_call | solution.py:37
  277.8 14.1 %collective-permute-done.47 = bf16[256,1152]{1,0:T(8,128)(2,1)S(1)} collective-permute-done((bf16[256,1152]{1,0:T(8,128)(2,1)S(1)}, bf16[256,1152]{1,0:T(8,128)(2,1)S(1)}, u32[]{:S(2)}, u32[]{:S(2)}) %collective-permute-start.47) | collective-permute-done | bytes 589856 | tf_op jit(solution)/shard_map/ppermute | solution.py:517
  294.4 14.8 %shard_map.236 = (bf16[512,1024]{1,0:T(8,128)(2,1)}, bf16[512,1024]{1,0:T(8,128)(2,1)}, bf16[512,1024]{1,0:T(8,128)(2,1)}, bf16[512,1024]{1,0:T(8,128)(2,1)}, bf...) custom-call(s32[2]{0:T(128)} %pad_add_fusion.refs_0_.idx, ...), custom_call_target="tpu_custom_call" | custom-call | tf_op jit(solution)/shard_map/pallas_call | solution.py:37
  310.5 12.5 %collective-permute-start.49 = (bf16[128,1152]{1,0:T(8,128)(2,1)S(1)}, bf16[128,1152]{1,0:T(8,128)(2,1)S(1)}, u32[]{:S(2)}, u32[]{:S(2)}) collective-permute-start(bf16[128,1152]{1,0:T(8,128)(2,1)S(1)} %slice.129), channel_id=1, source_target_pairs={{0,8},{4,12},{8,0},{12,4},{16,24},{20,28},{24,16},{28,20},{1,9},{5... | collective-permute-start | bytes 884744 | tf_op jit(solution)/shard_map/ppermute | solution.py:517
  326.1 4.5 collective-permute-done.49
  333.3 7.8 %collective-permute-done.50.refs_1_ = bf16[64,1152]{1,0:T(8,128)(2,1)S(1)} collective-permute-done((bf16[64,1152]{1,0:T(8,128)(2,1)S(1)}, bf16[64,1152]{1,0:T(8,128)(2,1)S(1)}, u32[]{:S(2)}, u32[]{:S(2)}) %collective-permute-start.50) | collective-permute-done | bytes 147488 | tf_op jit(solution)/shard_map/ppermute | solution.py:517
  346.3 4.4 collective-permute-done.53.refs_4_
  356.6 7.2 %shard_map.239 = (bf16[512,896]{1,0:T(8,128)(2,1)}, bf16[512,896]{1,0:T(8,128)(2,1)}, bf16[64,1024]{1,0:T(8,128)(2,1)}, bf16[64,1024]{1,0:T(8,128)(2,1)}, bf16[6...) custom-call(s32[2]{0:T(128)} %pad_add_fusion.refs_0_.idx, bf16[80,1152]{1,0:T(8,128)(2,1)} %get-tuple-element.137.refs_1_, ...), custom_call_target="tpu_custom_call" | custom-call | tf_op jit(solution)/shard_map/pallas_call | solution.py:37
  368.6 36.4 %collective-permute-done.63.refs_1_ = bf16[4,384,128]{2,1,0:T(8,128)(2,1)S(1)} collective-permute-done((bf16[4,384,128]{2,1,0:T(8,128)(2,1)S(1)}, bf16[4,384,128]{2,1,0:T(8,128)(2,1)S(1)}, u32[]{:S(2)}, u32[]{:S(2)}) %collective-permute-start.63) | collective-permute-done | bytes 393248 | tf_op jit(solution)/shard_map/ppermute | solution.py:517
  411.4 12.3 %collective-permute-done.65.refs_3_ = bf16[4,384,128]{2,1,0:T(8,128)(2,1)S(1)} collective-permute-done((bf16[4,384,128]{2,1,0:T(8,128)(2,1)S(1)}, bf16[4,384,128]{2,1,0:T(8,128)(2,1)S(1)}, u32[]{:S(2)}, u32[]{:S(2)}) %collective-permute-start.65) | collective-permute-done | bytes 393248 | tf_op jit(solution)/shard_map/ppermute | solution.py:517
  427.0 3.2 collective-permute-start.67
  443.3 5.0 collective-permute-done.68.refs_3_
  451.9 5.4 %collective-permute-done.73.refs_5_ = bf16[4,384,128]{2,1,0:T(8,128)(2,1)S(1)} collective-permute-done((bf16[4,384,128]{2,1,0:T(8,128)(2,1)}, bf16[4,384,128]{2,1,0:T(8,128)(2,1)S(1)}, u32[]{:S(2)}, u32[]{:S(2)}) %collective-permute-start.73) | collective-permute-done | bytes 393248 | tf_op jit(solution)/shard_map/ppermute | solution.py:517
  457.3 10.9 %collective-permute-done.74.refs_6_ = bf16[4,384,128]{2,1,0:T(8,128)(2,1)S(1)} collective-permute-done((bf16[4,384,128]{2,1,0:T(8,128)(2,1)S(1)}, bf16[4,384,128]{2,1,0:T(8,128)(2,1)S(1)}, u32[]{:S(2)}, u32[]{:S(2)}) %collective-permute-start.74) | collective-permute-done | bytes 393248 | tf_op jit(solution)/shard_map/ppermute | solution.py:517
  470.9 19.6 %collective-permute-done.59.refs_1_ = bf16[128,896]{1,0:T(8,128)(2,1)S(1)} collective-permute-done((bf16[128,896]{1,0:T(8,128)(2,1)S(1)}, bf16[128,896]{1,0:T(8,128)(2,1)S(1)}, u32[]{:S(2)}, u32[]{:S(2)}) %collective-permute-start.59) | collective-permute-done | bytes 229408 | tf_op jit(solution)/shard_map/ppermute | solution.py:517
  496.0 4.9 shard_map.244
  (289 shorter events, 145.4 us)
Async XLA Ops:
  0.7 46.6 %collective-permute-start.2 = (bf16[64,1024]{1,0:T(8,128)(2,1)}, bf16[64,1024]{1,0:T(8,128)(2,1)S(1)}, u32[]{:S(2)}, u32[]{:S(2)}) collective-permute-start(bf16[64,1024]{1,0:T(8,128)(2,1)} %refs_4_.3), channel_id=1, source_target_pairs={{0,3},{1,2},{2,1},{3,0},{4,7},{5,6},{6,5},{7,4},{8,11},{9,10},{10,... | collective-permute-start | bytes 393224 | tf_op jit(solution)/shard_map/ppermute | solution.py:511
  3.2 46.0 %collective-permute-start.1 = (bf16[64,1024]{1,0:T(8,128)(2,1)}, bf16[64,1024]{1,0:T(8,128)(2,1)}, u32[]{:S(2)}, u32[]{:S(2)}) collective-permute-start(bf16[64,1024]{1,0:T(8,128)(2,1)} %refs_4_.3), channel_id=1, source_target_pairs={{0,2},{1,3},{2,0},{3,1},{4,6},{5,7},{6,4},{7,5},{8,10},{9,11},{10,... | collective-permute-start | bytes 393224 | tf_op jit(solution)/shard_map/ppermute | solution.py:511
  47.3 43.4 %collective-permute-start.20 = (bf16[256,1152]{1,0:T(8,128)(2,1)S(1)}, bf16[256,1152]{1,0:T(8,128)(2,1)S(1)}, u32[]{:S(2)}, u32[]{:S(2)}) collective-permute-start(bf16[256,1152]{1,0:T(8,128)(2,1)S(1)} %pad_maximum_fusion.2), channel_id=1, source_target_pairs={{0,4},{4,0},{8,12},{12,8},{16,20},{20,16},{24,28},{28,24},{1,5},{5... | collective-permute-start | bytes 1769480 | tf_op jit(solution)/shard_map/ppermute | solution.py:517
  90.7 23.3 %collective-permute-start.28 = (bf16[4,384,128]{2,1,0:T(8,128)(2,1)}, bf16[4,384,128]{2,1,0:T(8,128)(2,1)}, u32[]{:S(2)}, u32[]{:S(2)}) collective-permute-start(bf16[4,384,128]{2,1,0:T(8,128)(2,1)} %get-tuple-element.109), channel_id=1, source_target_pairs={{0,1},{1,0},{2,3},{3,2},{4,5},{5,4},{6,7},{7,6},{8,9},{9,8},{10,11... | collective-permute-start | bytes 1179656 | tf_op jit(solution)/shard_map/ppermute | solution.py:511
  107.8 96.4 %collective-permute-start.22 = (bf16[512,1152]{1,0:T(8,128)(2,1)S(1)}, bf16[512,1152]{1,0:T(8,128)(2,1)}, u32[]{:S(2)}, u32[]{:S(2)}) collective-permute-start(bf16[512,1152]{1,0:T(8,128)(2,1)S(1)} %pad_maximum_fusion.refs_1_), channel_id=1, source_target_pairs={{0,2},{1,3},{2,0},{3,1},{4,6},{5,7},{6,4},{7,5},{8,10},{9,11},{10,... | collective-permute-start | bytes 3538952 | tf_op jit(solution)/shard_map/ppermute | solution.py:517
  109.4 97.8 %collective-permute-start.16 = (bf16[512,1152]{1,0:T(8,128)(2,1)S(1)}, bf16[512,1152]{1,0:T(8,128)(2,1)S(1)}, u32[]{:S(2)}, u32[]{:S(2)}) collective-permute-start(bf16[512,1152]{1,0:T(8,128)(2,1)S(1)} %constant_dynamic-update-slice_fusion.3.refs_1_), channel_id=1, source_target_pairs={{0,2},{1,3},{2,0},{3,1},{4,6},{5,7},{6,4},{7,5},{8,10},{9,11},{10,... | collective-permute-start | bytes 3538952 | tf_op jit(solution)/shard_map/ppermute | solution.py:517
  110.0 60.5 %collective-permute-start.29 = (bf16[4,384,128]{2,1,0:T(8,128)(2,1)}, bf16[4,384,128]{2,1,0:T(8,128)(2,1)}, u32[]{:S(2)}, u32[]{:S(2)}) collective-permute-start(bf16[4,384,128]{2,1,0:T(8,128)(2,1)} %get-tuple-element.110), channel_id=1, source_target_pairs={{0,2},{1,3},{2,0},{3,1},{4,6},{5,7},{6,4},{7,5},{8,10},{9,11},{10,... | collective-permute-start | bytes 1179656 | tf_op jit(solution)/shard_map/ppermute | solution.py:511
  111.5 64.0 %collective-permute-start.30 = (bf16[4,384,128]{2,1,0:T(8,128)(2,1)}, bf16[4,384,128]{2,1,0:T(8,128)(2,1)}, u32[]{:S(2)}, u32[]{:S(2)}) collective-permute-start(bf16[4,384,128]{2,1,0:T(8,128)(2,1)} %get-tuple-element.111), channel_id=1, source_target_pairs={{0,3},{1,2},{2,1},{3,0},{4,7},{5,6},{6,5},{7,4},{8,11},{9,10},{10,... | collective-permute-start | bytes 1179656 | tf_op jit(solution)/shard_map/ppermute | solution.py:511
  114.0 67.0 %collective-permute-start.27 = (bf16[4,384,128]{2,1,0:T(8,128)(2,1)}, bf16[4,384,128]{2,1,0:T(8,128)(2,1)}, u32[]{:S(2)}, u32[]{:S(2)}) collective-permute-start(bf16[4,384,128]{2,1,0:T(8,128)(2,1)} %get-tuple-element.107), channel_id=1, source_target_pairs={{0,4},{4,0},{8,12},{12,8},{16,20},{20,16},{24,28},{28,24},{1,5},{5... | collective-permute-start | bytes 1179656 | tf_op jit(solution)/shard_map/ppermute | solution.py:517
  170.4 26.7 %collective-permute-start.33 = (bf16[4,384,128]{2,1,0:T(8,128)(2,1)}, bf16[4,384,128]{2,1,0:T(8,128)(2,1)}, u32[]{:S(2)}, u32[]{:S(2)}) collective-permute-start(bf16[4,384,128]{2,1,0:T(8,128)(2,1)} %get-tuple-element.114), channel_id=1, source_target_pairs={{0,16},{4,20},{8,24},{12,28},{16,0},{20,4},{24,8},{28,12},{1,17},{... | collective-permute-start | bytes 1179656 | tf_op jit(solution)/shard_map/ppermute | solution.py:517
  175.5 28.7 %collective-permute-start.34 = (bf16[4,384,128]{2,1,0:T(8,128)(2,1)}, bf16[4,384,128]{2,1,0:T(8,128)(2,1)}, u32[]{:S(2)}, u32[]{:S(2)}) collective-permute-start(bf16[4,384,128]{2,1,0:T(8,128)(2,1)} %get-tuple-element.115), channel_id=1, source_target_pairs={{0,20},{4,16},{8,28},{12,24},{16,4},{20,0},{24,12},{28,8},{1,21},{... | collective-permute-start | bytes 1179656 | tf_op jit(solution)/shard_map/ppermute | solution.py:517
  181.1 26.1 %collective-permute-start.31 = (bf16[4,384,128]{2,1,0:T(8,128)(2,1)}, bf16[4,384,128]{2,1,0:T(8,128)(2,1)S(1)}, u32[]{:S(2)}, u32[]{:S(2)}) collective-permute-start(bf16[4,384,128]{2,1,0:T(8,128)(2,1)} %get-tuple-element.112), channel_id=1, source_target_pairs={{0,8},{4,12},{8,0},{12,4},{16,24},{20,28},{24,16},{28,20},{1,9},{5... | collective-permute-start | bytes 1179656 | tf_op jit(solution)/shard_map/ppermute | solution.py:517
  204.2 37.3 %collective-permute-start.21 = (bf16[512,1152]{1,0:T(8,128)(2,1)S(1)}, bf16[512,1152]{1,0:T(8,128)(2,1)S(1)}, u32[]{:S(2)}, u32[]{:S(2)}) collective-permute-start(bf16[512,1152]{1,0:T(8,128)(2,1)S(1)} %pad_maximum_fusion.refs_1_), channel_id=1, source_target_pairs={{0,1},{1,0},{2,3},{3,2},{4,5},{5,4},{6,7},{7,6},{8,9},{9,8},{10,11... | collective-permute-start | bytes 3538952 | tf_op jit(solution)/shard_map/ppermute | solution.py:517
  204.2 38.4 %collective-permute-start.23 = (bf16[512,1152]{1,0:T(8,128)(2,1)}, bf16[512,1152]{1,0:T(8,128)(2,1)S(1)}, u32[]{:S(2)}, u32[]{:S(2)}) collective-permute-start(bf16[512,1152]{1,0:T(8,128)(2,1)} %collective-permute-done.22.refs_3_), channel_id=1, source_target_pairs={{0,1},{1,0},{2,3},{3,2},{4,5},{5,4},{6,7},{7,6},{8,9},{9,8},{10,11... | collective-permute-start | bytes 3538952 | tf_op jit(solution)/shard_map/ppermute | solution.py:517
  207.1 47.8 %collective-permute-start.15 = (bf16[512,1152]{1,0:T(8,128)(2,1)S(1)}, bf16[512,1152]{1,0:T(8,128)(2,1)}, u32[]{:S(2)}, u32[]{:S(2)}) collective-permute-start(bf16[512,1152]{1,0:T(8,128)(2,1)S(1)} %constant_dynamic-update-slice_fusion.3.refs_1_), channel_id=1, source_target_pairs={{0,1},{1,0},{2,3},{3,2},{4,5},{5,4},{6,7},{7,6},{8,9},{9,8},{10,11... | collective-permute-start | bytes 3538952 | tf_op jit(solution)/shard_map/ppermute | solution.py:517
  207.2 47.8 %collective-permute-start.17 = (bf16[512,1152]{1,0:T(8,128)(2,1)S(1)}, bf16[512,1152]{1,0:T(8,128)(2,1)}, u32[]{:S(2)}, u32[]{:S(2)}) collective-permute-start(bf16[512,1152]{1,0:T(8,128)(2,1)S(1)} %collective-permute-done.16.refs_3_), channel_id=1, source_target_pairs={{0,1},{1,0},{2,3},{3,2},{4,5},{5,4},{6,7},{7,6},{8,9},{9,8},{10,11... | collective-permute-start | bytes 3538952 | tf_op jit(solution)/shard_map/ppermute | solution.py:517
  277.8 31.5 %collective-permute-start.46 = (bf16[256,1152]{1,0:T(8,128)(2,1)S(1)}, bf16[256,1152]{1,0:T(8,128)(2,1)S(1)}, u32[]{:S(2)}, u32[]{:S(2)}) collective-permute-start(bf16[256,1152]{1,0:T(8,128)(2,1)S(1)} %get-tuple-element.214), channel_id=1, source_target_pairs={{0,2},{1,3},{2,0},{3,1},{4,6},{5,7},{6,4},{7,5},{8,10},{9,11},{10,... | collective-permute-start | bytes 1769480 | tf_op jit(solution)/shard_map/ppermute | solution.py:517
  323.0 42.4 %collective-permute-start.37 = (bf16[512,1024]{1,0:T(8,128)(2,1)}, bf16[512,1024]{1,0:T(8,128)(2,1)S(1)}, u32[]{:S(2)}, u32[]{:S(2)}) collective-permute-start(bf16[512,1024]{1,0:T(8,128)(2,1)} %get-tuple-element.128), channel_id=1, source_target_pairs={{0,1},{1,0},{2,3},{3,2},{4,5},{5,4},{6,7},{7,6},{8,9},{9,8},{10,11... | collective-permute-start | bytes 3145736 | tf_op jit(solution)/shard_map/ppermute | solution.py:517
  324.1 41.3 %collective-permute-start.40 = (bf16[256,1024]{1,0:T(8,128)(2,1)}, bf16[256,1024]{1,0:T(8,128)(2,1)}, u32[]{:S(2)}, u32[]{:S(2)}) collective-permute-start(bf16[256,1024]{1,0:T(8,128)(2,1)} %get-tuple-element.217), channel_id=1, source_target_pairs={{0,2},{1,3},{2,0},{3,1},{4,6},{5,7},{6,4},{7,5},{8,10},{9,11},{10,... | collective-permute-start | bytes 1572872 | tf_op jit(solution)/shard_map/ppermute | solution.py:517
  350.7 54.8 %collective-permute-start.39 = (bf16[256,1024]{1,0:T(8,128)(2,1)S(1)}, bf16[256,1024]{1,0:T(8,128)(2,1)S(1)}, u32[]{:S(2)}, u32[]{:S(2)}) collective-permute-start(bf16[256,1024]{1,0:T(8,128)(2,1)S(1)} %get-tuple-element.216), channel_id=1, source_target_pairs={{0,2},{1,3},{2,0},{3,1},{4,6},{5,7},{6,4},{7,5},{8,10},{9,11},{10,... | collective-permute-start | bytes 1572872 | tf_op jit(solution)/shard_map/ppermute | solution.py:517
  363.8 44.5 %collective-permute-start.57 = (bf16[512,896]{1,0:T(8,128)(2,1)}, bf16[512,896]{1,0:T(8,128)(2,1)S(1)}, u32[]{:S(2)}, u32[]{:S(2)}) collective-permute-start(bf16[512,896]{1,0:T(8,128)(2,1)} %get-tuple-element.151), channel_id=1, source_target_pairs={{0,4},{4,0},{8,12},{12,8},{16,20},{20,16},{24,28},{28,24},{1,5},{5... | collective-permute-start | bytes 2752520 | tf_op jit(solution)/shard_map/ppermute | solution.py:517
  366.5 40.6 %collective-permute-start.41 = (bf16[256,1024]{1,0:T(8,128)(2,1)S(1)}, bf16[256,1024]{1,0:T(8,128)(2,1)S(1)}, u32[]{:S(2)}, u32[]{:S(2)}) collective-permute-start(bf16[256,1024]{1,0:T(8,128)(2,1)S(1)} %fusion.3), channel_id=1, source_target_pairs={{0,4},{4,0},{8,12},{12,8},{16,20},{20,16},{24,28},{28,24},{1,5},{5... | collective-permute-start | bytes 1572872 | tf_op jit(solution)/shard_map/ppermute | solution.py:517
  367.1 37.9 %collective-permute-start.63 = (bf16[4,384,128]{2,1,0:T(8,128)(2,1)S(1)}, bf16[4,384,128]{2,1,0:T(8,128)(2,1)S(1)}, u32[]{:S(2)}, u32[]{:S(2)}) collective-permute-start(bf16[4,384,128]{2,1,0:T(8,128)(2,1)S(1)} %copy-done.49), channel_id=1, source_target_pairs={{0,4},{4,0},{8,12},{12,8},{16,20},{20,16},{24,28},{28,24},{1,5},{5... | collective-permute-start | bytes 1179656 | tf_op jit(solution)/shard_map/ppermute | solution.py:517
  368.6 36.9 %collective-permute-start.64 = (bf16[4,384,128]{2,1,0:T(8,128)(2,1)S(1)}, bf16[4,384,128]{2,1,0:T(8,128)(2,1)S(1)}, u32[]{:S(2)}, u32[]{:S(2)}) collective-permute-start(bf16[4,384,128]{2,1,0:T(8,128)(2,1)S(1)} %copy-done.48), channel_id=1, source_target_pairs={{0,16},{4,20},{8,24},{12,28},{16,0},{20,4},{24,8},{28,12},{1,17},{... | collective-permute-start | bytes 1179656 | tf_op jit(solution)/shard_map/ppermute | solution.py:517
  407.2 23.0 %collective-permute-start.71 = (bf16[4,384,128]{2,1,0:T(8,128)(2,1)}, bf16[4,384,128]{2,1,0:T(8,128)(2,1)}, u32[]{:S(2)}, u32[]{:S(2)}) collective-permute-start(bf16[4,384,128]{2,1,0:T(8,128)(2,1)} %get-tuple-element.170), channel_id=1, source_target_pairs={{0,3},{1,2},{2,1},{3,0},{4,7},{5,6},{6,5},{7,4},{8,11},{9,10},{10,... | collective-permute-start | bytes 1179656 | tf_op jit(solution)/shard_map/ppermute | solution.py:511
  408.3 24.6 %collective-permute-start.42 = (bf16[128,1024]{1,0:T(8,128)(2,1)}, bf16[128,1024]{1,0:T(8,128)(2,1)}, u32[]{:S(2)}, u32[]{:S(2)}) collective-permute-start(bf16[128,1024]{1,0:T(8,128)(2,1)} %slice.121), channel_id=1, source_target_pairs={{0,8},{4,12},{8,0},{12,4},{16,24},{20,28},{24,16},{28,20},{1,9},{5... | collective-permute-start | bytes 786440 | tf_op jit(solution)/shard_map/ppermute | solution.py:517
  436.9 31.4 %collective-permute-start.74 = (bf16[4,384,128]{2,1,0:T(8,128)(2,1)S(1)}, bf16[4,384,128]{2,1,0:T(8,128)(2,1)S(1)}, u32[]{:S(2)}, u32[]{:S(2)}) collective-permute-start(bf16[4,384,128]{2,1,0:T(8,128)(2,1)S(1)} %copy-done.50), channel_id=1, source_target_pairs={{0,24},{4,28},{8,16},{12,20},{16,8},{20,12},{24,0},{28,4},{1,25},{... | collective-permute-start | bytes 1179656 | tf_op jit(solution)/shard_map/ppermute | solution.py:517
  440.4 52.7 %collective-permute-start.75 = (bf16[4,384,128]{2,1,0:T(8,128)(2,1)}, bf16[4,384,128]{2,1,0:T(8,128)(2,1)S(1)}, u32[]{:S(2)}, u32[]{:S(2)}) collective-permute-start(bf16[4,384,128]{2,1,0:T(8,128)(2,1)} %get-tuple-element.174), channel_id=1, source_target_pairs={{0,28},{4,24},{8,20},{12,16},{16,12},{20,8},{24,4},{28,0},{1,29},{... | collective-permute-start | bytes 1179656 | tf_op jit(solution)/shard_map/ppermute | solution.py:517
  448.3 42.2 %collective-permute-start.59 = (bf16[128,896]{1,0:T(8,128)(2,1)S(1)}, bf16[128,896]{1,0:T(8,128)(2,1)S(1)}, u32[]{:S(2)}, u32[]{:S(2)}) collective-permute-start(bf16[128,896]{1,0:T(8,128)(2,1)S(1)} %get-tuple-element.218), channel_id=1, source_target_pairs={{0,16},{4,20},{8,24},{12,28},{16,0},{20,4},{24,8},{28,12},{1,17},{... | collective-permute-start | bytes 688136 | tf_op jit(solution)/shard_map/ppermute | solution.py:517
  450.9 43.3 %collective-permute-start.43 = (bf16[64,1024]{1,0:T(8,128)(2,1)}, bf16[64,1024]{1,0:T(8,128)(2,1)S(1)}, u32[]{:S(2)}, u32[]{:S(2)}) collective-permute-start(bf16[64,1024]{1,0:T(8,128)(2,1)} %get-tuple-element.222), channel_id=1, source_target_pairs={{0,16},{4,20},{8,24},{12,28},{16,0},{20,4},{24,8},{28,12},{1,17},{... | collective-permute-start | bytes 393224 | tf_op jit(solution)/shard_map/ppermute | solution.py:517
  457.3 38.6 %collective-permute-start.54 = (bf16[64,1024]{1,0:T(8,128)(2,1)}, bf16[64,1024]{1,0:T(8,128)(2,1)S(1)}, u32[]{:S(2)}, u32[]{:S(2)}) collective-permute-start(bf16[64,1024]{1,0:T(8,128)(2,1)} %get-tuple-element.146), channel_id=1, source_target_pairs={{0,1},{1,0},{2,3},{3,2},{4,5},{5,4},{6,7},{7,6},{8,9},{9,8},{10,11... | collective-permute-start | bytes 393224 | tf_op jit(solution)/shard_map/ppermute | solution.py:511
  468.2 34.5 %collective-permute-start.55 = (bf16[64,1024]{1,0:T(8,128)(2,1)}, bf16[64,1024]{1,0:T(8,128)(2,1)S(1)}, u32[]{:S(2)}, u32[]{:S(2)}) collective-permute-start(bf16[64,1024]{1,0:T(8,128)(2,1)} %get-tuple-element.147), channel_id=1, source_target_pairs={{0,2},{1,3},{2,0},{3,1},{4,6},{5,7},{6,4},{7,5},{8,10},{9,11},{10,... | collective-permute-start | bytes 393224 | tf_op jit(solution)/shard_map/ppermute | solution.py:511
  (95 other events, 1443.6 us)

commit v5 on v4

--- a/solution.py
+++ b/solution.py
@@ -17,10 +17,11 @@
 score_scale = 0.125
 rope_base = 10000.0
 
-CHUNKS = ((0, 1, 4, 5), (2, 3, 6, 7))
+CHUNKS = ((0, 2, 4, 6), (1, 3, 5, 7))
 TOKEN_BITS = (4, 2, 1)
 QKV_BITS = (4, 2, 1)
 REST_BITS = (1, 4, 2)
+GRAD_BITS = (4, 1, 2)
 
 BF = jnp.bfloat16
 F32 = jnp.float32
@@ -317,10 +318,11 @@
 
 
 def expert_rest_kernel(peers, shares, step, *refs):
-    (idx,), ins, y_out, first_out, second_out, (scaled,) = split_refs(
-        refs, 1, 7, shares, len(CHUNKS[0]), shares, 1
+    (idx,), ins, y_out, first_out, second_out, scratch = split_refs(
+        refs, 1, 7, shares, len(CHUNKS[0]), shares, 3
     )
     rows, hid, gpu, gate_in, hot_in, grads, down = ins
+    scaled, both_s, down_s = scratch
     span = y_out[0].shape[0] // peers
     block = shares * span
     scaled[...] = (grads[...].astype(F32) * gate_in[:, 0:1]).astype(BF)
@@ -338,38 +340,19 @@
 
     lax.fori_loop(0, peers, out_rows, 0)
 
-    def model_rows(p):
-        q = jnp.bitwise_xor(p, idx[0] // 2)
+    low = idx[0] % 2
+    for pair in range(peers // 2):
+        q = jnp.bitwise_xor(pair, idx[0] // 2)
         at = pl.ds(pl.multiple_of(q * step, step), step)
-        both = mm(rows[:, at], gpu[...], 0, 0).astype(BF)
-        return both, mm(hid[...], scaled[:, at], 0, 0).astype(BF)
-
-    def store(to, both, down_g, s, t):
-        r = slice(s * 128, (s + 1) * 128)
-        to[0:128, :] = both[r, t * 128 : (t + 1) * 128]
-        to[128:256, :] = both[r, (shares + t) * 128 : (shares + t + 1) * 128]
-        to[256:384, :] = down_g[t * 128 : (t + 1) * 128, r]
-
-    low = idx[0] % 2
-    for pair in range(2):
-        both, down_g = model_rows(CHUNKS[0][pair * 2] // 2)
-        for s in range(2):
-            for odd in range(2):
-
-                @pl.when(jnp.bitwise_xor(low, s) == odd)
-                def _():
-                    for t in range(shares):
-                        store(first_out[pair * 2 + odd].at[t], both, down_g, s, t)
-
-    def body(pair, carry):
-        both, down_g = model_rows(pair * 2 + 1)
-        for s in range(2):
-            j = pair * 2 + jnp.bitwise_xor(low, s)
+        both_s[...] = mm(rows[:, at], gpu[...], 0, 0).astype(BF)
+        down_s[...] = mm(hid[...], scaled[:, at], 0, 0).astype(BF)
+        for odd in range(2):
+            r = pl.ds(pl.multiple_of(jnp.bitwise_xor(low, odd) * 128, 128), 128)
             for t in range(shares):
-                store(second_out[t].at[j], both, down_g, s, t)
-        return carry
-
-    lax.fori_loop(0, 2, body, 0)
+                to = second_out[t].at[pair] if odd else first_out[pair].at[t]
+                to[0:128, :] = both_s[r, t * 128 : (t + 1) * 128]
+                to[128:256, :] = both_s[r, (shares + t) * 128 : (shares + t + 1) * 128]
+                to[256:384, :] = down_s[t * 128 : (t + 1) * 128, r]
 
 
 def hi_lo_rows(row, count):
@@ -463,7 +446,7 @@
         rows = jnp.where(place == 32 + at, row, rows)
     sums[:, o_at:] = mm(rows2[...], logit, 0, 0) + jnp.transpose(rows)
     depth = width // peers
-    for k, m in enumerate(visit_order(TOKEN_BITS)):
+    for k, m in enumerate(visit_order(GRAD_BITS)):
         at = pl.multiple_of(jnp.bitwise_xor(idx[0], m) * depth, depth)
         out = g_out[k // (peers // 2)]
         k = k % (peers // 2)
@@ -532,13 +515,13 @@
     return first, beside, across, permute(across, "tensor", 1)
 
 
-def reduce_dp(even, odd, other=None):
-    got = permute(odd, "dp", 1)
-    even = even + got if other is None else even + other + got
-    half = even.shape[0] // 2
-    even = even[:half] + permute(even[half:], "dp", 2)
+def reduce_dp(near, far, bits, other=None):
+    got = permute(far, "dp", bits[2])
+    near = near + got if other is None else near + other + got
+    half = near.shape[0] // 2
+    near = near[:half] + permute(near[half:], "dp", bits[1])
     half = half // 2
-    return even[:half], permute(even[half:], "dp", 4)
+    return near[:half], permute(near[half:], "dp", bits[0])
 
 
 def reduce_all(parts):
@@ -548,7 +531,7 @@
     far_odd = permute(parts[2][half:] + far[half:], "tensor", 2)
     far_even = permute(parts[2][:half] + far[:half], "tensor", 2)
     odd = parts[0][half:] + own[half:] + far_odd
-    return reduce_dp(parts[0][:half] + own[:half], odd, far_even)
+    return reduce_dp(parts[0][:half] + own[:half], odd, TOKEN_BITS, far_even)
 
 
 def regroup(parts):
@@ -692,7 +675,7 @@
         [((peers * own, width), BF)] * shares
         + [((shares, 384, LANES), BF)] * len(CHUNKS[0])
         + [((len(CHUNKS[1]), 384, LANES), BF)] * shares,
-        scratch=[((slots, width), BF)],
+        scratch=[((slots, width), BF), ((256, 2 * ff), BF), ((ff, 256), BF)],
         smem=1,
     )(idx, *saved, hots, grad_rows, down)
     y_parts, first, second = rest[:shares], rest[shares : shares + 4], rest[shares + 4 :]
@@ -713,7 +696,7 @@
         smem=1,
     )(idx, *msgs, wall, qkv, att, logs, cosine, sine, seg_c, seg_r, hid, rows_near, x_all)
     msg2 = outs[2:]
-    terms = reduce_dp(outs[0], outs[1])
+    terms = reduce_dp(outs[0], outs[1], GRAD_BITS)
     if rep > 1:
         total = terms[0].astype(F32) + terms[1].astype(F32)
         terms = (lax.psum_scatter(total, "rep", scatter_dimension=0, tiled=True),)

time: 508 us -> 487 us (0.959)
  waiting for transfers between devices: 305 us -> 294 us
  starting transfers between devices: 86.3 us -> 78.4 us
    ppermute x49, waiting for transfers between devices: 227 us -> 216 us  [permute(): return lax.ppermute(value, axis, [(i, i ^ bit) for i in range(count)])]
  transfers between devices with their start and end apart: 76 -> 76, of which waited for: 34 -> 31; matrix products, arithmetic and copies ran while one was open for 4% -> 5% of each run, Pallas kernels for 13% -> 14%
where the time goes in v5:
time: 487 us
  waiting for transfers between devices  294 us (60%)
  Pallas kernels  83 us (17%)
  starting transfers between devices  78.4 us (16%)
  local copies, waits for them, and re-layouts  17.2 us (4%)
  other arithmetic  12.3 us (3%)
    ppermute x49, waiting for transfers between devices, permute(): return lax.ppermute(value, axis, [(i, i ^ bit) for i in range(count)])  216 us
    pallas_call x16, Pallas kernels, run(): pl.pallas_call(kernel, out_shape=[jax.ShapeDtypeStruct(s, d) for s, d in...  83 us
    ppermute x27, waiting for transfers between devices, swap(): lax.ppermute(values[m], axis, [(i, i ^ m) for i in range(len(values))])  78 us
    ppermute x49, starting transfers between devices, permute(): return lax.ppermute(value, axis, [(i, i ^ bit) for i in range(count)])  60.9 us
    ppermute x27, starting transfers between devices, swap(): lax.ppermute(values[m], axis, [(i, i ^ m) for i in range(len(values))])  17.5 us
    unnamed x110, local copies, waits for them, and re-layouts  10.3 us
  transfers between devices with their start and end apart: 76, of which 31 were waited for; matrix products, arithmetic and copies ran while one was open for 5% of the time, Pallas kernels for 14%

profile of v5, /device:TPU:0, one launch (start us, length us, event | category | flops | bytes accessed | tf_op | source)
XLA Modules:
  0.0 486.6 jit_solution(5888053425031738988)
XLA Ops:
  18.4 10.3 %collective-permute-done.3 = bf16[128,512]{1,0:T(8,128)(2,1)S(1)} collective-permute-done((bf16[128,512]{1,0:T(8,128)(2,1)S(1)}, bf16[128,512]{1,0:T(8,128)(2,1)S(1)}, u32[]{:S(2)}, u32[]{:S(2)}) %collective-permute-start.3) | collective-permute-done | bytes 131104 | tf_op jit(solution)/shard_map/ppermute | solution.py:500
  36.0 4.9 %collective-permute-done.4 = bf16[256,512]{1,0:T(8,128)(2,1)S(1)} collective-permute-done((bf16[256,512]{1,0:T(8,128)(2,1)S(1)}, bf16[256,512]{1,0:T(8,128)(2,1)S(1)}, u32[]{:S(2)}, u32[]{:S(2)}) %collective-permute-start.4) | collective-permute-done | bytes 262176 | tf_op jit(solution)/shard_map/ppermute | solution.py:500
  42.7 4.5 collective-permute-done.19
  49.2 6.3 %collective-permute-done.8.refs_8_ = bf16[512,384]{1,0:T(8,128)(2,1)S(1)} collective-permute-done((bf16[512,384]{1,0:T(8,128)(2,1)S(1)}, bf16[512,384]{1,0:T(8,128)(2,1)S(1)}, u32[]{:S(2)}, u32[]{:S(2)}) %collective-permute-start.8) | collective-permute-done | bytes 393248 | tf_op jit(solution)/shard_map/ppermute | solution.py:500
  56.2 5.3 %shard_map.229 = (bf16[64,1024]{1,0:T(8,128)(2,1)}, bf16[64,1024]{1,0:T(8,128)(2,1)}, bf16[64,1024]{1,0:T(8,128)(2,1)}, bf16[64,1024]{1,0:T(8,128)(2,1)}, bf16[1...) custom-call(s32[2]{0:T(128)} %pad_add_fusion.refs_0_.idx, ...), custom_call_target="tpu_custom_call" | custom-call | tf_op jit(solution)/shard_map/pallas_call | solution.py:38
  63.5 4.8 collective-permute-done.10.refs_2_
  74.6 8.8 %collective-permute-done.12 = bf16[64,1152]{1,0:T(8,128)(2,1)S(1)} collective-permute-done((bf16[64,1152]{1,0:T(8,128)(2,1)}, bf16[64,1152]{1,0:T(8,128)(2,1)S(1)}, u32[]{:S(2)}, u32[]{:S(2)}) %collective-permute-start.12) | collective-permute-done | bytes 147488 | tf_op jit(solution)/shard_map/ppermute | solution.py:500
  85.1 3.7 shard_map.231
  94.4 13.4 %collective-permute-done.14 = bf16[256,1152]{1,0:T(8,128)(2,1)S(1)} collective-permute-done((bf16[256,1152]{1,0:T(8,128)(2,1)S(1)}, bf16[256,1152]{1,0:T(8,128)(2,1)S(1)}, u32[]{:S(2)}, u32[]{:S(2)}) %collective-permute-start.14) | collective-permute-done | bytes 589856 | tf_op jit(solution)/shard_map/ppermute | solution.py:500
  115.5 55.0 %collective-permute-done.28.refs_2_ = bf16[4,384,128]{2,1,0:T(8,128)(2,1)} collective-permute-done((bf16[4,384,128]{2,1,0:T(8,128)(2,1)}, bf16[4,384,128]{2,1,0:T(8,128)(2,1)}, u32[]{:S(2)}, u32[]{:S(2)}) %collective-permute-start.28) | collective-permute-done | bytes 393248 | tf_op jit(solution)/shard_map/ppermute | solution.py:494
  175.5 3.6 collective-permute-start.35
  182.1 14.9 %collective-permute-done.33.refs_9_ = bf16[4,384,128]{2,1,0:T(8,128)(2,1)} collective-permute-done((bf16[4,384,128]{2,1,0:T(8,128)(2,1)}, bf16[4,384,128]{2,1,0:T(8,128)(2,1)}, u32[]{:S(2)}, u32[]{:S(2)}) %collective-permute-start.33) | collective-permute-done | bytes 393248 | tf_op jit(solution)/shard_map/ppermute | solution.py:500
  198.2 8.5 %collective-permute-done.32.refs_8_ = bf16[4,384,128]{2,1,0:T(8,128)(2,1)S(1)} collective-permute-done((bf16[4,384,128]{2,1,0:T(8,128)(2,1)}, bf16[4,384,128]{2,1,0:T(8,128)(2,1)S(1)}, u32[]{:S(2)}, u32[]{:S(2)}) %collective-permute-start.32) | collective-permute-done | bytes 393248 | tf_op jit(solution)/shard_map/ppermute | solution.py:500
  208.1 17.3 %collective-permute-done.34.refs_10_ = bf16[4,384,128]{2,1,0:T(8,128)(2,1)S(1)} collective-permute-done((bf16[4,384,128]{2,1,0:T(8,128)(2,1)}, bf16[4,384,128]{2,1,0:T(8,128)(2,1)S(1)}, u32[]{:S(2)}, u32[]{:S(2)}) %collective-permute-start.34) | collective-permute-done | bytes 393248 | tf_op jit(solution)/shard_map/ppermute | solution.py:500
  227.3 10.0 %collective-permute-done.36.refs_12_ = bf16[4,384,128]{2,1,0:T(8,128)(2,1)S(1)} collective-permute-done((bf16[4,384,128]{2,1,0:T(8,128)(2,1)}, bf16[4,384,128]{2,1,0:T(8,128)(2,1)S(1)}, u32[]{:S(2)}, u32[]{:S(2)}) %collective-permute-start.36) | collective-permute-done | bytes 393248 | tf_op jit(solution)/shard_map/ppermute | solution.py:500
  239.5 11.2 %shard_map.234 = (bf16[2048,128]{1,0:T(8,128)(2,1)}, bf16[1024,1024]{1,0:T(8,128)(2,1)}, f32[1024,512]{1,0:T(8,128)}, bf16[1024,1024]{1,0:T(8,128)(2,1)}, bf16[512,1024]{1,0:T(8,128)(2,1)}) custom-call(s32[2]{0:T(128)} %pad_add_fusion.refs_0_.idx, bf16[512,1152]{1,0:T(8,128)(2,1)} %copy-done.2, bf16[512,1152]{1,0:T(8,128)(2,1)} %copy-done.11, ...), custom_call_target="tpu_custom_call" | custom-call | tf_op jit(solution)/shard_map/pallas_call | solution.py:38
  250.7 16.1 %shard_map.235 = (bf16[512,1152]{1,0:T(8,128)(2,1)}, bf16[512,1152]{1,0:T(8,128)(2,1)}, bf16[512,1152]{1,0:T(8,128)(2,1)}, bf16[512,1152]{1,0:T(8,128)(2,1)}, bf...) custom-call(s32[2]{0:T(128)} %pad_add_fusion.refs_0_.idx, ...), custom_call_target="tpu_custom_call" | custom-call | tf_op jit(solution)/shard_map/pallas_call | solution.py:38
  273.4 14.2 %collective-permute-done.47 = bf16[256,1152]{1,0:T(8,128)(2,1)S(1)} collective-permute-done((bf16[256,1152]{1,0:T(8,128)(2,1)S(1)}, bf16[256,1152]{1,0:T(8,128)(2,1)S(1)}, u32[]{:S(2)}, u32[]{:S(2)}) %collective-permute-start.47) | collective-permute-done | bytes 589856 | tf_op jit(solution)/shard_map/ppermute | solution.py:500
  291.0 13.8 %shard_map.236 = (bf16[512,1024]{1,0:T(8,128)(2,1)}, bf16[512,1024]{1,0:T(8,128)(2,1)}, bf16[512,1024]{1,0:T(8,128)(2,1)}, bf16[512,1024]{1,0:T(8,128)(2,1)}, bf...) custom-call(s32[2]{0:T(128)} %pad_add_fusion.refs_0_.idx, ...), custom_call_target="tpu_custom_call" | custom-call | tf_op jit(solution)/shard_map/pallas_call | solution.py:38
  306.2 4.2 collective-permute-start.49
  313.0 5.0 %collective-permute-done.49 = bf16[128,1152]{1,0:T(8,128)(2,1)S(1)} collective-permute-done((bf16[128,1152]{1,0:T(8,128)(2,1)S(1)}, bf16[128,1152]{1,0:T(8,128)(2,1)S(1)}, u32[]{:S(2)}, u32[]{:S(2)}) %collective-permute-start.49) | collective-permute-done | bytes 294944 | tf_op jit(solution)/shard_map/ppermute | solution.py:500
  321.0 7.5 %collective-permute-done.50.refs_1_ = bf16[64,1152]{1,0:T(8,128)(2,1)S(1)} collective-permute-done((bf16[64,1152]{1,0:T(8,128)(2,1)S(1)}, bf16[64,1152]{1,0:T(8,128)(2,1)S(1)}, u32[]{:S(2)}, u32[]{:S(2)}) %collective-permute-start.50) | collective-permute-done | bytes 147488 | tf_op jit(solution)/shard_map/ppermute | solution.py:500
  333.4 5.2 %collective-permute-done.53.refs_4_ = bf16[80,1152]{1,0:T(8,128)(2,1)S(1)} collective-permute-done((bf16[80,1152]{1,0:T(8,128)(2,1)}, bf16[80,1152]{1,0:T(8,128)(2,1)S(1)}, u32[]{:S(2)}, u32[]{:S(2)}) %collective-permute-start.53) | collective-permute-done | bytes 184352 | tf_op jit(solution)/shard_map/ppermute | solution.py:494
  343.5 7.2 %shard_map.239 = (bf16[512,896]{1,0:T(8,128)(2,1)}, bf16[512,896]{1,0:T(8,128)(2,1)}, bf16[64,1024]{1,0:T(8,128)(2,1)}, bf16[64,1024]{1,0:T(8,128)(2,1)}, bf16[6...) custom-call(s32[2]{0:T(128)} %pad_add_fusion.refs_0_.idx, bf16[80,1152]{1,0:T(8,128)(2,1)} %get-tuple-element.137.refs_1_, ...), custom_call_target="tpu_custom_call" | custom-call | tf_op jit(solution)/shard_map/pallas_call | solution.py:38
  356.7 33.4 %collective-permute-done.63.refs_1_ = bf16[4,384,128]{2,1,0:T(8,128)(2,1)S(1)} collective-permute-done((bf16[4,384,128]{2,1,0:T(8,128)(2,1)S(1)}, bf16[4,384,128]{2,1,0:T(8,128)(2,1)S(1)}, u32[]{:S(2)}, u32[]{:S(2)}) %collective-permute-start.63) | collective-permute-done | bytes 393248 | tf_op jit(solution)/shard_map/ppermute | solution.py:500
  395.0 8.8 %collective-permute-done.65.refs_3_ = bf16[4,384,128]{2,1,0:T(8,128)(2,1)S(1)} collective-permute-done((bf16[4,384,128]{2,1,0:T(8,128)(2,1)S(1)}, bf16[4,384,128]{2,1,0:T(8,128)(2,1)S(1)}, u32[]{:S(2)}, u32[]{:S(2)}) %collective-permute-start.65) | collective-permute-done | bytes 393248 | tf_op jit(solution)/shard_map/ppermute | solution.py:500
  424.5 3.9 collective-permute-done.68.refs_3_
  428.5 4.5 collective-permute-start.59
  433.7 17.0 %collective-permute-done.72.refs_4_ = bf16[4,384,128]{2,1,0:T(8,128)(2,1)} collective-permute-done((bf16[4,384,128]{2,1,0:T(8,128)(2,1)}, bf16[4,384,128]{2,1,0:T(8,128)(2,1)}, u32[]{:S(2)}, u32[]{:S(2)}) %collective-permute-start.72) | collective-permute-done | bytes 393248 | tf_op jit(solution)/shard_map/ppermute | solution.py:500
  450.8 8.2 %collective-permute-done.74.refs_6_ = bf16[4,384,128]{2,1,0:T(8,128)(2,1)S(1)} collective-permute-done((bf16[4,384,128]{2,1,0:T(8,128)(2,1)S(1)}, bf16[4,384,128]{2,1,0:T(8,128)(2,1)S(1)}, u32[]{:S(2)}, u32[]{:S(2)}) %collective-permute-start.74) | collective-permute-done | bytes 393248 | tf_op jit(solution)/shard_map/ppermute | solution.py:500
  459.4 11.6 %collective-permute-done.59.refs_1_ = bf16[128,896]{1,0:T(8,128)(2,1)S(1)} collective-permute-done((bf16[128,896]{1,0:T(8,128)(2,1)S(1)}, bf16[128,896]{1,0:T(8,128)(2,1)S(1)}, u32[]{:S(2)}, u32[]{:S(2)}) %collective-permute-start.59) | collective-permute-done | bytes 229408 | tf_op jit(solution)/shard_map/ppermute | solution.py:500
  475.8 4.9 %shard_map.244 = (f32[32,128,128]{2,1,0:T(8,128)}, f32[32,128,128]{2,1,0:T(8,128)}, f32[32,128,128]{2,1,0:T(8,128)}) custom-call(s32[2]{0:T(128)} %pad_add_fusion.refs_0_.idx, bf16[4,384,128]{2,1,0:T(8,128)(2,1)} %get-tuple-element.163.refs_0_, bf16[4,384,128]{2,1,0:T(8,128)(2,1)} %copy-done.23, bf16[4,384,128]{2,1,0:T(8,128)(2,1)} %copy-done.24, ...), custom_call_target="tpu_custom_call" | custom-call | tf_op jit(solution)/shard_map/pallas_call | solution.py:38
  (289 shorter events, 137.2 us)
Async XLA Ops:
  0.7 46.6 %collective-permute-start.2 = (bf16[64,1024]{1,0:T(8,128)(2,1)}, bf16[64,1024]{1,0:T(8,128)(2,1)S(1)}, u32[]{:S(2)}, u32[]{:S(2)}) collective-permute-start(bf16[64,1024]{1,0:T(8,128)(2,1)} %refs_4_.3), channel_id=1, source_target_pairs={{0,3},{1,2},{2,1},{3,0},{4,7},{5,6},{6,5},{7,4},{8,11},{9,10},{10,... | collective-permute-start | bytes 393224 | tf_op jit(solution)/shard_map/ppermute | solution.py:494
  3.2 46.0 %collective-permute-start.1 = (bf16[64,1024]{1,0:T(8,128)(2,1)}, bf16[64,1024]{1,0:T(8,128)(2,1)}, u32[]{:S(2)}, u32[]{:S(2)}) collective-permute-start(bf16[64,1024]{1,0:T(8,128)(2,1)} %refs_4_.3), channel_id=1, source_target_pairs={{0,2},{1,3},{2,0},{3,1},{4,6},{5,7},{6,4},{7,5},{8,10},{9,11},{10,... | collective-permute-start | bytes 393224 | tf_op jit(solution)/shard_map/ppermute | solution.py:494
  47.3 43.4 %collective-permute-start.20 = (bf16[256,1152]{1,0:T(8,128)(2,1)S(1)}, bf16[256,1152]{1,0:T(8,128)(2,1)S(1)}, u32[]{:S(2)}, u32[]{:S(2)}) collective-permute-start(bf16[256,1152]{1,0:T(8,128)(2,1)S(1)} %pad_maximum_fusion.2), channel_id=1, source_target_pairs={{0,4},{4,0},{8,12},{12,8},{16,20},{20,16},{24,28},{28,24},{1,5},{5... | collective-permute-start | bytes 1769480 | tf_op jit(solution)/shard_map/ppermute | solution.py:500
  88.8 21.2 %collective-permute-start.25 = (bf16[4,384,128]{2,1,0:T(8,128)(2,1)}, bf16[4,384,128]{2,1,0:T(8,128)(2,1)}, u32[]{:S(2)}, u32[]{:S(2)}) collective-permute-start(bf16[4,384,128]{2,1,0:T(8,128)(2,1)} %get-tuple-element.104), channel_id=1, source_target_pairs={{0,2},{1,3},{2,0},{3,1},{4,6},{5,7},{6,4},{7,5},{8,10},{9,11},{10,... | collective-permute-start | bytes 1179656 | tf_op jit(solution)/shard_map/ppermute | solution.py:494
  90.7 23.3 %collective-permute-start.27 = (bf16[4,384,128]{2,1,0:T(8,128)(2,1)}, bf16[4,384,128]{2,1,0:T(8,128)(2,1)}, u32[]{:S(2)}, u32[]{:S(2)}) collective-permute-start(bf16[4,384,128]{2,1,0:T(8,128)(2,1)} %get-tuple-element.108), channel_id=1, source_target_pairs={{0,1},{1,0},{2,3},{3,2},{4,5},{5,4},{6,7},{7,6},{8,9},{9,8},{10,11... | collective-permute-start | bytes 1179656 | tf_op jit(solution)/shard_map/ppermute | solution.py:494
  107.8 89.3 %collective-permute-start.22 = (bf16[512,1152]{1,0:T(8,128)(2,1)S(1)}, bf16[512,1152]{1,0:T(8,128)(2,1)}, u32[]{:S(2)}, u32[]{:S(2)}) collective-permute-start(bf16[512,1152]{1,0:T(8,128)(2,1)S(1)} %pad_maximum_fusion.refs_1_), channel_id=1, source_target_pairs={{0,2},{1,3},{2,0},{3,1},{4,6},{5,7},{6,4},{7,5},{8,10},{9,11},{10,... | collective-permute-start | bytes 3538952 | tf_op jit(solution)/shard_map/ppermute | solution.py:500
  109.4 88.4 %collective-permute-start.16 = (bf16[512,1152]{1,0:T(8,128)(2,1)S(1)}, bf16[512,1152]{1,0:T(8,128)(2,1)S(1)}, u32[]{:S(2)}, u32[]{:S(2)}) collective-permute-start(bf16[512,1152]{1,0:T(8,128)(2,1)S(1)} %constant_dynamic-update-slice_fusion.3.refs_1_), channel_id=1, source_target_pairs={{0,2},{1,3},{2,0},{3,1},{4,6},{5,7},{6,4},{7,5},{8,10},{9,11},{10,... | collective-permute-start | bytes 3538952 | tf_op jit(solution)/shard_map/ppermute | solution.py:500
  110.0 60.5 %collective-permute-start.28 = (bf16[4,384,128]{2,1,0:T(8,128)(2,1)}, bf16[4,384,128]{2,1,0:T(8,128)(2,1)}, u32[]{:S(2)}, u32[]{:S(2)}) collective-permute-start(bf16[4,384,128]{2,1,0:T(8,128)(2,1)} %get-tuple-element.109), channel_id=1, source_target_pairs={{0,2},{1,3},{2,0},{3,1},{4,6},{5,7},{6,4},{7,5},{8,10},{9,11},{10,... | collective-permute-start | bytes 1179656 | tf_op jit(solution)/shard_map/ppermute | solution.py:494
  111.5 64.0 %collective-permute-start.29 = (bf16[4,384,128]{2,1,0:T(8,128)(2,1)}, bf16[4,384,128]{2,1,0:T(8,128)(2,1)}, u32[]{:S(2)}, u32[]{:S(2)}) collective-permute-start(bf16[4,384,128]{2,1,0:T(8,128)(2,1)} %get-tuple-element.110), channel_id=1, source_target_pairs={{0,3},{1,2},{2,1},{3,0},{4,7},{5,6},{6,5},{7,4},{8,11},{9,10},{10,... | collective-permute-start | bytes 1179656 | tf_op jit(solution)/shard_map/ppermute | solution.py:494
  114.0 67.6 %collective-permute-start.31 = (bf16[4,384,128]{2,1,0:T(8,128)(2,1)}, bf16[4,384,128]{2,1,0:T(8,128)(2,1)}, u32[]{:S(2)}, u32[]{:S(2)}) collective-permute-start(bf16[4,384,128]{2,1,0:T(8,128)(2,1)} %get-tuple-element.112), channel_id=1, source_target_pairs={{0,8},{4,12},{8,0},{12,4},{16,24},{20,28},{24,16},{28,20},{1,9},{5... | collective-permute-start | bytes 1179656 | tf_op jit(solution)/shard_map/ppermute | solution.py:500
  170.4 26.6 %collective-permute-start.33 = (bf16[4,384,128]{2,1,0:T(8,128)(2,1)}, bf16[4,384,128]{2,1,0:T(8,128)(2,1)}, u32[]{:S(2)}, u32[]{:S(2)}) collective-permute-start(bf16[4,384,128]{2,1,0:T(8,128)(2,1)} %get-tuple-element.114), channel_id=1, source_target_pairs={{0,16},{4,20},{8,24},{12,28},{16,0},{20,4},{24,8},{28,12},{1,17},{... | collective-permute-start | bytes 1179656 | tf_op jit(solution)/shard_map/ppermute | solution.py:500
  175.5 21.5 %collective-permute-start.35 = (bf16[4,384,128]{2,1,0:T(8,128)(2,1)}, bf16[4,384,128]{2,1,0:T(8,128)(2,1)}, u32[]{:S(2)}, u32[]{:S(2)}) collective-permute-start(bf16[4,384,128]{2,1,0:T(8,128)(2,1)} %get-tuple-element.116), channel_id=1, source_target_pairs={{0,24},{4,28},{8,16},{12,20},{16,8},{20,12},{24,0},{28,4},{1,25},{... | collective-permute-start | bytes 1179656 | tf_op jit(solution)/shard_map/ppermute | solution.py:500
  197.0 40.3 %collective-permute-start.21 = (bf16[512,1152]{1,0:T(8,128)(2,1)S(1)}, bf16[512,1152]{1,0:T(8,128)(2,1)S(1)}, u32[]{:S(2)}, u32[]{:S(2)}) collective-permute-start(bf16[512,1152]{1,0:T(8,128)(2,1)S(1)} %pad_maximum_fusion.refs_1_), channel_id=1, source_target_pairs={{0,1},{1,0},{2,3},{3,2},{4,5},{5,4},{6,7},{7,6},{8,9},{9,8},{10,11... | collective-permute-start | bytes 3538952 | tf_op jit(solution)/shard_map/ppermute | solution.py:500
  197.1 41.3 %collective-permute-start.23 = (bf16[512,1152]{1,0:T(8,128)(2,1)}, bf16[512,1152]{1,0:T(8,128)(2,1)S(1)}, u32[]{:S(2)}, u32[]{:S(2)}) collective-permute-start(bf16[512,1152]{1,0:T(8,128)(2,1)} %collective-permute-done.22.refs_3_), channel_id=1, source_target_pairs={{0,1},{1,0},{2,3},{3,2},{4,5},{5,4},{6,7},{7,6},{8,9},{9,8},{10,11... | collective-permute-start | bytes 3538952 | tf_op jit(solution)/shard_map/ppermute | solution.py:500
  197.6 53.1 %collective-permute-start.15 = (bf16[512,1152]{1,0:T(8,128)(2,1)S(1)}, bf16[512,1152]{1,0:T(8,128)(2,1)}, u32[]{:S(2)}, u32[]{:S(2)}) collective-permute-start(bf16[512,1152]{1,0:T(8,128)(2,1)S(1)} %constant_dynamic-update-slice_fusion.3.refs_1_), channel_id=1, source_target_pairs={{0,1},{1,0},{2,3},{3,2},{4,5},{5,4},{6,7},{7,6},{8,9},{9,8},{10,11... | collective-permute-start | bytes 3538952 | tf_op jit(solution)/shard_map/ppermute | solution.py:500
  197.8 52.9 %collective-permute-start.17 = (bf16[512,1152]{1,0:T(8,128)(2,1)S(1)}, bf16[512,1152]{1,0:T(8,128)(2,1)}, u32[]{:S(2)}, u32[]{:S(2)}) collective-permute-start(bf16[512,1152]{1,0:T(8,128)(2,1)S(1)} %collective-permute-done.16.refs_3_), channel_id=1, source_target_pairs={{0,1},{1,0},{2,3},{3,2},{4,5},{5,4},{6,7},{7,6},{8,9},{9,8},{10,11... | collective-permute-start | bytes 3538952 | tf_op jit(solution)/shard_map/ppermute | solution.py:500
  272.9 32.0 %collective-permute-start.46 = (bf16[256,1152]{1,0:T(8,128)(2,1)S(1)}, bf16[256,1152]{1,0:T(8,128)(2,1)S(1)}, u32[]{:S(2)}, u32[]{:S(2)}) collective-permute-start(bf16[256,1152]{1,0:T(8,128)(2,1)S(1)} %get-tuple-element.214), channel_id=1, source_target_pairs={{0,2},{1,3},{2,0},{3,1},{4,6},{5,7},{6,4},{7,5},{8,10},{9,11},{10,... | collective-permute-start | bytes 1769480 | tf_op jit(solution)/shard_map/ppermute | solution.py:500
  310.4 40.4 %collective-permute-start.37 = (bf16[512,1024]{1,0:T(8,128)(2,1)}, bf16[512,1024]{1,0:T(8,128)(2,1)S(1)}, u32[]{:S(2)}, u32[]{:S(2)}) collective-permute-start(bf16[512,1024]{1,0:T(8,128)(2,1)} %get-tuple-element.128), channel_id=1, source_target_pairs={{0,1},{1,0},{2,3},{3,2},{4,5},{5,4},{6,7},{7,6},{8,9},{9,8},{10,11... | collective-permute-start | bytes 3145736 | tf_op jit(solution)/shard_map/ppermute | solution.py:500
  311.5 39.4 %collective-permute-start.40 = (bf16[256,1024]{1,0:T(8,128)(2,1)}, bf16[256,1024]{1,0:T(8,128)(2,1)}, u32[]{:S(2)}, u32[]{:S(2)}) collective-permute-start(bf16[256,1024]{1,0:T(8,128)(2,1)} %get-tuple-element.217), channel_id=1, source_target_pairs={{0,2},{1,3},{2,0},{3,1},{4,6},{5,7},{6,4},{7,5},{8,10},{9,11},{10,... | collective-permute-start | bytes 1572872 | tf_op jit(solution)/shard_map/ppermute | solution.py:500
  338.6 53.3 %collective-permute-start.39 = (bf16[256,1024]{1,0:T(8,128)(2,1)S(1)}, bf16[256,1024]{1,0:T(8,128)(2,1)S(1)}, u32[]{:S(2)}, u32[]{:S(2)}) collective-permute-start(bf16[256,1024]{1,0:T(8,128)(2,1)S(1)} %get-tuple-element.216), channel_id=1, source_target_pairs={{0,2},{1,3},{2,0},{3,1},{4,6},{5,7},{6,4},{7,5},{8,10},{9,11},{10,... | collective-permute-start | bytes 1572872 | tf_op jit(solution)/shard_map/ppermute | solution.py:500
  350.7 44.0 %collective-permute-start.57 = (bf16[512,896]{1,0:T(8,128)(2,1)}, bf16[512,896]{1,0:T(8,128)(2,1)S(1)}, u32[]{:S(2)}, u32[]{:S(2)}) collective-permute-start(bf16[512,896]{1,0:T(8,128)(2,1)} %get-tuple-element.151), channel_id=1, source_target_pairs={{0,8},{4,12},{8,0},{12,4},{16,24},{20,28},{24,16},{28,20},{1,9},{5... | collective-permute-start | bytes 2752520 | tf_op jit(solution)/shard_map/ppermute | solution.py:500
  352.0 40.6 %collective-permute-start.41 = (bf16[256,1024]{1,0:T(8,128)(2,1)S(1)}, bf16[256,1024]{1,0:T(8,128)(2,1)S(1)}, u32[]{:S(2)}, u32[]{:S(2)}) collective-permute-start(bf16[256,1024]{1,0:T(8,128)(2,1)S(1)} %fusion.3), channel_id=1, source_target_pairs={{0,4},{4,0},{8,12},{12,8},{16,20},{20,16},{24,28},{28,24},{1,5},{5... | collective-permute-start | bytes 1572872 | tf_op jit(solution)/shard_map/ppermute | solution.py:500
  353.6 36.5 %collective-permute-start.63 = (bf16[4,384,128]{2,1,0:T(8,128)(2,1)S(1)}, bf16[4,384,128]{2,1,0:T(8,128)(2,1)S(1)}, u32[]{:S(2)}, u32[]{:S(2)}) collective-permute-start(bf16[4,384,128]{2,1,0:T(8,128)(2,1)S(1)} %copy-done.49), channel_id=1, source_target_pairs={{0,8},{4,12},{8,0},{12,4},{16,24},{20,28},{24,16},{28,20},{1,9},{5... | collective-permute-start | bytes 1179656 | tf_op jit(solution)/shard_map/ppermute | solution.py:500
  355.5 36.5 %collective-permute-start.64 = (bf16[4,384,128]{2,1,0:T(8,128)(2,1)S(1)}, bf16[4,384,128]{2,1,0:T(8,128)(2,1)S(1)}, u32[]{:S(2)}, u32[]{:S(2)}) collective-permute-start(bf16[4,384,128]{2,1,0:T(8,128)(2,1)S(1)} %copy-done.48), channel_id=1, source_target_pairs={{0,16},{4,20},{8,24},{12,28},{16,0},{20,4},{24,8},{28,12},{1,17},{... | collective-permute-start | bytes 1179656 | tf_op jit(solution)/shard_map/ppermute | solution.py:500
  415.1 35.6 %collective-permute-start.72 = (bf16[4,384,128]{2,1,0:T(8,128)(2,1)}, bf16[4,384,128]{2,1,0:T(8,128)(2,1)}, u32[]{:S(2)}, u32[]{:S(2)}) collective-permute-start(bf16[4,384,128]{2,1,0:T(8,128)(2,1)} %get-tuple-element.171), channel_id=1, source_target_pairs={{0,4},{4,0},{8,12},{12,8},{16,20},{20,16},{24,28},{28,24},{1,5},{5... | collective-permute-start | bytes 1179656 | tf_op jit(solution)/shard_map/ppermute | solution.py:500
  418.6 32.1 %collective-permute-start.73 = (bf16[4,384,128]{2,1,0:T(8,128)(2,1)}, bf16[4,384,128]{2,1,0:T(8,128)(2,1)S(1)}, u32[]{:S(2)}, u32[]{:S(2)}) collective-permute-start(bf16[4,384,128]{2,1,0:T(8,128)(2,1)} %get-tuple-element.172), channel_id=1, source_target_pairs={{0,12},{4,8},{8,4},{12,0},{16,28},{20,24},{24,20},{28,16},{1,13},{... | collective-permute-start | bytes 1179656 | tf_op jit(solution)/shard_map/ppermute | solution.py:500
  420.6 38.5 %collective-permute-start.74 = (bf16[4,384,128]{2,1,0:T(8,128)(2,1)S(1)}, bf16[4,384,128]{2,1,0:T(8,128)(2,1)S(1)}, u32[]{:S(2)}, u32[]{:S(2)}) collective-permute-start(bf16[4,384,128]{2,1,0:T(8,128)(2,1)S(1)} %copy-done.50), channel_id=1, source_target_pairs={{0,20},{4,16},{8,28},{12,24},{16,4},{20,0},{24,12},{28,8},{1,21},{... | collective-permute-start | bytes 1179656 | tf_op jit(solution)/shard_map/ppermute | solution.py:500
  422.4 51.2 %collective-permute-start.75 = (bf16[4,384,128]{2,1,0:T(8,128)(2,1)}, bf16[4,384,128]{2,1,0:T(8,128)(2,1)S(1)}, u32[]{:S(2)}, u32[]{:S(2)}) collective-permute-start(bf16[4,384,128]{2,1,0:T(8,128)(2,1)} %get-tuple-element.174), channel_id=1, source_target_pairs={{0,28},{4,24},{8,20},{12,16},{16,12},{20,8},{24,4},{28,0},{1,29},{... | collective-permute-start | bytes 1179656 | tf_op jit(solution)/shard_map/ppermute | solution.py:500
  428.5 42.6 %collective-permute-start.59 = (bf16[128,896]{1,0:T(8,128)(2,1)S(1)}, bf16[128,896]{1,0:T(8,128)(2,1)S(1)}, u32[]{:S(2)}, u32[]{:S(2)}) collective-permute-start(bf16[128,896]{1,0:T(8,128)(2,1)S(1)} %get-tuple-element.218), channel_id=1, source_target_pairs={{0,16},{4,20},{8,24},{12,28},{16,0},{20,4},{24,8},{28,12},{1,17},{... | collective-permute-start | bytes 688136 | tf_op jit(solution)/shard_map/ppermute | solution.py:500
  450.7 24.0 %collective-permute-start.43 = (bf16[64,1024]{1,0:T(8,128)(2,1)}, bf16[64,1024]{1,0:T(8,128)(2,1)S(1)}, u32[]{:S(2)}, u32[]{:S(2)}) collective-permute-start(bf16[64,1024]{1,0:T(8,128)(2,1)} %get-tuple-element.222), channel_id=1, source_target_pairs={{0,16},{4,20},{8,24},{12,28},{16,0},{20,4},{24,8},{28,12},{1,17},{... | collective-permute-start | bytes 393224 | tf_op jit(solution)/shard_map/ppermute | solution.py:500
  450.8 24.9 %collective-permute-start.54 = (bf16[64,1024]{1,0:T(8,128)(2,1)}, bf16[64,1024]{1,0:T(8,128)(2,1)S(1)}, u32[]{:S(2)}, u32[]{:S(2)}) collective-permute-start(bf16[64,1024]{1,0:T(8,128)(2,1)} %get-tuple-element.146), channel_id=1, source_target_pairs={{0,1},{1,0},{2,3},{3,2},{4,5},{5,4},{6,7},{7,6},{8,9},{9,8},{10,11... | collective-permute-start | bytes 393224 | tf_op jit(solution)/shard_map/ppermute | solution.py:494
  459.1 23.5 %collective-permute-start.55 = (bf16[64,1024]{1,0:T(8,128)(2,1)}, bf16[64,1024]{1,0:T(8,128)(2,1)S(1)}, u32[]{:S(2)}, u32[]{:S(2)}) collective-permute-start(bf16[64,1024]{1,0:T(8,128)(2,1)} %get-tuple-element.147), channel_id=1, source_target_pairs={{0,2},{1,3},{2,0},{3,1},{4,6},{5,7},{6,4},{7,5},{8,10},{9,11},{10,... | collective-permute-start | bytes 393224 | tf_op jit(solution)/shard_map/ppermute | solution.py:494
  (95 other events, 1356.5 us)

commit v6 on v5

--- a/solution.py
+++ b/solution.py
@@ -217,11 +217,11 @@
 
 def expert_pre_kernel(peers, shares, *refs):
     (idx,), grads_in, pieces, (hot_out, grads_out, raw, wgu, down) = split_refs(
-        refs, 1, shares, peers, 5
+        refs, 1, 2 * shares, peers, 5
     )
     ff = shares * 128
     width = grads_out.shape[1]
-    span = grads_in[0].shape[0] // peers
+    span = 2 * grads_in[0].shape[0] // peers
     block = shares * span
     for m, piece in enumerate(pieces):
         at = pl.ds(pl.multiple_of(jnp.bitwise_xor(idx[0], m) * 128, 128), 128)
@@ -235,12 +235,13 @@
     lower = jnp.where(r > c, 1.0, 0.0).astype(BF)
     slot = lax.broadcasted_iota(jnp.int32, (block, CAP), 1)
 
-    def body(step, carry):
+    def body(part, step, carry):
         grads = []
         for half in range(2):
             k = step * 2 + half
             at = pl.ds(pl.multiple_of(k * span, span), span)
-            tokens = jnp.concatenate([ref[at, :] for ref in grads_in], 0)
+            tokens = jnp.concatenate([ref[at, :] for ref in grads_in[part::2]], 0)
+            k = k + part * (peers // 2)
             member = jnp.where(slot == expert, tokens[:, width:].astype(F32), 0.0)
             rank = jnp.dot(lower, member.astype(BF), preferred_element_type=F32)
             rank = jnp.sum(jnp.where(slot == expert, rank, 0.0), -1, keepdims=True)
@@ -250,38 +251,42 @@
             hot_out[pl.ds(pl.multiple_of(k * block, block), block), :] = hot
             grads.append(mm(hot, tokens[:, :width], 0, 0).astype(BF))
         grad_rows = jnp.concatenate(grads, 0)
+        step = step + part * (peers // 4)
         at = pl.ds(pl.multiple_of(step * 2 * CAP, 2 * CAP), 2 * CAP)
         grads_out[at, :] = grad_rows
         raw[at, :] = mm(grad_rows, down[...], 1, 1)
         return carry
 
-    lax.fori_loop(0, peers // 2, body, 0)
+    for part in range(2):
+        lax.fori_loop(0, peers // 4, functools.partial(body, part), 0)
 
 
 def expert_main_kernel(peers, shares, *refs):
     (idx,), rows_in, (hot_in, raw_in, wgu), back, outs = split_refs(
-        refs, 1, shares, 3, shares, 5
+        refs, 1, 2 * shares, 3, shares, 5
     )
     rows_out, hid, gpu, gate_out, near_out = outs
     ff = raw_in.shape[1]
     width = rows_out.shape[1]
-    span = rows_in[0].shape[0] // peers
+    span = 2 * rows_in[0].shape[0] // peers
     block = shares * span
     for s in range(shares):
-        near_out[s * span : (s + 1) * span, :] = rows_in[s][0:span, :width]
+        near_out[s * span : (s + 1) * span, :] = rows_in[2 * s][0:span, :width]
     expert = idx[0] * shares + idx[1]
     lane = lax.broadcasted_iota(jnp.int32, (2 * CAP, LANES), 1)
 
-    def body(step, carry):
+    def body(part, step, carry):
         slots, hots = [], []
         for half in range(2):
             k = step * 2 + half
             at = pl.ds(pl.multiple_of(k * span, span), span)
-            tokens = jnp.concatenate([ref[at, :] for ref in rows_in], 0)
+            tokens = jnp.concatenate([ref[at, :] for ref in rows_in[part::2]], 0)
+            k = k + part * (peers // 2)
             hot = hot_in[pl.ds(pl.multiple_of(k * block, block), block), :]
             hots.append(hot)
             slots.append(mm(hot, tokens, 0, 0).astype(BF))
         rows = jnp.concatenate(slots, 0)
+        step = step + part * (peers // 4)
         at = pl.ds(pl.multiple_of(step * 2 * CAP, 2 * CAP), 2 * CAP)
         gate = gate_column(rows[:, width:], expert)
         rows = rows[:, :width]
@@ -314,7 +319,8 @@
                 back[s][to, width:] = tail[s * span : (s + 1) * span, :]
         return carry
 
-    lax.fori_loop(0, peers // 2, body, 0)
+    for part in range(2):
+        lax.fori_loop(0, peers // 4, functools.partial(body, part), 0)
 
 
 def expert_rest_kernel(peers, shares, step, *refs):
@@ -509,10 +515,11 @@
 
 
 def gather_all(value):
-    first = jnp.concatenate(gather_dp(value, TOKEN_BITS), 0)
-    across = permute(first, "tensor", 2)
-    beside = permute(first, "tensor", 1)
-    return first, beside, across, permute(across, "tensor", 1)
+    near = gather_dp(value, TOKEN_BITS)
+    across = [permute(v, "tensor", 2) for v in near]
+    beside = [permute(v, "tensor", 1) for v in near]
+    corner = [permute(v, "tensor", 1) for v in across]
+    return *near, *beside, *across, *corner
 
 
 def reduce_dp(near, far, bits, other=None):
@@ -537,7 +544,8 @@
 def regroup(parts):
     shape = parts[0].shape
     return call(
-        functools.partial(regroup_kernel, len(parts)), [((len(parts),) + shape[1:], BF)] * shape[0]
+        functools.partial(regroup_kernel, len(parts)),
+        [((len(parts),) + shape[1:], BF)] * shape[0],
     )(*parts)
 
 
@@ -601,7 +609,10 @@
         smem=1,
     )(idx, w_gate, w_up, w_down)
     pieces = move_chunks(
-        [swap(weight_parts[c * shares : (c + 1) * shares], "tensor") for c in range(len(CHUNKS))],
+        [
+            swap(weight_parts[c * shares : (c + 1) * shares], "tensor")
+            for c in range(len(CHUNKS))
+        ],
     )
     ids_own = lax.dynamic_slice_in_dim(expert_ids, lax.axis_index("tensor") * own, own, 0)
     lanes = jnp.arange(LANES, dtype=jnp.int32)
@@ -723,7 +734,9 @@
     (layer_output,) = call(layer_out_kernel, [((own, width), BF)])(*mixed, res)
 
     gate_grad, up_grad, down_grad = call(
-        functools.partial(weight_grad_kernel, shares), [((experts, 128, LANES), F32)] * 3, smem=1
+        functools.partial(weight_grad_kernel, shares),
+        [((experts, 128, LANES), F32)] * 3,
+        smem=1,
     )(idx, *first, *second)
     if rep > 1:
         gate_grad = lax.psum_scatter(gate_grad, "rep", scatter_dimension=1, tiled=True)

time: 487 us -> 458 us (0.940)
  waiting for transfers between devices: 294 us -> 270 us
  starting transfers between devices: 78.4 us -> 73.5 us
    ppermute x27, waiting for transfers between devices: 78 us -> 22.6 us  [swap(): lax.ppermute(values[m], axis, [(i, i ^ m) for i in range(len(values))])]
    ppermute x49 -> x55, waiting for transfers between devices: 216 us -> 247 us  [permute(): return lax.ppermute(value, axis, [(i, i ^ bit) for i in range(count)])]
    ppermute x49 -> x55, starting transfers between devices: 60.9 us -> 52.8 us  [permute(): return lax.ppermute(value, axis, [(i, i ^ bit) for i in range(count)])]
    unnamed x110 -> x143, local copies, waits for them, and re-layouts: 10.3 us -> 9.39 us
  transfers between devices with their start and end apart: 76 -> 82, of which waited for: 31 -> 28; matrix products, arithmetic and copies ran while one was open for 5% -> 5% of each run, Pallas kernels for 14% -> 15%
where the time goes in v6:
time: 458 us; the launch traced here: 457 us
  waiting for transfers between devices  270 us (59%)
  Pallas kernels  83.5 us (18%)
  starting transfers between devices  73.5 us (16%)
  local copies, waits for them, and re-layouts  16.3 us (4%)
  other arithmetic  12.2 us (3%)
    ppermute x55, waiting for transfers between devices, permute(): return lax.ppermute(value, axis, [(i, i ^ bit) for i in range(count)])  247 us
    pallas_call x16, Pallas kernels, run(): pl.pallas_call(kernel, out_shape=[jax.ShapeDtypeStruct(s, d) for s, d in...  83.5 us
    ppermute x55, starting transfers between devices, permute(): return lax.ppermute(value, axis, [(i, i ^ bit) for i in range(count)])  52.8 us
    ppermute x27, waiting for transfers between devices, swap(): lax.ppermute(values[m], axis, [(i, i ^ m) for i in range(len(values))])  22.6 us
    ppermute x27, starting transfers between devices, swap(): lax.ppermute(values[m], axis, [(i, i ^ m) for i in range(len(values))])  20.7 us
    unnamed x143, local copies, waits for them, and re-layouts  9.39 us
  transfers between devices with their start and end apart: 82, of which 28 were waited for; matrix products, arithmetic and copies ran while one was open for 5% of the time, Pallas kernels for 15%

profile of v6, /device:TPU:0, one launch (start us, length us, event | category | flops | bytes accessed | tf_op | source)
XLA Modules:
  0.0 457.1 jit_solution(6046560114142467969)
XLA Ops:
  15.8 10.0 %collective-permute-done.3 = bf16[128,512]{1,0:T(8,128)(2,1)S(1)} collective-permute-done((bf16[128,512]{1,0:T(8,128)(2,1)S(1)}, bf16[128,512]{1,0:T(8,128)(2,1)S(1)}, u32[]{:S(2)}, u32[]{:S(2)}) %collective-permute-start.3) | collective-permute-done | bytes 131104 | tf_op jit(solution)/shard_map/ppermute | solution.py:506
  26.7 3.7 shard_map.231
  34.7 4.1 collective-permute-start.21
  40.3 6.0 %collective-permute-done.21 = bf16[64,1152]{1,0:T(8,128)(2,1)S(1)} collective-permute-done((bf16[64,1152]{1,0:T(8,128)(2,1)S(1)}, bf16[64,1152]{1,0:T(8,128)(2,1)S(1)}, u32[]{:S(2)}, u32[]{:S(2)}) %collective-permute-start.21) | collective-permute-done | bytes 147488 | tf_op jit(solution)/shard_map/ppermute | solution.py:506
  56.2 5.4 %shard_map.229 = (bf16[64,1024]{1,0:T(8,128)(2,1)}, bf16[64,1024]{1,0:T(8,128)(2,1)}, bf16[64,1024]{1,0:T(8,128)(2,1)}, bf16[64,1024]{1,0:T(8,128)(2,1)}, bf16[1...) custom-call(s32[2]{0:T(128)} %pad_add_fusion.refs_0_.idx, ...), custom_call_target="tpu_custom_call" | custom-call | tf_op jit(solution)/shard_map/pallas_call | solution.py:38
  62.8 3.2 collective-permute-done.34.refs_2_
  69.6 5.3 %collective-permute-done.35.refs_3_ = bf16[4,384,128]{2,1,0:T(8,128)(2,1)} collective-permute-done((bf16[4,384,128]{2,1,0:T(8,128)(2,1)}, bf16[4,384,128]{2,1,0:T(8,128)(2,1)}, u32[]{:S(2)}, u32[]{:S(2)}) %collective-permute-start.35) | collective-permute-done | bytes 393248 | tf_op jit(solution)/shard_map/ppermute | solution.py:500
  74.9 4.8 %collective-permute-start.37 = (bf16[4,384,128]{2,1,0:T(8,128)(2,1)}, bf16[4,384,128]{2,1,0:T(8,128)(2,1)S(1)}, u32[]{:S(2)}, u32[]{:S(2)}) collective-permute-start(bf16[4,384,128]{2,1,0:T(8,128)(2,1)} %get-tuple-element.112), channel_id=1, source_target_pairs={{0,8},{4,12},{8,0},{12,4},{16,24},{20,28},{24,16},{28,20},{1,9},{5... | collective-permute-start | bytes 1179656 | tf_op jit(solution)/shard_map/ppermute | solution.py:506
  89.5 36.4 %collective-permute-done.12 = bf16[64,1152]{1,0:T(8,128)(2,1)S(1)} collective-permute-done((bf16[64,1152]{1,0:T(8,128)(2,1)}, bf16[64,1152]{1,0:T(8,128)(2,1)S(1)}, u32[]{:S(2)}, u32[]{:S(2)}) %collective-permute-start.12) | collective-permute-done | bytes 147488 | tf_op jit(solution)/shard_map/ppermute | solution.py:506
  129.5 14.8 %collective-permute-done.13 = bf16[128,1152]{1,0:T(8,128)(2,1)S(1)} collective-permute-done((bf16[128,1152]{1,0:T(8,128)(2,1)S(1)}, bf16[128,1152]{1,0:T(8,128)(2,1)S(1)}, u32[]{:S(2)}, u32[]{:S(2)}) %collective-permute-start.13) | collective-permute-done | bytes 294944 | tf_op jit(solution)/shard_map/ppermute | solution.py:506
  144.9 5.8 %collective-permute-done.38.refs_12_ = bf16[4,384,128]{2,1,0:T(8,128)(2,1)S(1)} collective-permute-done((bf16[4,384,128]{2,1,0:T(8,128)(2,1)S(1)}, bf16[4,384,128]{2,1,0:T(8,128)(2,1)S(1)}, u32[]{:S(2)}, u32[]{:S(2)}) %collective-permute-start.38) | collective-permute-done | bytes 393248 | tf_op jit(solution)/shard_map/ppermute | solution.py:506
  152.4 19.5 %collective-permute-done.23.refs_2_ = bf16[256,1152]{1,0:T(8,128)(2,1)S(1)} collective-permute-done((bf16[256,1152]{1,0:T(8,128)(2,1)S(1)}, bf16[256,1152]{1,0:T(8,128)(2,1)S(1)}, u32[]{:S(2)}, u32[]{:S(2)}) %collective-permute-start.23) | collective-permute-done | bytes 589856 | tf_op jit(solution)/shard_map/ppermute | solution.py:506
  174.0 9.7 %collective-permute-done.14.refs_2_ = bf16[256,1152]{1,0:T(8,128)(2,1)S(1)} collective-permute-done((bf16[256,1152]{1,0:T(8,128)(2,1)S(1)}, bf16[256,1152]{1,0:T(8,128)(2,1)S(1)}, u32[]{:S(2)}, u32[]{:S(2)}) %collective-permute-start.14) | collective-permute-done | bytes 589856 | tf_op jit(solution)/shard_map/ppermute | solution.py:506
  184.3 3.8 collective-permute-done.27.refs_6_
  188.6 12.1 %collective-permute-done.17.refs_5_ = bf16[256,1152]{1,0:T(8,128)(2,1)S(1)} collective-permute-done((bf16[256,1152]{1,0:T(8,128)(2,1)S(1)}, bf16[256,1152]{1,0:T(8,128)(2,1)S(1)}, u32[]{:S(2)}, u32[]{:S(2)}) %collective-permute-start.17) | collective-permute-done | bytes 589856 | tf_op jit(solution)/shard_map/ppermute | solution.py:506
  200.7 10.2 %collective-permute-done.18.refs_6_ = bf16[256,1152]{1,0:T(8,128)(2,1)S(1)} collective-permute-done((bf16[256,1152]{1,0:T(8,128)(2,1)S(1)}, bf16[256,1152]{1,0:T(8,128)(2,1)S(1)}, u32[]{:S(2)}, u32[]{:S(2)}) %collective-permute-start.18) | collective-permute-done | bytes 589856 | tf_op jit(solution)/shard_map/ppermute | solution.py:506
  211.9 11.4 %shard_map.234 = (bf16[2048,128]{1,0:T(8,128)(2,1)}, bf16[1024,1024]{1,0:T(8,128)(2,1)}, f32[1024,512]{1,0:T(8,128)}, bf16[1024,1024]{1,0:T(8,128)(2,1)}, bf16[512,1024]{1,0:T(8,128)(2,1)}) custom-call(s32[2]{0:T(128)} %pad_add_fusion.refs_0_.idx, bf16[256,1152]{1,0:T(8,128)(2,1)} %copy-done.2, bf16[256,1152]{1,0:T(8,128)(2,1)} %copy-done.17, ...), custom_call_target="tpu_custom_call" | custom-call | tf_op jit(solution)/shard_map/pallas_call | solution.py:38
  224.1 16.2 %shard_map.235 = (bf16[512,1152]{1,0:T(8,128)(2,1)}, bf16[512,1152]{1,0:T(8,128)(2,1)}, bf16[512,1152]{1,0:T(8,128)(2,1)}, bf16[512,1152]{1,0:T(8,128)(2,1)}, bf...) custom-call(s32[2]{0:T(128)} %pad_add_fusion.refs_0_.idx, ...), custom_call_target="tpu_custom_call" | custom-call | tf_op jit(solution)/shard_map/pallas_call | solution.py:38
  247.0 14.2 %collective-permute-done.53 = bf16[256,1152]{1,0:T(8,128)(2,1)S(1)} collective-permute-done((bf16[256,1152]{1,0:T(8,128)(2,1)S(1)}, bf16[256,1152]{1,0:T(8,128)(2,1)S(1)}, u32[]{:S(2)}, u32[]{:S(2)}) %collective-permute-start.53) | collective-permute-done | bytes 589856 | tf_op jit(solution)/shard_map/ppermute | solution.py:506
  262.7 14.0 %shard_map.236 = (bf16[512,1024]{1,0:T(8,128)(2,1)}, bf16[512,1024]{1,0:T(8,128)(2,1)}, bf16[512,1024]{1,0:T(8,128)(2,1)}, bf16[512,1024]{1,0:T(8,128)(2,1)}, bf...) custom-call(s32[2]{0:T(128)} %pad_add_fusion.refs_0_.idx, ...), custom_call_target="tpu_custom_call" | custom-call | tf_op jit(solution)/shard_map/pallas_call | solution.py:38
  282.5 5.7 %collective-permute-done.55 = bf16[128,1152]{1,0:T(8,128)(2,1)S(1)} collective-permute-done((bf16[128,1152]{1,0:T(8,128)(2,1)S(1)}, bf16[128,1152]{1,0:T(8,128)(2,1)S(1)}, u32[]{:S(2)}, u32[]{:S(2)}) %collective-permute-start.55) | collective-permute-done | bytes 294944 | tf_op jit(solution)/shard_map/ppermute | solution.py:506
  288.9 9.8 %collective-permute-done.56.refs_1_ = bf16[64,1152]{1,0:T(8,128)(2,1)S(1)} collective-permute-done((bf16[64,1152]{1,0:T(8,128)(2,1)S(1)}, bf16[64,1152]{1,0:T(8,128)(2,1)S(1)}, u32[]{:S(2)}, u32[]{:S(2)}) %collective-permute-start.56) | collective-permute-done | bytes 147488 | tf_op jit(solution)/shard_map/ppermute | solution.py:506
  303.6 5.3 %collective-permute-done.59.refs_4_ = bf16[80,1152]{1,0:T(8,128)(2,1)S(1)} collective-permute-done((bf16[80,1152]{1,0:T(8,128)(2,1)}, bf16[80,1152]{1,0:T(8,128)(2,1)S(1)}, u32[]{:S(2)}, u32[]{:S(2)}) %collective-permute-start.59) | collective-permute-done | bytes 184352 | tf_op jit(solution)/shard_map/ppermute | solution.py:500
  312.4 7.2 %shard_map.239 = (bf16[512,896]{1,0:T(8,128)(2,1)}, bf16[512,896]{1,0:T(8,128)(2,1)}, bf16[64,1024]{1,0:T(8,128)(2,1)}, bf16[64,1024]{1,0:T(8,128)(2,1)}, bf16[6...) custom-call(s32[2]{0:T(128)} %pad_add_fusion.refs_0_.idx, bf16[80,1152]{1,0:T(8,128)(2,1)} %get-tuple-element.137.refs_1_, ...), custom_call_target="tpu_custom_call" | custom-call | tf_op jit(solution)/shard_map/pallas_call | solution.py:38
  324.6 34.9 %collective-permute-done.69.refs_1_ = bf16[4,384,128]{2,1,0:T(8,128)(2,1)S(1)} collective-permute-done((bf16[4,384,128]{2,1,0:T(8,128)(2,1)S(1)}, bf16[4,384,128]{2,1,0:T(8,128)(2,1)S(1)}, u32[]{:S(2)}, u32[]{:S(2)}) %collective-permute-start.69) | collective-permute-done | bytes 393248 | tf_op jit(solution)/shard_map/ppermute | solution.py:506
  364.4 8.9 %collective-permute-done.71.refs_3_ = bf16[4,384,128]{2,1,0:T(8,128)(2,1)S(1)} collective-permute-done((bf16[4,384,128]{2,1,0:T(8,128)(2,1)S(1)}, bf16[4,384,128]{2,1,0:T(8,128)(2,1)S(1)}, u32[]{:S(2)}, u32[]{:S(2)}) %collective-permute-start.71) | collective-permute-done | bytes 393248 | tf_op jit(solution)/shard_map/ppermute | solution.py:506
  386.3 2.9 collective-permute-start.79
  393.9 3.9 collective-permute-done.74.refs_3_
  401.4 18.3 %collective-permute-done.78.refs_4_ = bf16[4,384,128]{2,1,0:T(8,128)(2,1)} collective-permute-done((bf16[4,384,128]{2,1,0:T(8,128)(2,1)}, bf16[4,384,128]{2,1,0:T(8,128)(2,1)}, u32[]{:S(2)}, u32[]{:S(2)}) %collective-permute-start.78) | collective-permute-done | bytes 393248 | tf_op jit(solution)/shard_map/ppermute | solution.py:506
  419.7 8.8 %collective-permute-done.80.refs_6_ = bf16[4,384,128]{2,1,0:T(8,128)(2,1)S(1)} collective-permute-done((bf16[4,384,128]{2,1,0:T(8,128)(2,1)S(1)}, bf16[4,384,128]{2,1,0:T(8,128)(2,1)S(1)}, u32[]{:S(2)}, u32[]{:S(2)}) %collective-permute-start.80) | collective-permute-done | bytes 393248 | tf_op jit(solution)/shard_map/ppermute | solution.py:506
  429.7 11.2 %collective-permute-done.65.refs_1_ = bf16[128,896]{1,0:T(8,128)(2,1)S(1)} collective-permute-done((bf16[128,896]{1,0:T(8,128)(2,1)S(1)}, bf16[128,896]{1,0:T(8,128)(2,1)S(1)}, u32[]{:S(2)}, u32[]{:S(2)}) %collective-permute-start.65) | collective-permute-done | bytes 229408 | tf_op jit(solution)/shard_map/ppermute | solution.py:506
  446.3 4.9 %shard_map.244 = (f32[32,128,128]{2,1,0:T(8,128)}, f32[32,128,128]{2,1,0:T(8,128)}, f32[32,128,128]{2,1,0:T(8,128)}) custom-call(s32[2]{0:T(128)} %pad_add_fusion.refs_0_.idx, bf16[4,384,128]{2,1,0:T(8,128)(2,1)} %get-tuple-element.163.refs_0_, bf16[4,384,128]{2,1,0:T(8,128)(2,1)} %copy-done.37, bf16[4,384,128]{2,1,0:T(8,128)(2,1)} %copy-done.38, ...), custom_call_target="tpu_custom_call" | custom-call | tf_op jit(solution)/shard_map/pallas_call | solution.py:38
  (332 shorter events, 123.1 us)
Async XLA Ops:
  0.7 29.9 %collective-permute-start.2 = (bf16[64,1024]{1,0:T(8,128)(2,1)}, bf16[64,1024]{1,0:T(8,128)(2,1)S(1)}, u32[]{:S(2)}, u32[]{:S(2)}) collective-permute-start(bf16[64,1024]{1,0:T(8,128)(2,1)} %refs_4_.3), channel_id=1, source_target_pairs={{0,3},{1,2},{2,1},{3,0},{4,7},{5,6},{6,5},{7,4},{8,11},{9,10},{10,... | collective-permute-start | bytes 393224 | tf_op jit(solution)/shard_map/ppermute | solution.py:500
  3.2 31.6 %collective-permute-start.1 = (bf16[64,1024]{1,0:T(8,128)(2,1)}, bf16[64,1024]{1,0:T(8,128)(2,1)S(1)}, u32[]{:S(2)}, u32[]{:S(2)}) collective-permute-start(bf16[64,1024]{1,0:T(8,128)(2,1)} %refs_4_.3), channel_id=1, source_target_pairs={{0,2},{1,3},{2,0},{3,1},{4,6},{5,7},{6,4},{7,5},{8,10},{9,11},{10,... | collective-permute-start | bytes 393224 | tf_op jit(solution)/shard_map/ppermute | solution.py:500
  3.8 35.0 %collective-permute-start = (bf16[64,1024]{1,0:T(8,128)(2,1)}, bf16[64,1024]{1,0:T(8,128)(2,1)S(1)}, u32[]{:S(2)}, u32[]{:S(2)}) collective-permute-start(bf16[64,1024]{1,0:T(8,128)(2,1)} %refs_4_.3), channel_id=1, source_target_pairs={{0,1},{1,0},{2,3},{3,2},{4,5},{5,4},{6,7},{7,6},{8,9},{9,8},{10,11... | collective-permute-start | bytes 393224 | tf_op jit(solution)/shard_map/ppermute | solution.py:500
  48.6 26.3 %collective-permute-start.35 = (bf16[4,384,128]{2,1,0:T(8,128)(2,1)}, bf16[4,384,128]{2,1,0:T(8,128)(2,1)}, u32[]{:S(2)}, u32[]{:S(2)}) collective-permute-start(bf16[4,384,128]{2,1,0:T(8,128)(2,1)} %get-tuple-element.110), channel_id=1, source_target_pairs={{0,3},{1,2},{2,1},{3,0},{4,7},{5,6},{6,5},{7,4},{8,11},{9,10},{10,... | collective-permute-start | bytes 1179656 | tf_op jit(solution)/shard_map/ppermute | solution.py:500
  52.2 35.6 %collective-permute-start.22 = (bf16[128,1152]{1,0:T(8,128)(2,1)}, bf16[128,1152]{1,0:T(8,128)(2,1)}, u32[]{:S(2)}, u32[]{:S(2)}) collective-permute-start(bf16[128,1152]{1,0:T(8,128)(2,1)} %pad_maximum_fusion.4), channel_id=1, source_target_pairs={{0,8},{4,12},{8,0},{12,4},{16,24},{20,28},{24,16},{28,20},{1,9},{5... | collective-permute-start | bytes 884744 | tf_op jit(solution)/shard_map/ppermute | solution.py:506
  74.9 51.1 %collective-permute-start.37 = (bf16[4,384,128]{2,1,0:T(8,128)(2,1)}, bf16[4,384,128]{2,1,0:T(8,128)(2,1)S(1)}, u32[]{:S(2)}, u32[]{:S(2)}) collective-permute-start(bf16[4,384,128]{2,1,0:T(8,128)(2,1)} %get-tuple-element.112), channel_id=1, source_target_pairs={{0,8},{4,12},{8,0},{12,4},{16,24},{20,28},{24,16},{28,20},{1,9},{5... | collective-permute-start | bytes 1179656 | tf_op jit(solution)/shard_map/ppermute | solution.py:506
  82.3 45.8 %collective-permute-start.39 = (bf16[4,384,128]{2,1,0:T(8,128)(2,1)}, bf16[4,384,128]{2,1,0:T(8,128)(2,1)S(1)}, u32[]{:S(2)}, u32[]{:S(2)}) collective-permute-start(bf16[4,384,128]{2,1,0:T(8,128)(2,1)} %get-tuple-element.114), channel_id=1, source_target_pairs={{0,16},{4,20},{8,24},{12,28},{16,0},{20,4},{24,8},{28,12},{1,17},{... | collective-permute-start | bytes 1179656 | tf_op jit(solution)/shard_map/ppermute | solution.py:506
  82.4 46.3 %collective-permute-start.41 = (bf16[4,384,128]{2,1,0:T(8,128)(2,1)}, bf16[4,384,128]{2,1,0:T(8,128)(2,1)S(1)}, u32[]{:S(2)}, u32[]{:S(2)}) collective-permute-start(bf16[4,384,128]{2,1,0:T(8,128)(2,1)} %get-tuple-element.116), channel_id=1, source_target_pairs={{0,24},{4,28},{8,16},{12,20},{16,8},{20,12},{24,0},{28,4},{1,25},{... | collective-permute-start | bytes 1179656 | tf_op jit(solution)/shard_map/ppermute | solution.py:506
  84.8 60.1 %collective-permute-start.36 = (bf16[4,384,128]{2,1,0:T(8,128)(2,1)}, bf16[4,384,128]{2,1,0:T(8,128)(2,1)S(1)}, u32[]{:S(2)}, u32[]{:S(2)}) collective-permute-start(bf16[4,384,128]{2,1,0:T(8,128)(2,1)} %get-tuple-element.111), channel_id=1, source_target_pairs={{0,4},{4,0},{8,12},{12,8},{16,20},{20,16},{24,28},{28,24},{1,5},{5... | collective-permute-start | bytes 1179656 | tf_op jit(solution)/shard_map/ppermute | solution.py:506
  87.8 38.1 %collective-permute-start.12 = (bf16[64,1152]{1,0:T(8,128)(2,1)}, bf16[64,1152]{1,0:T(8,128)(2,1)S(1)}, u32[]{:S(2)}, u32[]{:S(2)}) collective-permute-start(bf16[64,1152]{1,0:T(8,128)(2,1)} %get-tuple-element.101), channel_id=1, source_target_pairs={{0,16},{4,20},{8,24},{12,28},{16,0},{20,4},{24,8},{28,12},{1,17},{... | collective-permute-start | bytes 442376 | tf_op jit(solution)/shard_map/ppermute | solution.py:506
  144.3 27.6 %collective-permute-start.23 = (bf16[256,1152]{1,0:T(8,128)(2,1)S(1)}, bf16[256,1152]{1,0:T(8,128)(2,1)S(1)}, u32[]{:S(2)}, u32[]{:S(2)}) collective-permute-start(bf16[256,1152]{1,0:T(8,128)(2,1)S(1)} %pad_maximum_fusion.refs_1_), channel_id=1, source_target_pairs={{0,4},{4,0},{8,12},{12,8},{16,20},{20,16},{24,28},{28,24},{1,5},{5... | collective-permute-start | bytes 1769480 | tf_op jit(solution)/shard_map/ppermute | solution.py:506
  144.9 27.4 %collective-permute-start.24 = (bf16[256,1152]{1,0:T(8,128)(2,1)S(1)}, bf16[256,1152]{1,0:T(8,128)(2,1)S(1)}, u32[]{:S(2)}, u32[]{:S(2)}) collective-permute-start(bf16[256,1152]{1,0:T(8,128)(2,1)S(1)} %pad_maximum_fusion.refs_1_), channel_id=1, source_target_pairs={{0,1},{1,0},{2,3},{3,2},{4,5},{5,4},{6,7},{7,6},{8,9},{9,8},{10,11... | collective-permute-start | bytes 1769480 | tf_op jit(solution)/shard_map/ppermute | solution.py:506
  150.8 32.9 %collective-permute-start.14 = (bf16[256,1152]{1,0:T(8,128)(2,1)S(1)}, bf16[256,1152]{1,0:T(8,128)(2,1)S(1)}, u32[]{:S(2)}, u32[]{:S(2)}) collective-permute-start(bf16[256,1152]{1,0:T(8,128)(2,1)S(1)} %constant_dynamic-update-slice_fusion.3.refs_1_), channel_id=1, source_target_pairs={{0,4},{4,0},{8,12},{12,8},{16,20},{20,16},{24,28},{28,24},{1,5},{5... | collective-permute-start | bytes 1769480 | tf_op jit(solution)/shard_map/ppermute | solution.py:506
  152.3 32.0 %collective-permute-start.28 = (bf16[256,1152]{1,0:T(8,128)(2,1)S(1)}, bf16[256,1152]{1,0:T(8,128)(2,1)S(1)}, u32[]{:S(2)}, u32[]{:S(2)}) collective-permute-start(bf16[256,1152]{1,0:T(8,128)(2,1)S(1)} %collective-permute-done.26.refs_5_), channel_id=1, source_target_pairs={{0,1},{1,0},{2,3},{3,2},{4,5},{5,4},{6,7},{7,6},{8,9},{9,8},{10,11... | collective-permute-start | bytes 1769480 | tf_op jit(solution)/shard_map/ppermute | solution.py:506
  172.3 28.4 %collective-permute-start.17 = (bf16[256,1152]{1,0:T(8,128)(2,1)S(1)}, bf16[256,1152]{1,0:T(8,128)(2,1)S(1)}, u32[]{:S(2)}, u32[]{:S(2)}) collective-permute-start(bf16[256,1152]{1,0:T(8,128)(2,1)S(1)} %constant_dynamic-update-slice_fusion.3.refs_1_), channel_id=1, source_target_pairs={{0,2},{1,3},{2,0},{3,1},{4,6},{5,7},{6,4},{7,5},{8,10},{9,11},{10,... | collective-permute-start | bytes 1769480 | tf_op jit(solution)/shard_map/ppermute | solution.py:506
  183.7 27.2 %collective-permute-start.18 = (bf16[256,1152]{1,0:T(8,128)(2,1)S(1)}, bf16[256,1152]{1,0:T(8,128)(2,1)S(1)}, u32[]{:S(2)}, u32[]{:S(2)}) collective-permute-start(bf16[256,1152]{1,0:T(8,128)(2,1)S(1)} %collective-permute-done.14.refs_2_), channel_id=1, source_target_pairs={{0,2},{1,3},{2,0},{3,1},{4,6},{5,7},{6,4},{7,5},{8,10},{9,11},{10,... | collective-permute-start | bytes 1769480 | tf_op jit(solution)/shard_map/ppermute | solution.py:506
  184.3 39.0 %collective-permute-start.15 = (bf16[256,1152]{1,0:T(8,128)(2,1)S(1)}, bf16[256,1152]{1,0:T(8,128)(2,1)S(1)}, u32[]{:S(2)}, u32[]{:S(2)}) collective-permute-start(bf16[256,1152]{1,0:T(8,128)(2,1)S(1)} %constant_dynamic-update-slice_fusion.3.refs_1_), channel_id=1, source_target_pairs={{0,1},{1,0},{2,3},{3,2},{4,5},{5,4},{6,7},{7,6},{8,9},{9,8},{10,11... | collective-permute-start | bytes 1769480 | tf_op jit(solution)/shard_map/ppermute | solution.py:506
  188.1 35.3 %collective-permute-start.16 = (bf16[256,1152]{1,0:T(8,128)(2,1)S(1)}, bf16[256,1152]{1,0:T(8,128)(2,1)}, u32[]{:S(2)}, u32[]{:S(2)}) collective-permute-start(bf16[256,1152]{1,0:T(8,128)(2,1)S(1)} %collective-permute-done.14.refs_2_), channel_id=1, source_target_pairs={{0,1},{1,0},{2,3},{3,2},{4,5},{5,4},{6,7},{7,6},{8,9},{9,8},{10,11... | collective-permute-start | bytes 1769480 | tf_op jit(solution)/shard_map/ppermute | solution.py:506
  245.7 31.1 %collective-permute-start.52 = (bf16[256,1152]{1,0:T(8,128)(2,1)S(1)}, bf16[256,1152]{1,0:T(8,128)(2,1)S(1)}, u32[]{:S(2)}, u32[]{:S(2)}) collective-permute-start(bf16[256,1152]{1,0:T(8,128)(2,1)S(1)} %get-tuple-element.214), channel_id=1, source_target_pairs={{0,2},{1,3},{2,0},{3,1},{4,6},{5,7},{6,4},{7,5},{8,10},{9,11},{10,... | collective-permute-start | bytes 1769480 | tf_op jit(solution)/shard_map/ppermute | solution.py:506
  280.6 39.2 %collective-permute-start.43 = (bf16[512,1024]{1,0:T(8,128)(2,1)}, bf16[512,1024]{1,0:T(8,128)(2,1)S(1)}, u32[]{:S(2)}, u32[]{:S(2)}) collective-permute-start(bf16[512,1024]{1,0:T(8,128)(2,1)} %get-tuple-element.128), channel_id=1, source_target_pairs={{0,1},{1,0},{2,3},{3,2},{4,5},{5,4},{6,7},{7,6},{8,9},{9,8},{10,11... | collective-permute-start | bytes 3145736 | tf_op jit(solution)/shard_map/ppermute | solution.py:506
  281.6 38.1 %collective-permute-start.46 = (bf16[256,1024]{1,0:T(8,128)(2,1)}, bf16[256,1024]{1,0:T(8,128)(2,1)}, u32[]{:S(2)}, u32[]{:S(2)}) collective-permute-start(bf16[256,1024]{1,0:T(8,128)(2,1)} %get-tuple-element.217), channel_id=1, source_target_pairs={{0,2},{1,3},{2,0},{3,1},{4,6},{5,7},{6,4},{7,5},{8,10},{9,11},{10,... | collective-permute-start | bytes 1572872 | tf_op jit(solution)/shard_map/ppermute | solution.py:506
  308.9 52.5 %collective-permute-start.45 = (bf16[256,1024]{1,0:T(8,128)(2,1)S(1)}, bf16[256,1024]{1,0:T(8,128)(2,1)S(1)}, u32[]{:S(2)}, u32[]{:S(2)}) collective-permute-start(bf16[256,1024]{1,0:T(8,128)(2,1)S(1)} %get-tuple-element.216), channel_id=1, source_target_pairs={{0,2},{1,3},{2,0},{3,1},{4,6},{5,7},{6,4},{7,5},{8,10},{9,11},{10,... | collective-permute-start | bytes 1572872 | tf_op jit(solution)/shard_map/ppermute | solution.py:506
  319.7 44.4 %collective-permute-start.63 = (bf16[512,896]{1,0:T(8,128)(2,1)}, bf16[512,896]{1,0:T(8,128)(2,1)S(1)}, u32[]{:S(2)}, u32[]{:S(2)}) collective-permute-start(bf16[512,896]{1,0:T(8,128)(2,1)} %get-tuple-element.151), channel_id=1, source_target_pairs={{0,8},{4,12},{8,0},{12,4},{16,24},{20,28},{24,16},{28,20},{1,9},{5... | collective-permute-start | bytes 2752520 | tf_op jit(solution)/shard_map/ppermute | solution.py:506
  321.0 41.3 %collective-permute-start.47 = (bf16[256,1024]{1,0:T(8,128)(2,1)S(1)}, bf16[256,1024]{1,0:T(8,128)(2,1)S(1)}, u32[]{:S(2)}, u32[]{:S(2)}) collective-permute-start(bf16[256,1024]{1,0:T(8,128)(2,1)S(1)} %fusion.3), channel_id=1, source_target_pairs={{0,4},{4,0},{8,12},{12,8},{16,20},{20,16},{24,28},{28,24},{1,5},{5... | collective-permute-start | bytes 1572872 | tf_op jit(solution)/shard_map/ppermute | solution.py:506
  321.2 38.3 %collective-permute-start.69 = (bf16[4,384,128]{2,1,0:T(8,128)(2,1)S(1)}, bf16[4,384,128]{2,1,0:T(8,128)(2,1)S(1)}, u32[]{:S(2)}, u32[]{:S(2)}) collective-permute-start(bf16[4,384,128]{2,1,0:T(8,128)(2,1)S(1)} %copy-done.63), channel_id=1, source_target_pairs={{0,8},{4,12},{8,0},{12,4},{16,24},{20,28},{24,16},{28,20},{1,9},{5... | collective-permute-start | bytes 1179656 | tf_op jit(solution)/shard_map/ppermute | solution.py:506
  323.1 38.2 %collective-permute-start.70 = (bf16[4,384,128]{2,1,0:T(8,128)(2,1)S(1)}, bf16[4,384,128]{2,1,0:T(8,128)(2,1)S(1)}, u32[]{:S(2)}, u32[]{:S(2)}) collective-permute-start(bf16[4,384,128]{2,1,0:T(8,128)(2,1)S(1)} %copy-done.62), channel_id=1, source_target_pairs={{0,16},{4,20},{8,24},{12,28},{16,0},{20,4},{24,8},{28,12},{1,17},{... | collective-permute-start | bytes 1179656 | tf_op jit(solution)/shard_map/ppermute | solution.py:506
  385.2 34.5 %collective-permute-start.78 = (bf16[4,384,128]{2,1,0:T(8,128)(2,1)}, bf16[4,384,128]{2,1,0:T(8,128)(2,1)}, u32[]{:S(2)}, u32[]{:S(2)}) collective-permute-start(bf16[4,384,128]{2,1,0:T(8,128)(2,1)} %get-tuple-element.171), channel_id=1, source_target_pairs={{0,4},{4,0},{8,12},{12,8},{16,20},{20,16},{24,28},{28,24},{1,5},{5... | collective-permute-start | bytes 1179656 | tf_op jit(solution)/shard_map/ppermute | solution.py:506
  386.3 33.4 %collective-permute-start.79 = (bf16[4,384,128]{2,1,0:T(8,128)(2,1)}, bf16[4,384,128]{2,1,0:T(8,128)(2,1)S(1)}, u32[]{:S(2)}, u32[]{:S(2)}) collective-permute-start(bf16[4,384,128]{2,1,0:T(8,128)(2,1)} %get-tuple-element.172), channel_id=1, source_target_pairs={{0,12},{4,8},{8,4},{12,0},{16,28},{20,24},{24,20},{28,16},{1,13},{... | collective-permute-start | bytes 1179656 | tf_op jit(solution)/shard_map/ppermute | solution.py:506
  389.3 39.2 %collective-permute-start.80 = (bf16[4,384,128]{2,1,0:T(8,128)(2,1)S(1)}, bf16[4,384,128]{2,1,0:T(8,128)(2,1)S(1)}, u32[]{:S(2)}, u32[]{:S(2)}) collective-permute-start(bf16[4,384,128]{2,1,0:T(8,128)(2,1)S(1)} %copy-done.67), channel_id=1, source_target_pairs={{0,20},{4,16},{8,28},{12,24},{16,4},{20,0},{24,12},{28,8},{1,21},{... | collective-permute-start | bytes 1179656 | tf_op jit(solution)/shard_map/ppermute | solution.py:506
  390.8 52.6 %collective-permute-start.81 = (bf16[4,384,128]{2,1,0:T(8,128)(2,1)}, bf16[4,384,128]{2,1,0:T(8,128)(2,1)S(1)}, u32[]{:S(2)}, u32[]{:S(2)}) collective-permute-start(bf16[4,384,128]{2,1,0:T(8,128)(2,1)} %get-tuple-element.174), channel_id=1, source_target_pairs={{0,28},{4,24},{8,20},{12,16},{16,12},{20,8},{24,4},{28,0},{1,29},{... | collective-permute-start | bytes 1179656 | tf_op jit(solution)/shard_map/ppermute | solution.py:506
  397.9 43.1 %collective-permute-start.65 = (bf16[128,896]{1,0:T(8,128)(2,1)S(1)}, bf16[128,896]{1,0:T(8,128)(2,1)S(1)}, u32[]{:S(2)}, u32[]{:S(2)}) collective-permute-start(bf16[128,896]{1,0:T(8,128)(2,1)S(1)} %get-tuple-element.218), channel_id=1, source_target_pairs={{0,16},{4,20},{8,24},{12,28},{16,0},{20,4},{24,8},{28,12},{1,17},{... | collective-permute-start | bytes 688136 | tf_op jit(solution)/shard_map/ppermute | solution.py:506
  419.6 26.5 %collective-permute-start.60 = (bf16[64,1024]{1,0:T(8,128)(2,1)}, bf16[64,1024]{1,0:T(8,128)(2,1)S(1)}, u32[]{:S(2)}, u32[]{:S(2)}) collective-permute-start(bf16[64,1024]{1,0:T(8,128)(2,1)} %get-tuple-element.146), channel_id=1, source_target_pairs={{0,1},{1,0},{2,3},{3,2},{4,5},{5,4},{6,7},{7,6},{8,9},{9,8},{10,11... | collective-permute-start | bytes 393224 | tf_op jit(solution)/shard_map/ppermute | solution.py:500
  (118 other events, 2200.4 us)
